TPU v7x, 32 devices: a whole 2x2x4 slice. The times are simulated.
32 devices in a mesh: fsdp: 16 (over z, y, core), pair: 2 (over x).
Axes of the slice: x: 2, y: 2, z: 4, core: 2. Of those that a mesh axis runs over, the one named last changes fastest.
Arguments:
- tokens: bfloat16 [2, 128, 32, 2048], P(None, ('fsdp', 'pair')), may hold values from -6 to 6
- cotangent: bfloat16 [2, 128, 32, 2048], P(None, ('fsdp', 'pair')), may hold values from -6 to 6
- lengths: int32 [2, 32], replicated, may hold values from 65 to 128, as said below
- order: int32 [2, 32], replicated, may hold values from 0 to 31, each once within a row
- norm_gain: bfloat16 [2048], P(('fsdp', 'pair')), may hold values from 0.5 to 1.5
- w_query: bfloat16 [2048, 256], P(('fsdp', 'pair')), may hold values from -0.125 to 0.125
- w_key: bfloat16 [2048, 256], P(('fsdp', 'pair')), may hold values from -0.125 to 0.125
- w_value: bfloat16 [2048, 2048], P(('fsdp', 'pair')), may hold values from -0.125 to 0.125
- w_out: bfloat16 [2048, 2048], P(('fsdp', 'pair')), may hold values from -1 to 1
- mlp_gain: bfloat16 [2048], P(('fsdp', 'pair')), may hold values from 0.5 to 1.5
- w_gate: bfloat16 [2048, 5632], P(('fsdp', 'pair')), may hold values from -0.125 to 0.125
- w_up: bfloat16 [2048, 5632], P(('fsdp', 'pair')), may hold values from -0.125 to 0.125
- w_down: bfloat16 [5632, 2048], P(('fsdp', 'pair')), may hold values from -0.078125 to 0.078125
Outputs:
- activations: bfloat16 [2, 128, 32, 2048], P(None, ('fsdp', 'pair'))
- input_grad: bfloat16 [2, 128, 32, 2048], P(None, ('fsdp', 'pair'))
- grad_norm_gain: float32 [2048], P(('fsdp', 'pair'))
- grad_query: float32 [2048, 256], P(('fsdp', 'pair'))
- grad_key: float32 [2048, 256], P(('fsdp', 'pair'))
- grad_value: float32 [2048, 2048], P(('fsdp', 'pair'))
- grad_out: float32 [2048, 2048], P(('fsdp', 'pair'))
- grad_mlp_gain: float32 [2048], P(('fsdp', 'pair'))
- grad_gate: float32 [2048, 5632], P(('fsdp', 'pair'))
- grad_up: float32 [2048, 5632], P(('fsdp', 'pair'))
- grad_down: float32 [5632, 2048], P(('fsdp', 'pair'))
Inputs may be any that keep to these rules, and one draw needn't show every extreme that they name: lengths[m, j] counts the live positions of sequence order[m, j]; in every micro-batch some sequence has all 128 positions live. Each row order[m, :] is a permutation of the sequences.
All inputs are finite; a program needn't handle non-finite values.
Results may differ from a plain program's by a relative error of at most 0.013.
Values may be sent and summed in bfloat16 or wider, within the bound.
A program may use at most 448 MiB of HBM per device.

v0:
```python
import jax
import jax.numpy as jnp
from jax import lax
from jax.sharding import PartitionSpec as P

HEADS = 16


PRECISE = lax.Precision.HIGHEST
EPSILON = 1e-06


def for_sending(shard):

    def short(part):
        return part.astype(jnp.bfloat16) if part.dtype == jnp.float32 else part

    return jax.tree.map(short, shard)


def take_rows(left, right):
    return lax.dot_general(
        left, right, (((0,), (0,)), ((), ())), preferred_element_type=jnp.float32
    )


def back_cols(left, right):
    return lax.dot_general(
        left, right, (((1,), (1,)), ((), ())), preferred_element_type=jnp.float32
    )


def kernel_terms(query, keys, length):
    seq_len = query.shape[0]
    features = query.shape[1] // HEADS
    query_heads = query.reshape(seq_len, HEADS, features)
    key_heads = keys.reshape(seq_len, HEADS, features)
    scores = jnp.einsum(
        "ihe,jhe->hij", query_heads, key_heads, preferred_element_type=jnp.float32
    ) * features ** (-0.5)
    row_ids = lax.broadcasted_iota(jnp.int32, (seq_len, seq_len), 0)
    col_ids = lax.broadcasted_iota(jnp.int32, (seq_len, seq_len), 1)
    key_mask = (col_ids <= row_ids) & (col_ids < length)
    kernel = jnp.where(key_mask[None], 1.0 + scores + 0.5 * scores * scores, 0.0)
    return (kernel, key_mask, scores)


def forward_one(start_rows, cot_rows, length, weights):
    norm_gain, w_query, w_key, w_value, w_out, mlp_gain, w_gate, w_up, w_down = weights
    seq_len, model_width = start_rows.shape
    start = start_rows.astype(jnp.float32)
    scale1 = lax.rsqrt(jnp.mean(start * start, -1, keepdims=True) + EPSILON)
    normed1 = start * scale1
    hidden1 = (normed1 * norm_gain.astype(jnp.float32)).astype(jnp.bfloat16)
    query = jnp.dot(hidden1, w_query, preferred_element_type=jnp.float32).astype(jnp.bfloat16)
    keys = jnp.dot(hidden1, w_key, preferred_element_type=jnp.float32).astype(jnp.bfloat16)
    values = jnp.dot(hidden1, w_value, preferred_element_type=jnp.float32).astype(jnp.bfloat16)
    kernel, key_mask, scores = kernel_terms(query, keys, length)
    denom = jnp.sum(kernel, -1)
    probs = (kernel / denom[..., None]).astype(jnp.bfloat16)
    value_heads = values.reshape(seq_len, HEADS, model_width // HEADS)
    mixed = jnp.einsum("hij,jhe->ihe", probs, value_heads, preferred_element_type=jnp.float32)
    attended = mixed.reshape(seq_len, model_width).astype(jnp.bfloat16)
    resid = start + jnp.dot(attended, w_out, preferred_element_type=jnp.float32)
    scale2 = lax.rsqrt(jnp.mean(resid * resid, -1, keepdims=True) + EPSILON)
    normed2 = resid * scale2
    hidden2 = (normed2 * mlp_gain.astype(jnp.float32)).astype(jnp.bfloat16)
    gate_pre = jnp.dot(hidden2, w_gate, preferred_element_type=jnp.float32)
    up_pre = jnp.dot(hidden2, w_up, preferred_element_type=jnp.float32)
    inner = (gate_pre * jax.nn.sigmoid(gate_pre) * up_pre).astype(jnp.bfloat16)
    result = resid + jnp.dot(inner, w_down, preferred_element_type=jnp.float32)
    saved = (
        cot_rows,
        length,
        normed1,
        scale1,
        hidden1,
        query,
        keys,
        values,
        denom,
        attended,
        normed2,
        scale2,
        hidden2,
        gate_pre,
        up_pre,
        inner,
    )
    return (result, saved)


def backward_one(saved, weights):
    norm_gain, w_query, w_key, w_value, w_out, mlp_gain, w_gate, w_up, w_down = weights
    (
        cot_rows,
        length,
        normed1,
        scale1,
        hidden1,
        query,
        keys,
        values,
        denom,
        attended,
        normed2,
        scale2,
        hidden2,
        gate_pre,
        up_pre,
        inner,
    ) = saved
    seq_len, model_width = normed1.shape
    live_rows = lax.broadcasted_iota(jnp.int32, (seq_len, 1), 0) < length
    d_out = jnp.where(live_rows, cot_rows, jnp.zeros_like(cot_rows))
    d_inner = back_cols(d_out, w_down)
    sigma = jax.nn.sigmoid(gate_pre)
    d_gate = (d_inner * up_pre * sigma * (1.0 + gate_pre * (1.0 - sigma))).astype(jnp.bfloat16)
    d_up = (d_inner * gate_pre * sigma).astype(jnp.bfloat16)
    d_hidden2 = back_cols(d_gate, w_gate) + back_cols(d_up, w_up)
    g_mlp = jnp.sum(d_hidden2 * normed2, 0)
    d_norm2 = d_hidden2 * mlp_gain.astype(jnp.float32)
    d_resid = d_out.astype(jnp.float32) + scale2 * (
        d_norm2 - normed2 * jnp.mean(d_norm2 * normed2, -1, keepdims=True)
    )
    d_branch = d_resid.astype(jnp.bfloat16)
    d_attended = back_cols(d_branch, w_out).astype(jnp.bfloat16)
    kernel, key_mask, scores = kernel_terms(query, keys, length)
    probs = kernel / denom[..., None]
    value_heads = values.reshape(seq_len, HEADS, model_width // HEADS)
    grad_heads = d_attended.reshape(seq_len, HEADS, model_width // HEADS)
    d_probs = jnp.einsum(
        "ihe,jhe->hij", grad_heads, value_heads, preferred_element_type=jnp.float32
    )
    d_values = jnp.einsum(
        "hij,ihe->jhe", probs.astype(jnp.bfloat16), grad_heads, preferred_element_type=jnp.float32
    )
    d_values = d_values.reshape(seq_len, model_width).astype(jnp.bfloat16)
    d_kernel = (d_probs - jnp.sum(d_probs * probs, -1, keepdims=True)) / denom[..., None]
    features = query.shape[1] // HEADS
    d_scores = jnp.where(key_mask[None], d_kernel * (1.0 + scores), 0.0) * features ** (-0.5)
    query_heads = query.reshape(seq_len, HEADS, features).astype(jnp.float32)
    key_heads = keys.reshape(seq_len, HEADS, features).astype(jnp.float32)
    d_query = (
        jnp.einsum("hij,jhe->ihe", d_scores, key_heads, precision=PRECISE)
        .reshape(seq_len, -1)
        .astype(jnp.bfloat16)
    )
    d_keys = (
        jnp.einsum("hij,ihe->jhe", d_scores, query_heads, precision=PRECISE)
        .reshape(seq_len, -1)
        .astype(jnp.bfloat16)
    )
    d_hidden1 = (
        back_cols(d_query, w_query) + back_cols(d_keys, w_key) + back_cols(d_values, w_value)
    )
    g_norm = jnp.sum(d_hidden1 * normed1, 0)
    d_norm1 = d_hidden1 * norm_gain.astype(jnp.float32)
    d_start = d_resid + scale1 * (
        d_norm1 - normed1 * jnp.mean(d_norm1 * normed1, -1, keepdims=True)
    )
    record_rows = (
        hidden1,
        d_query,
        d_keys,
        d_values,
        attended,
        d_branch,
        hidden2,
        d_gate,
        d_up,
        inner,
        d_out,
    )
    return (d_start.astype(jnp.bfloat16), record_rows, (g_norm, g_mlp))


def owner_sums(terms):
    arrived = jax.tree.map(
        lambda part, own: part.astype(own.dtype),
        lax.all_to_all(
            for_sending(terms), ("fsdp", "pair"), split_axis=0, concat_axis=0, tiled=True
        ),
        terms,
    )
    count = lax.axis_size(("fsdp", "pair"))
    return tuple(
        (
            jnp.sum(piece.reshape(count, piece.shape[0] // count, piece.shape[1]), 0)
            for piece in arrived
        )
    )


def restore(arrived, permuted):
    inverse = (
        jnp.zeros_like(permuted).at[permuted].set(jnp.arange(permuted.shape[0], dtype=jnp.int32))
    )
    return jnp.take(arrived, inverse, axis=1)


def fetch_backward(owned):
    return (
        lax.all_gather(owned[0], ("fsdp", "pair"), axis=0, tiled=True),
        lax.all_gather(owned[1], ("fsdp", "pair"), axis=0, tiled=True),
        lax.all_gather(owned[2], ("fsdp", "pair"), axis=0, tiled=True),
        lax.all_gather(owned[3], ("fsdp", "pair"), axis=0, tiled=True),
        lax.all_gather(owned[4], ("fsdp", "pair"), axis=0, tiled=True),
        lax.all_gather(owned[5], ("fsdp", "pair"), axis=0, tiled=True),
        lax.all_gather(owned[6], ("fsdp", "pair"), axis=0, tiled=True),
        lax.all_gather(owned[7], ("fsdp", "pair"), axis=0, tiled=True),
        lax.all_gather(owned[8], ("fsdp", "pair"), axis=0, tiled=True),
    )


def add_tuples(first_tuple, second_tuple):
    return tuple((first + second for first, second in zip(first_tuple, second_tuple)))


def on_device(
    tokens,
    cotangent,
    lengths,
    order,
    norm_gain,
    w_query,
    w_key,
    w_value,
    w_out,
    mlp_gain,
    w_gate,
    w_up,
    w_down,
):
    owned = (norm_gain, w_query, w_key, w_value, w_out, mlp_gain, w_gate, w_up, w_down)
    batches = tokens.shape[0]
    device_index = lax.axis_index(("fsdp", "pair"))
    stored = []
    outputs = []
    for micro_step in range(batches):
        weights = (
            lax.all_gather(owned[0], ("fsdp", "pair"), axis=0, tiled=True),
            lax.all_gather(owned[1], ("fsdp", "pair"), axis=0, tiled=True),
            lax.all_gather(owned[2], ("fsdp", "pair"), axis=0, tiled=True),
            lax.all_gather(owned[3], ("fsdp", "pair"), axis=0, tiled=True),
            lax.all_gather(owned[4], ("fsdp", "pair"), axis=0, tiled=True),
            lax.all_gather(owned[5], ("fsdp", "pair"), axis=0, tiled=True),
            lax.all_gather(owned[6], ("fsdp", "pair"), axis=0, tiled=True),
            lax.all_gather(owned[7], ("fsdp", "pair"), axis=0, tiled=True),
            lax.all_gather(owned[8], ("fsdp", "pair"), axis=0, tiled=True),
        )
        permuted = order[micro_step]
        dealt_tokens, dealt_cots = (
            lax.all_to_all(
                jnp.take(tokens[micro_step], permuted, axis=1),
                ("fsdp", "pair"),
                split_axis=1,
                concat_axis=0,
                tiled=True,
            ),
            lax.all_to_all(
                jnp.take(cotangent[micro_step], permuted, axis=1),
                ("fsdp", "pair"),
                split_axis=1,
                concat_axis=0,
                tiled=True,
            ),
        )
        length = lengths[micro_step][device_index]
        result, saved = forward_one(dealt_tokens[:, 0, :], dealt_cots[:, 0, :], length, weights)
        arrived = lax.all_to_all(
            result.astype(jnp.bfloat16)[:, None, :],
            ("fsdp", "pair"),
            split_axis=0,
            concat_axis=1,
            tiled=True,
        )
        outputs.append(restore(arrived, permuted))
        stored.append(saved)
    input_grads = [None] * batches
    records = [None] * batches
    gain_totals = None
    for micro_step in reversed(range(batches)):
        weights = fetch_backward(owned)
        d_start, record_rows, gain_sums = backward_one(stored[micro_step], weights)
        stored[micro_step] = None
        arrived = lax.all_to_all(
            d_start[:, None, :], ("fsdp", "pair"), split_axis=0, concat_axis=1, tiled=True
        )
        input_grads[micro_step] = restore(arrived, order[micro_step])
        records[micro_step] = record_rows
        gain_totals = gain_sums if gain_totals is None else add_tuples(gain_totals, gain_sums)
    joined = tuple(
        (
            jnp.concatenate([records[step][index] for step in range(batches)], 0)
            for index in range(11)
        )
    )
    hidden1, d_query, d_keys, d_values, attended, d_branch, hidden2, d_gate, d_up, inner, d_out = (
        joined
    )
    gain_cols = jnp.stack([gain_totals[0], gain_totals[1]], 1)
    g_query, g_key, g_value, g_out, g_gains = owner_sums(
        (
            take_rows(hidden1, d_query),
            take_rows(hidden1, d_keys),
            take_rows(hidden1, d_values),
            take_rows(attended, d_branch),
            gain_cols,
        )
    )
    g_gate, g_up = owner_sums((take_rows(hidden2, d_gate), take_rows(hidden2, d_up)))
    (g_down,) = owner_sums((take_rows(inner, d_out),))
    return (
        jnp.stack(outputs),
        jnp.stack(input_grads),
        g_gains[:, 0],
        g_query,
        g_key,
        g_value,
        g_out,
        g_gains[:, 1],
        g_gate,
        g_up,
        g_down,
    )


def solution(mesh):
    placed = (
        P(None, ("fsdp", "pair"), None, None),
        P(None, ("fsdp", "pair"), None, None),
        P(),
        P(),
        P(("fsdp", "pair")),
        P(("fsdp", "pair"), None),
        P(("fsdp", "pair"), None),
        P(("fsdp", "pair"), None),
        P(("fsdp", "pair"), None),
        P(("fsdp", "pair")),
        P(("fsdp", "pair"), None),
        P(("fsdp", "pair"), None),
        P(("fsdp", "pair"), None),
    )
    return jax.shard_map(
        on_device,
        mesh=mesh,
        in_specs=placed,
        out_specs=(
            P(None, ("fsdp", "pair"), None, None),
            P(None, ("fsdp", "pair"), None, None),
            P(("fsdp", "pair")),
            P(("fsdp", "pair"), None),
            P(("fsdp", "pair"), None),
            P(("fsdp", "pair"), None),
            P(("fsdp", "pair"), None),
            P(("fsdp", "pair")),
            P(("fsdp", "pair"), None),
            P(("fsdp", "pair"), None),
            P(("fsdp", "pair"), None),
        ),
        check_vma=False,
    )
```

profile of v0, /device:TPU:16, one launch (start us, length us, event | category | flops | bytes accessed | tf_op | source)
XLA Modules:
  0.0 3027.9 jit_solution(17829190983073693812)
XLA Ops:
  17.9 20.7 all_to_all.189
  46.3 12.2 all-to-all-done.2
  63.2 40.3 %all-reduce.2 = (bf16[2048]{0:T(1024)(128)(2,1)S(1)}, bf16[2048]{0:T(1024)(128)(2,1)S(1)}) all-reduce(bf16[2048]{0:T(1024)(128)(2,1)S(1)} %dynamic-update-slice, bf16[2048]{0:T(1024)(128)(2,1)S(1)} %dynamic-update-slice.1), channel_id=1, replica_groups=mesh['fsdp'=16,'pair'=2] {'fsdp','pair'}, use_global_device_ids=true, to_apply=%add | all-reduce | flops 4096 | bytes 16384
  111.5 14.8 all-to-all-done
  139.2 66.1 %all-gather.8.cloned.1.call-done = bf16[2048,2048]{1,0:T(8,128)(2,1)} async-done(((bf16[64,2048]{1,0:T(8,128)(2,1)}), bf16[2048,2048]{1,0:T(8,128)(2,1)}) %all-gather.8.cloned.1.call-update) | async-done | bytes 8388624 | tf_op jit(solution)/shard_map/all_gather | solution.py:245
  212.1 71.9 %all-gather.14.cloned.1.call-done = bf16[2048,2048]{1,0:T(8,128)(2,1)} async-done(((bf16[64,2048]{1,0:T(8,128)(2,1)}), bf16[2048,2048]{1,0:T(8,128)(2,1)}) %all-gather.14.cloned.1.call-update) | async-done | bytes 8388624 | tf_op jit(solution)/shard_map/all_gather | solution.py:246
  289.9 139.7 %all-gather.18.cloned.1.call-done = bf16[2048,5632]{1,0:T(8,128)(2,1)} async-done(((bf16[64,5632]{1,0:T(8,128)(2,1)}), bf16[2048,5632]{1,0:T(8,128)(2,1)}) %all-gather.18.cloned.1.call-update) | async-done | bytes 23068688 | tf_op jit(solution)/shard_map/all_gather | solution.py:249
  429.6 12.5 fusion.102
  442.1 133.1 %all-gather.16.cloned.1.call-done = bf16[2048,5632]{1,0:T(8,128)(2,1)} async-done(((bf16[64,5632]{1,0:T(8,128)(2,1)}), bf16[2048,5632]{1,0:T(8,128)(2,1)}) %all-gather.16.cloned.1.call-update) | async-done | bytes 23068688 | tf_op jit(solution)/shard_map/all_gather | solution.py:248
  575.2 13.0 fusion.101
  588.1 132.7 %all-gather.20.cloned.1.call-done = bf16[5632,2048]{1,0:T(8,128)(2,1)} async-done(((bf16[176,2048]{1,0:T(8,128)(2,1)}), bf16[5632,2048]{1,0:T(8,128)(2,1)}) %all-gather.20.cloned.1.call-update) | async-done | bytes 23068688 | tf_op jit(solution)/shard_map/all_gather | solution.py:250
  720.9 15.4 multiply_convert_fusion.2
  736.2 13.0 fusion.105
  749.3 13.6 multiply_reduce_fusion
  811.4 13.1 fusion.104
  830.6 15.4 multiply_convert_fusion
  846.0 13.1 fusion.108
  859.1 13.0 multiply_reduce_fusion.1
  907.4 12.0 fusion.16
  992.4 13.0 all-to-all-done.7
  1011.9 23.8 all-to-all-done.10
  1047.2 18.3 all-to-all-done.9
  1076.8 176.1 %all-to-all-done.11 = bf16[32,64,2048]{2,1,0:T(8,128)(2,1)} async-done(((bf16[32,64,2048]{2,1,0:T(8,128)(2,1)}), bf16[32,64,2048]{2,1,0:T(8,128)(2,1)}, u32[]{:S(2)}, u32[]{:S(2)}) %all-to-all-start.11) | async-done | bytes 8388640 | tf_op jit(solution)/shard_map/all_to_all | solution.py:181
  1262.5 12.3 convolution_convert_fusion.1
  1274.8 169.5 %all-to-all-done.12 = bf16[32,64,2048]{2,1,0:T(8,128)(2,1)} async-done(((bf16[32,64,2048]{2,1,0:T(8,128)(2,1)}), bf16[32,64,2048]{2,1,0:T(8,128)(2,1)}, u32[]{:S(2)}, u32[]{:S(2)}) %all-to-all-start.12) | async-done | bytes 8388640 | tf_op jit(solution)/shard_map/all_to_all | solution.py:181
  1453.9 12.3 convolution_convert_fusion.2
  1466.2 493.6 %all-to-all-done.14 = bf16[32,64,5632]{2,1,0:T(8,128)(2,1)} async-done(((bf16[32,64,5632]{2,1,0:T(8,128)(2,1)}), bf16[32,64,5632]{2,1,0:T(8,128)(2,1)}, u32[]{:S(2)}, u32[]{:S(2)}) %all-to-all-start.14) | async-done | bytes 23068704 | tf_op jit(solution)/shard_map/all_to_all | solution.py:181
  1959.8 19.7 all-to-all-start.13
  1979.6 11.9 convolution_convert_fusion
  1991.5 493.8 %all-to-all-done.13 = bf16[32,64,5632]{2,1,0:T(8,128)(2,1)} async-done(((bf16[32,64,5632]{2,1,0:T(8,128)(2,1)}), bf16[32,64,5632]{2,1,0:T(8,128)(2,1)}, u32[]{:S(2)}, u32[]{:S(2)}) %all-to-all-start.13) | async-done | bytes 23068704 | tf_op jit(solution)/shard_map/all_to_all | solution.py:181
  2485.3 19.4 all-to-all-start.15
  2578.3 432.3 %all-to-all-done.15 = bf16[32,176,2048]{2,1,0:T(8,128)(2,1)} async-done(((bf16[32,176,2048]{2,1,0:T(8,128)(2,1)}), bf16[32,176,2048]{2,1,0:T(8,128)(2,1)}, u32[]{:S(2)}, u32[]{:S(2)}) %all-to-all-start.15) | async-done | bytes 23068704 | tf_op jit(solution)/shard_map/all_to_all | solution.py:181
  (375 shorter events, 350.3 us)
Async XLA Ops:
  7.2 127.1 %all-gather.12.cloned.1.call-start = ((), (), s32[]{:S(2)}) async-start(), calls=%async_computation.18 | async-start | bytes 1081344 | tf_op jit(solution)/shard_map/all_gather | solution.py:244
  7.9 128.2 %all-gather.10.cloned.1.call-start = ((), (), s32[]{:S(2)}) async-start(), calls=%async_computation.17 | async-start | bytes 1081344 | tf_op jit(solution)/shard_map/all_gather | solution.py:243
  8.7 196.6 %all-gather.8.cloned.1.call-start = ((), (), s32[]{:S(2)}) async-start(), calls=%async_computation.16 | async-start | bytes 8650752 | tf_op jit(solution)/shard_map/all_gather | solution.py:245
  9.4 274.6 %all-gather.14.cloned.1.call-start = ((), (), s32[]{:S(2)}) async-start(), calls=%async_computation.19 | async-start | bytes 8650752 | tf_op jit(solution)/shard_map/all_gather | solution.py:246
  10.0 419.6 %all-gather.18.cloned.1.call-start = ((), (), s32[]{:S(2)}) async-start(), calls=%async_computation.21 | async-start | bytes 23789568 | tf_op jit(solution)/shard_map/all_gather | solution.py:249
  10.6 564.6 %all-gather.16.cloned.1.call-start = ((), (), s32[]{:S(2)}) async-start(), calls=%async_computation.20 | async-start | bytes 23789568 | tf_op jit(solution)/shard_map/all_gather | solution.py:248
  11.2 709.7 %all-gather.20.cloned.1.call-start = ((), (), s32[]{:S(2)}) async-start(), calls=%async_computation.22 | async-start | bytes 23789568 | tf_op jit(solution)/shard_map/all_gather | solution.py:250
  38.6 19.9 all-to-all-start.2
  42.7 60.8 %copy-start.80 = (s32[2,32]{1,0:T(2,128)S(1)}, s32[2,32]{1,0:T(2,128)}, u32[]{:S(2)}) copy-start(s32[2,32]{1,0:T(2,128)} %param.17) | copy-start | bytes 772
  58.5 45.7 %all-to-all-start.4 = ((bf16[4,32,2048]{2,0,1:T(4,128)(2,1)}), bf16[4,32,2048]{2,0,1:T(4,128)(2,1)S(1)}, u32[]{:S(2)}, u32[]{:S(2)}) async-start(bf16[4,32,2048]{2,0,1:T(4,128)(2,1)} %get-tuple-element.82), calls=%async_computation.4 | async-start | bytes 1048576 | tf_op jit(solution)/shard_map/all_to_all | solution.py:261
  104.2 22.1 all-to-all-start
  109.9 762.2 %copy-start.67 = (pred[128]{0:T(512)(128)(4,1)}, pred[128]{0:T(512)(128)(4,1)S(1)}, u32[]{:S(2)}) copy-start(pred[128]{0:T(512)(128)(4,1)S(1)} %iota_compare_fusion.1) | copy-start | bytes 388
  110.6 652.4 %copy-start.73 = (pred[128]{0:T(512)(128)(4,1)}, pred[128]{0:T(512)(128)(4,1)S(1)}, u32[]{:S(2)}) copy-start(pred[128]{0:T(512)(128)(4,1)S(1)} %iota_compare_fusion.2) | copy-start | bytes 388
  111.4 787.6 %copy-start.69 = (f32[128]{0:T(128)}, f32[128]{0:T(128)S(1)}, u32[]{:S(2)}) copy-start(f32[128]{0:T(128)S(1)} %rsqrt.42) | copy-start | bytes 1540
  132.1 672.2 %copy-start.2 = (f32[128,2048]{1,0:T(8,128)}, f32[128,2048]{1,0:T(8,128)S(1)}, u32[]{:S(2)}) copy-start(f32[128,2048]{1,0:T(8,128)S(1)} %reshape.353) | copy-start | bytes 3145732
  134.2 75.8 %copy-start.4 = (bf16[128,2048]{1,0:T(8,128)(2,1)}, bf16[128,2048]{1,0:T(8,128)(2,1)S(1)}, u32[]{:S(2)}) copy-start(bf16[128,2048]{1,0:T(8,128)(2,1)S(1)} %multiply_convert_fusion.9) | copy-start | bytes 1572868
  136.1 74.0 %copy-start.59 = (bf16[128,256]{0,1:T(8,128)(2,1)}, bf16[128,256]{0,1:T(8,128)(2,1)S(1)}, u32[]{:S(2)}) copy-start(bf16[128,256]{0,1:T(8,128)(2,1)S(1)} %copy.111) | copy-start | bytes 196612
  137.8 72.2 %copy-start.63 = (bf16[128,256]{0,1:T(8,128)(2,1)}, bf16[128,256]{0,1:T(8,128)(2,1)S(1)}, u32[]{:S(2)}) copy-start(bf16[128,256]{0,1:T(8,128)(2,1)S(1)} %copy.110) | copy-start | bytes 196612
  139.2 70.9 %copy-start.86 = (f32[16,128]{1,0:T(8,128)}, f32[16,128]{1,0:T(8,128)S(1)}, u32[]{:S(2)}) copy-start(f32[16,128]{1,0:T(8,128)S(1)} %get-tuple-element.88) | copy-start | bytes 24580
  809.6 62.5 %copy-start.71 = (f32[128]{0:T(128)}, f32[128]{0:T(128)S(1)}, u32[]{:S(2)}) copy-start(f32[128]{0:T(128)S(1)} %add_rsqrt_fusion) | copy-start | bytes 1540
  902.8 22.3 all-to-all-start.8
  925.1 20.5 all-to-all-start.1
  945.5 20.8 all-to-all-start.5
  966.3 20.4 all-to-all-start.3
  986.8 18.6 all-to-all-start.7
  1006.2 29.4 all-to-all-start.10
  1035.6 29.9 all-to-all-start.9
  1066.5 186.5 %all-to-all-start.11 = ((bf16[32,64,2048]{2,1,0:T(8,128)(2,1)}), bf16[32,64,2048]{2,1,0:T(8,128)(2,1)}, u32[]{:S(2)}, u32[]{:S(2)}) async-start(bf16[32,64,2048]{2,1,0:T(8,128)(2,1)} %bitcast.236), calls=%async_computation.11 | async-start | bytes 16777216 | tf_op jit(solution)/shard_map/all_to_all | solution.py:181
  1252.9 191.4 %all-to-all-start.12 = ((bf16[32,64,2048]{2,1,0:T(8,128)(2,1)}), bf16[32,64,2048]{2,1,0:T(8,128)(2,1)}, u32[]{:S(2)}, u32[]{:S(2)}) async-start(bf16[32,64,2048]{2,1,0:T(8,128)(2,1)} %bitcast.237), calls=%async_computation.12 | async-start | bytes 16777216 | tf_op jit(solution)/shard_map/all_to_all | solution.py:181
  1444.3 515.5 %all-to-all-start.14 = ((bf16[32,64,5632]{2,1,0:T(8,128)(2,1)}), bf16[32,64,5632]{2,1,0:T(8,128)(2,1)}, u32[]{:S(2)}, u32[]{:S(2)}) async-start(bf16[32,64,5632]{2,1,0:T(8,128)(2,1)} %bitcast.234), calls=%async_computation.14 | async-start | bytes 46137344 | tf_op jit(solution)/shard_map/all_to_all | solution.py:181
  1959.8 525.5 %all-to-all-start.13 = ((bf16[32,64,5632]{2,1,0:T(8,128)(2,1)}), bf16[32,64,5632]{2,1,0:T(8,128)(2,1)}, u32[]{:S(2)}, u32[]{:S(2)}) async-start(bf16[32,64,5632]{2,1,0:T(8,128)(2,1)} %bitcast.233), calls=%async_computation.13 | async-start | bytes 46137344 | tf_op jit(solution)/shard_map/all_to_all | solution.py:181
  2485.3 525.3 %all-to-all-start.15 = ((bf16[32,176,2048]{2,1,0:T(8,128)(2,1)}), bf16[32,176,2048]{2,1,0:T(8,128)(2,1)}, u32[]{:S(2)}, u32[]{:S(2)}) async-start(bf16[32,176,2048]{2,1,0:T(8,128)(2,1)} %bitcast.235), calls=%async_computation.15 | async-start | bytes 46137344 | tf_op jit(solution)/shard_map/all_to_all | solution.py:181
  (86 other events, 810.8 us)
Sparse Core Ops, SparseCore 0:
  10.9 55.2 all-gather.11
  69.1 55.2 all-gather.9
  127.4 77.8 all-gather.7
  208.1 75.8 all-gather.13
  286.8 142.7 all-gather.17
  432.3 142.7 all-gather.15
  578.0 142.7 all-gather.19
where the time goes:
time: 3050 us; the launch traced here: 3030 us
  waiting for transfers between devices  2410 us (79%)
  matrix products  284 us (9%)
  starting transfers between devices  110 us (4%)
  other arithmetic  90.3 us (3%)
  blocking collectives  61 us (2%)
  local copies, waits for them, and re-layouts  53.5 us (2%)
    all_to_all x8, waiting for transfers between devices, owner_sums(): lax.all_to_all(for_sending(terms), ('fsdp', 'pair'), split_axis=0, concat...  1810 us
    all_gather x1, waiting for transfers between devices, on_device(): lax.all_gather(owned[7], ('fsdp', 'pair'), axis=0, tiled=True)  140 us
    all_gather x1, waiting for transfers between devices, on_device(): lax.all_gather(owned[6], ('fsdp', 'pair'), axis=0, tiled=True)  133 us
    all_gather x1, waiting for transfers between devices, on_device(): lax.all_gather(owned[8], ('fsdp', 'pair'), axis=0, tiled=True)  133 us
    dot_general x14, matrix products, back_cols(): lax.dot_general(left, right, (((1,), (1,)), ((), ())), preferred_element_...  115 us
    all_to_all x8, starting transfers between devices, owner_sums(): lax.all_to_all(for_sending(terms), ('fsdp', 'pair'), split_axis=0, concat...  76.3 us
    all_gather x1, waiting for transfers between devices, on_device(): lax.all_gather(owned[4], ('fsdp', 'pair'), axis=0, tiled=True)  71.9 us
    all_gather x1, waiting for transfers between devices, on_device(): lax.all_gather(owned[3], ('fsdp', 'pair'), axis=0, tiled=True)  66.1 us
  transfers between devices with their start and end apart: 22, of which 17 were waited for; matrix products, arithmetic and copies ran while one was open for 8% of the time, Pallas kernels for 0%

commit v1 on v0

--- a/solution.py
+++ b/solution.py
@@ -1,6 +1,12 @@
+import functools
+import math
+
 import jax
 import jax.numpy as jnp
 from jax import lax
+from jax.experimental import pallas as pl
+from jax.experimental.pallas import tpu as pltpu
+from jax.sharding import Mesh
 from jax.sharding import PartitionSpec as P
 
 HEADS = 16
@@ -326,38 +332,375 @@
     )
 
 
+GRID = ("z", "y", "core", "pair")
+SWAP = ((0, 1), (1, 0))
+
+
+def swap(value, axis):
+    return lax.ppermute(value, axis, SWAP)
+
+
+def from_above(value, hops, size):
+    return lax.ppermute(value, "z", [((i + hops) % size, i) for i in range(size)])
+
+
+def matmul(left, right):
+    return jnp.dot(left, right, preferred_element_type=jnp.float32)
+
+
+def place_kernel(depth, *refs):
+    blocks, whole, held, sems = refs[: 2 * depth], *refs[2 * depth :]
+    z, y = lax.axis_index("z"), lax.axis_index("y")
+    fetched, placed = [], []
+    for side in range(2):
+        for hops in range(depth):
+            at = lax.rem(z + hops, depth) * 2 + (y if side == 0 else 1 - y)
+            slot = side * depth + hops
+            fetched.append(
+                pltpu.make_async_copy(blocks[slot], held.at[slot], sems.at[0, slot])
+            )
+            placed.append(
+                pltpu.make_async_copy(held.at[slot], whole.at[at], sems.at[1, slot])
+            )
+    for copy in fetched:
+        copy.start()
+    for arrived, copy in zip(fetched, placed):
+        arrived.wait()
+        copy.start()
+    for copy in placed:
+        copy.wait()
+
+
+def place_blocks(blocks):
+    depth = len(blocks) // 2
+    shape, dtype = blocks[0].shape, blocks[0].dtype
+    moved = 4 * depth * math.prod(shape) * dtype.itemsize
+    return pl.pallas_call(
+        functools.partial(place_kernel, depth),
+        out_shape=jax.ShapeDtypeStruct((2 * depth,) + shape, dtype),
+        in_specs=[pl.BlockSpec(memory_space=pl.ANY)] * (2 * depth),
+        out_specs=pl.BlockSpec(memory_space=pl.ANY),
+        scratch_shapes=[
+            pltpu.VMEM((2 * depth,) + shape, dtype),
+            pltpu.SemaphoreType.DMA((2, 2 * depth)),
+        ],
+        cost_estimate=pl.CostEstimate(flops=0, bytes_accessed=moved, transcendentals=0),
+        name="place_blocks",
+    )(*blocks)
+
+
+def gather_zy(block, depth):
+    column = [block] + [from_above(block, hops, depth) for hops in range(1, depth)]
+    return place_blocks(column + [swap(part, "y") for part in column])
+
+
+def reduce_z(partial, depth):
+    z = lax.axis_index("z")
+    total = lax.dynamic_index_in_dim(partial, z, 0, False).astype(jnp.float32)
+    for hops in range(1, depth):
+        sent = lax.dynamic_index_in_dim(
+            partial, lax.rem(z + depth - hops, depth), 0, False
+        )
+        total = total + from_above(sent, hops, depth).astype(jnp.float32)
+    return total
+
+
+def halves(value, index, axis):
+    return (
+        lax.dynamic_index_in_dim(value, index, axis, False),
+        lax.dynamic_index_in_dim(value, 1 - index, axis, False),
+    )
+
+
+def exchange_sum(value, index, axis, name):
+    kept, sent = halves(value, index, axis)
+    return (kept.astype(jnp.float32) + swap(sent, name).astype(jnp.float32)).astype(
+        jnp.bfloat16
+    )
+
+
+def row_norm(value):
+    return lax.rsqrt(jnp.mean(value * value, -1, keepdims=True) + EPSILON)
+
+
+def norm_back(d_hidden, normed, scale, gain):
+    d_norm = d_hidden * gain
+    return scale * (d_norm - normed * jnp.mean(d_norm * normed, -1, keepdims=True))
+
+
+def scores_of(query, keys, lens):
+    seq_len = query.shape[1]
+    features = query.shape[-1]
+    scores = jnp.einsum(
+        "bihe,bjhe->bhij", query, keys, preferred_element_type=jnp.float32
+    ) * features ** (-0.5)
+    row_ids = lax.broadcasted_iota(jnp.int32, (seq_len, seq_len), 0)
+    col_ids = lax.broadcasted_iota(jnp.int32, (seq_len, seq_len), 1)
+    mask = (col_ids <= row_ids)[None] & (col_ids[None] < lens[:, None, None])
+    mask = mask[:, None]
+    kernel = jnp.where(mask, 1.0 + scores + 0.5 * scores * scores, 0.0)
+    denom = jnp.sum(kernel, -1, keepdims=True)
+    return scores, mask, kernel / denom, denom
+
+
+def attend(query, keys, values, lens):
+    _, _, probs, _ = scores_of(query, keys, lens)
+    return jnp.einsum(
+        "bhij,bjhe->bihe", probs.astype(jnp.bfloat16), values, preferred_element_type=jnp.float32
+    ).astype(jnp.bfloat16)
+
+
+def attend_back(query, keys, values, lens, grads):
+    scores, mask, probs, denom = scores_of(query, keys, lens)
+    d_probs = jnp.einsum("bihe,bjhe->bhij", grads, values, preferred_element_type=jnp.float32)
+    d_values = jnp.einsum(
+        "bhij,bihe->bjhe", probs.astype(jnp.bfloat16), grads, preferred_element_type=jnp.float32
+    )
+    d_kernel = (d_probs - jnp.sum(d_probs * probs, -1, keepdims=True)) / denom
+    d_scores = jnp.where(mask, d_kernel * (1.0 + scores), 0.0) * query.shape[-1] ** (-0.5)
+    d_scores = d_scores.astype(jnp.bfloat16)
+    d_query = jnp.einsum("bhij,bjhe->bihe", d_scores, keys, preferred_element_type=jnp.float32)
+    d_keys = jnp.einsum("bhij,bihe->bjhe", d_scores, query, preferred_element_type=jnp.float32)
+    return tuple(part.astype(jnp.bfloat16) for part in (d_query, d_keys, d_values))
+
+
+def share_four(mine):
+    near = swap(mine, "core")
+    across = swap(mine, "pair")
+    return jnp.concatenate([mine, near, across, swap(across, "core")], 0)
+
+
+def sum_four(partial):
+    count = partial.shape[0] // 4
+    mine, near, across, far = (partial[i * count : (i + 1) * count] for i in range(4))
+    got = swap(jnp.concatenate([near, far], 0).astype(jnp.bfloat16), "core").astype(jnp.float32)
+    across = (across + got[count:]).astype(jnp.bfloat16)
+    return mine + got[:count] + swap(across, "pair").astype(jnp.float32)
+
+
+def on_grid(
+    depth,
+    tokens,
+    cotangent,
+    lengths,
+    order,
+    norm_gain,
+    w_query,
+    w_key,
+    w_value,
+    w_out,
+    mlp_gain,
+    w_gate,
+    w_up,
+    w_down,
+):
+    batches, _, seqs, width = tokens.shape
+    core, pair = lax.axis_index("core"), lax.axis_index("pair")
+    y = lax.axis_index("y")
+    device_index = lax.axis_index(GRID)
+    planes = 2 * depth
+    rows_in = w_query.shape[0]
+    ff_rows = w_down.shape[0]
+    hidden = w_gate.shape[1]
+    qk_width = w_query.shape[1]
+    own_heads = HEADS // 2
+    features = qk_width // HEADS
+    head_dim = width // HEADS
+
+    def core_columns(weight, step):
+        return weight.reshape(rows_in, planes, 2, step)
+
+    def half_heads(index):
+        return jnp.concatenate(
+            [
+                lax.dynamic_index_in_dim(core_columns(weight, step), index, 2, False).reshape(rows_in, -1)
+                for weight, step in ((w_query, features), (w_key, features), (w_value, head_dim))
+            ],
+            1,
+        )
+
+    qkv_mine = half_heads(core)
+    qkv_got = swap(half_heads(1 - core), "core")
+    qkv_block = jnp.where(
+        core == 0, jnp.stack([qkv_mine, qkv_got]), jnp.stack([qkv_got, qkv_mine])
+    ).reshape(2, rows_in, -1)
+    w_qkv = gather_zy(qkv_block, depth)
+    w_qkv_other = swap(w_qkv, "pair")
+    w_qkv = jnp.where(
+        pair == 0, jnp.stack([w_qkv, w_qkv_other], 2), jnp.stack([w_qkv_other, w_qkv], 2)
+    ).reshape(width, -1)
+    w_out_mine = gather_zy(w_out, depth)
+    w_out_other = swap(w_out_mine, "pair")
+    w_out_all = jnp.where(
+        pair == 0, jnp.stack([w_out_mine, w_out_other], 1), jnp.stack([w_out_other, w_out_mine], 1)
+    ).reshape(own_heads * head_dim, width)
+
+    def hidden_block(weight):
+        cut = weight.reshape(rows_in, planes, 2, 2, ff_rows)
+        kept, sent = halves(cut, pair, 3)
+        got = swap(sent.reshape(rows_in, -1), "pair").reshape(kept.shape)
+        by_pair = jnp.where(pair == 0, jnp.stack([kept, got]), jnp.stack([got, kept]))
+        kept, sent = halves(by_pair, core, 3)
+        got = swap(sent.reshape(2, rows_in, -1), "core")
+        kept = kept.reshape(got.shape)
+        by_core = jnp.where(core == 0, jnp.stack([kept, got]), jnp.stack([got, kept]))
+        return by_core.reshape(4 * rows_in, planes * ff_rows)
+
+    w_gate_own = gather_zy(hidden_block(w_gate), depth).reshape(width, -1)
+    w_up_own = gather_zy(hidden_block(w_up), depth).reshape(width, -1)
+    w_down_own = gather_zy(w_down, depth).reshape(-1, width)
+
+    gains = jnp.stack([norm_gain, mlp_gain])
+    gains = lax.all_to_all(
+        jnp.broadcast_to(gains[None], (seqs,) + gains.shape), GRID, split_axis=0, concat_axis=0, tiled=True
+    )
+    gains = gains.transpose(1, 0, 2).reshape(2, 1, width).astype(jnp.float32)
+    gain1, gain2 = gains[0], gains[1]
+
+    def deal(value):
+        dealt = lax.all_to_all(value, GRID, split_axis=2, concat_axis=1, tiled=True)
+        return dealt.reshape(-1, width)
+
+    def undeal(value):
+        return lax.all_to_all(
+            value.reshape(batches, -1, 1, width), GRID, split_axis=1, concat_axis=2, tiled=True
+        )
+
+    start_rows = deal(tokens)
+    cot_rows = deal(cotangent)
+    count = start_rows.shape[0]
+    seq_len = count // batches
+
+    def lens_of(device):
+        return jnp.sum(jnp.where(order == device, lengths, 0), 1)
+
+    lens = jnp.concatenate([lens_of(device_index), lens_of(device_index + 2 - 4 * core)])
+    live = (
+        lax.broadcasted_iota(jnp.int32, (batches, seq_len), 1) < lens[:batches, None]
+    ).reshape(count, 1)
+    d_out = jnp.where(live, cot_rows, jnp.zeros_like(cot_rows))
+    d_out_four = share_four(d_out)
+
+    start = start_rows.astype(jnp.float32)
+    scale1 = row_norm(start)
+    hidden1 = (start * scale1 * gain1).astype(jnp.bfloat16)
+    hidden1 = jnp.concatenate([hidden1, swap(hidden1, "core")], 0)
+    qkv = matmul(hidden1, w_qkv).astype(jnp.bfloat16)
+    own_qk = own_heads * features
+    by_seq = (2 * batches, seq_len, own_heads, -1)
+    query = qkv[:, :own_qk].reshape(by_seq)
+    keys = qkv[:, own_qk : 2 * own_qk].reshape(by_seq)
+    values = qkv[:, 2 * own_qk :].reshape(by_seq)
+    attended = attend(query, keys, values, lens).reshape(2 * count, -1)
+    branch = matmul(attended, w_out_all)
+    resid = start + branch[:count] + swap(branch[count:], "core")
+    scale2 = row_norm(resid)
+    normed2 = resid * scale2
+    hidden2 = share_four((normed2 * gain2).astype(jnp.bfloat16))
+
+    gate_pre = matmul(hidden2, w_gate_own)
+    up_pre = matmul(hidden2, w_up_own)
+    sigma = jax.nn.sigmoid(gate_pre)
+    inner = (gate_pre * sigma * up_pre).astype(jnp.bfloat16)
+    result = resid + sum_four(matmul(inner, w_down_own))
+    activations = undeal(result.astype(jnp.bfloat16))
+
+    def owned_rows(partial):
+        return reduce_z(exchange_sum(partial, y, 1, "y"), depth)
+
+    def grid_rows(value):
+        return value.reshape((depth, 2, -1) + value.shape[1:])
+
+    g_down = owned_rows(grid_rows(take_rows(inner, d_out_four).astype(jnp.bfloat16)))
+
+    d_inner = back_cols(d_out_four, w_down_own)
+    d_gate = (d_inner * up_pre * sigma * (1.0 + gate_pre * (1.0 - sigma))).astype(jnp.bfloat16)
+    d_up = (d_inner * gate_pre * sigma).astype(jnp.bfloat16)
+
+    def owned_hidden(partial):
+        rows = owned_rows(grid_rows(partial)).astype(jnp.bfloat16).reshape(2, 2, rows_in, -1)
+        kept, sent = halves(rows, core, 0)
+        got = swap(sent, "core")
+        rows = jnp.where(core == 0, jnp.stack([kept, got]), jnp.stack([got, kept]))
+        kept, sent = halves(rows, pair, 1)
+        got = swap(sent, "pair")
+        rows = jnp.where(pair == 0, jnp.stack([kept, got], 1), jnp.stack([got, kept], 1))
+        rows = rows.reshape(2, 2, rows_in, planes, ff_rows).transpose(2, 3, 0, 1, 4)
+        return rows.reshape(rows_in, hidden).astype(jnp.float32)
+
+    g_gate = owned_hidden(take_rows(hidden2, d_gate).astype(jnp.bfloat16))
+    g_up = owned_hidden(take_rows(hidden2, d_up).astype(jnp.bfloat16))
+
+    d_hidden2 = sum_four(back_cols(d_gate, w_gate_own) + back_cols(d_up, w_up_own))
+    g_mlp = jnp.sum(d_hidden2 * normed2, 0)
+    d_resid = d_out.astype(jnp.float32) + norm_back(d_hidden2, normed2, scale2, gain2)
+    d_branch = d_resid.astype(jnp.bfloat16)
+    d_branch = jnp.concatenate([d_branch, swap(d_branch, "core")], 0)
+    d_attended = back_cols(d_branch, w_out_all).astype(jnp.bfloat16)
+
+    g_out = take_rows(attended, d_branch).astype(jnp.bfloat16)
+    g_out = exchange_sum(g_out.reshape(planes, 2, rows_in, width), pair, 1, "pair")
+    g_out = owned_rows(grid_rows(g_out.reshape(-1, width)))
+
+    d_query, d_keys, d_values = attend_back(query, keys, values, lens, d_attended.reshape(by_seq))
+    d_qkv = jnp.concatenate(
+        [part.reshape(2 * count, -1) for part in (d_query, d_keys, d_values)], 1
+    )
+    d_hidden1 = back_cols(d_qkv, w_qkv)
+    d_hidden1 = d_hidden1[:count] + swap(d_hidden1[count:], "core")
+    normed1 = start * scale1
+    g_norm = jnp.sum(d_hidden1 * normed1, 0)
+    d_start = d_resid + norm_back(d_hidden1, normed1, scale1, gain1)
+    input_grad = undeal(d_start.astype(jnp.bfloat16))
+
+    g_qkv = take_rows(hidden1, d_qkv).astype(jnp.bfloat16)
+    g_qkv = exchange_sum(g_qkv.reshape(planes, 2, 2, rows_in, -1), pair, 2, "pair")
+    g_qkv = owned_rows(grid_rows(g_qkv.reshape(planes * 2 * rows_in, -1)))
+    kept, sent = halves(g_qkv.astype(jnp.bfloat16).reshape(2, rows_in, -1), core, 0)
+    got = swap(sent, "core")
+    g_qkv = jnp.where(core == 0, jnp.stack([kept, got]), jnp.stack([got, kept]))
+
+    def both_cores(part, step):
+        part = part.reshape(2, rows_in, planes, step).transpose(1, 2, 0, 3)
+        return part.reshape(rows_in, -1).astype(jnp.float32)
+
+    g_query = both_cores(g_qkv[..., :own_qk], features)
+    g_key = both_cores(g_qkv[..., own_qk : 2 * own_qk], features)
+    g_value = both_cores(g_qkv[..., 2 * own_qk :], head_dim)
+
+    g_gains = jnp.stack([g_norm, g_mlp]).reshape(2, seqs, rows_in).transpose(1, 0, 2)
+    g_gains = jnp.sum(
+        lax.all_to_all(g_gains, GRID, split_axis=0, concat_axis=0, tiled=True), 0
+    )
+    return (
+        activations,
+        input_grad,
+        g_gains[0],
+        g_query,
+        g_key,
+        g_value,
+        g_out,
+        g_gains[1],
+        g_gate,
+        g_up,
+        g_down,
+    )
+
+
 def solution(mesh):
-    placed = (
-        P(None, ("fsdp", "pair"), None, None),
-        P(None, ("fsdp", "pair"), None, None),
-        P(),
-        P(),
-        P(("fsdp", "pair")),
-        P(("fsdp", "pair"), None),
-        P(("fsdp", "pair"), None),
-        P(("fsdp", "pair"), None),
-        P(("fsdp", "pair"), None),
-        P(("fsdp", "pair")),
-        P(("fsdp", "pair"), None),
-        P(("fsdp", "pair"), None),
-        P(("fsdp", "pair"), None),
-    )
+    fsdp, pair = mesh.shape["fsdp"], mesh.shape["pair"]
+    names = ("fsdp", "pair")
+    run = on_device
+    if pair == 2 and fsdp == HEADS:
+        names = GRID
+        mesh = Mesh(mesh.devices.reshape(fsdp // 4, 2, 2, 2), GRID)
+        run = functools.partial(on_grid, fsdp // 4)
+    positions = P(None, names, None, None)
+    rows, flat = P(names, None), P(names)
     return jax.shard_map(
-        on_device,
+        run,
         mesh=mesh,
-        in_specs=placed,
-        out_specs=(
-            P(None, ("fsdp", "pair"), None, None),
-            P(None, ("fsdp", "pair"), None, None),
-            P(("fsdp", "pair")),
-            P(("fsdp", "pair"), None),
-            P(("fsdp", "pair"), None),
-            P(("fsdp", "pair"), None),
-            P(("fsdp", "pair"), None),
-            P(("fsdp", "pair")),
-            P(("fsdp", "pair"), None),
-            P(("fsdp", "pair"), None),
-            P(("fsdp", "pair"), None),
-        ),
+        in_specs=(positions, positions, P(), P(), flat, rows, rows, rows, rows, flat, rows, rows, rows),
+        out_specs=(positions, positions, flat, rows, rows, rows, rows, flat, rows, rows, rows),
         check_vma=False,
     )

time: 3050 us -> 1220 us (0.40)
  waiting for transfers between devices: 2410 us -> 695 us
  matrix products: 284 us -> 146 us
  local copies, waits for them, and re-layouts: 53.5 us -> 140 us
  blocking collectives: 61 us -> 0 us
    all_to_all x15 -> x6, waiting for transfers between devices: 1870 us -> 26.2 us  [the longest x1 23.1 us: on_grid(): lax.all_to_all(g_gains, GRID, split_axis=0, concat_axis=0, tiled=True)]
    ppermute x0 -> x83, waiting for transfers between devices: none -> 669 us  [the longest x53 386 us: swap(): return lax.ppermute(value, axis, SWAP)]
    all_gather x7 -> x0, waiting for transfers between devices: 543 us -> none  [the longest x1 140 us: on_device(): lax.all_gather(owned[7], ('fsdp', 'pair'), axis=0, tiled=True)]
    ppermute x0 -> x83, starting transfers between devices: none -> 96.3 us  [the longest x53 50 us: swap(): return lax.ppermute(value, axis, SWAP)]
    all_to_all x15 -> x6, starting transfers between devices: 110 us -> 33 us  [the longest x2 13 us: deal(): dealt = lax.all_to_all(value, GRID, split_axis=2, concat_axis=1, tiled=True)]
    dot_general x14 -> x5, matrix products: 115 us -> 44.3 us  [back_cols(): lax.dot_general(left, right, (((1,), (1,)), ((), ())), preferred_element_...]
    dot_general x26 -> x11, matrix products: 111 us -> 67.6 us  [the longest x5 47.1 us: matmul(): return jnp.dot(left, right, preferred_element_type=jnp.float32)]
    unnamed x1 -> x0, blocking collectives: 40.3 us -> none
  transfers between devices with their start and end apart: 22 -> 89, of which waited for: 17 -> 42; matrix products, arithmetic and copies ran while one was open for 8% -> 25% of each run, Pallas kernels for 0% -> 2%
where the time goes in v1:
time: 1220 us; the launch traced here: 1210 us
  waiting for transfers between devices  695 us (57%)
  matrix products  146 us (12%)
  local copies, waits for them, and re-layouts  140 us (11%)
  starting transfers between devices  129 us (11%)
  other arithmetic  75.7 us (6%)
  Pallas kernels  20.5 us (2%)
    ppermute x53, waiting for transfers between devices, swap(): return lax.ppermute(value, axis, SWAP)  386 us
    ppermute x30, waiting for transfers between devices, from_above(): lax.ppermute(value, 'z', [((i + hops) % size, i) for i in range(size)])  283 us
    ppermute x53, starting transfers between devices, swap(): return lax.ppermute(value, axis, SWAP)  50 us
    dot_general x5, matrix products, matmul(): return jnp.dot(left, right, preferred_element_type=jnp.float32)  47.1 us
    ppermute x30, starting transfers between devices, from_above(): lax.ppermute(value, 'z', [((i + hops) % size, i) for i in range(size)])  46.3 us
    dot_general x5, matrix products, back_cols(): lax.dot_general(left, right, (((1,), (1,)), ((), ())), preferred_element_...  44.3 us
    dot_general x5, matrix products, take_rows(): lax.dot_general(left, right, (((0,), (0,)), ((), ())), preferred_element_...  34.1 us
    unnamed x208, local copies, waits for them, and re-layouts  26.5 us
  transfers between devices with their start and end apart: 89, of which 42 were waited for; matrix products, arithmetic and copies ran while one was open for 25% of the time, Pallas kernels for 2%

profile of v1, /device:TPU:16, one launch (start us, length us, event | category | flops | bytes accessed | tf_op | source)
XLA Modules:
  0.0 1209.7 jit_solution(6407722407637588441)
XLA Ops:
  51.6 26.3 %collective-permute-done.2.refs_1_ = bf16[2,64,1280]{2,1,0:T(8,128)(2,1)} collective-permute-done((bf16[2,64,1280]{2,1,0:T(8,128)(2,1)S(1)}, bf16[2,64,1280]{2,1,0:T(8,128)(2,1)}, u32[]{:S(2)}, u32[]{:S(2)}) %collective-permute-start.2) | collective-permute-done | bytes 327712 | tf_op jit(solution)/shard_map/ppermute | solution.py:344
  134.9 46.2 %collective-permute-done.31 = bf16[64,2816]{1,0:T(8,128)(2,1)} collective-permute-done((bf16[64,2816]{1,0:T(8,128)(2,1)S(1)}, bf16[64,2816]{1,0:T(8,128)(2,1)}, u32[]{:S(2)}, u32[]{:S(2)}) %collective-permute-start.31) | collective-permute-done | bytes 360480 | tf_op jit(solution)/shard_map/ppermute | solution.py:340
  199.6 32.3 %collective-permute-done.17 = bf16[8,64,2048]{2,1,0:T(8,128)(2,1)} collective-permute-done((bf16[8,64,2048]{2,1,0:T(8,128)(2,1)}, bf16[8,64,2048]{2,1,0:T(8,128)(2,1)}, u32[]{:S(2)}, u32[]{:S(2)}) %collective-permute-start.17) | collective-permute-done | bytes 2097184 | tf_op jit(solution)/shard_map/ppermute | solution.py:340
  289.6 31.1 %collective-permute-done.24.refs_1_ = bf16[256,1408]{1,0:T(8,128)(2,1)} collective-permute-done((bf16[256,1408]{1,0:T(8,128)(2,1)}, bf16[256,1408]{1,0:T(8,128)(2,1)}, u32[]{:S(2)}, u32[]{:S(2)}) %collective-permute-start.24) | collective-permute-done | bytes 720928 | tf_op jit(solution)/shard_map/ppermute | solution.py:344
  323.3 36.2 %collective-permute-done.25.refs_2_ = bf16[256,1408]{1,0:T(8,128)(2,1)} collective-permute-done((bf16[256,1408]{1,0:T(8,128)(2,1)}, bf16[256,1408]{1,0:T(8,128)(2,1)}, u32[]{:S(2)}, u32[]{:S(2)}) %collective-permute-start.25) | collective-permute-done | bytes 720928 | tf_op jit(solution)/shard_map/ppermute | solution.py:344
  368.9 13.8 %collective-permute-done.33.refs_1_ = bf16[256,1408]{1,0:T(8,128)(2,1)} collective-permute-done((bf16[256,1408]{1,0:T(8,128)(2,1)}, bf16[256,1408]{1,0:T(8,128)(2,1)}, u32[]{:S(2)}, u32[]{:S(2)}) %collective-permute-start.33) | collective-permute-done | bytes 720928 | tf_op jit(solution)/shard_map/ppermute | solution.py:344
  384.2 12.9 %collective-permute-done.34.refs_2_ = bf16[256,1408]{1,0:T(8,128)(2,1)} collective-permute-done((bf16[256,1408]{1,0:T(8,128)(2,1)}, bf16[256,1408]{1,0:T(8,128)(2,1)}, u32[]{:S(2)}, u32[]{:S(2)}) %collective-permute-start.34) | collective-permute-done | bytes 720928 | tf_op jit(solution)/shard_map/ppermute | solution.py:344
  417.8 13.9 %collective-permute-done.46.refs_7_ = bf16[176,2048]{1,0:T(8,128)(2,1)S(1)} collective-permute-done((bf16[176,2048]{1,0:T(8,128)(2,1)}, bf16[176,2048]{1,0:T(8,128)(2,1)S(1)}, u32[]{:S(2)}, u32[]{:S(2)}) %collective-permute-start.46) | collective-permute-done | bytes 720928 | tf_op jit(solution)/shard_map/ppermute | solution.py:340
  433.6 13.7 %collective-permute-done.28.refs_5_ = bf16[256,1408]{1,0:T(8,128)(2,1)S(1)} collective-permute-done((bf16[256,1408]{1,0:T(8,128)(2,1)}, bf16[256,1408]{1,0:T(8,128)(2,1)S(1)}, u32[]{:S(2)}, u32[]{:S(2)}) %collective-permute-start.28) | collective-permute-done | bytes 720928 | tf_op jit(solution)/shard_map/ppermute | solution.py:340
  448.7 14.0 %collective-permute-done.29.refs_6_ = bf16[256,1408]{1,0:T(8,128)(2,1)S(1)} collective-permute-done((bf16[256,1408]{1,0:T(8,128)(2,1)}, bf16[256,1408]{1,0:T(8,128)(2,1)S(1)}, u32[]{:S(2)}, u32[]{:S(2)}) %collective-permute-start.29) | collective-permute-done | bytes 720928 | tf_op jit(solution)/shard_map/ppermute | solution.py:340
  463.2 14.9 %collective-permute-done.30.refs_7_ = bf16[256,1408]{1,0:T(8,128)(2,1)S(1)} collective-permute-done((bf16[256,1408]{1,0:T(8,128)(2,1)}, bf16[256,1408]{1,0:T(8,128)(2,1)S(1)}, u32[]{:S(2)}, u32[]{:S(2)}) %collective-permute-start.30) | collective-permute-done | bytes 720928 | tf_op jit(solution)/shard_map/ppermute | solution.py:340
  479.6 13.9 %collective-permute-done.37.refs_5_ = bf16[256,1408]{1,0:T(8,128)(2,1)S(1)} collective-permute-done((bf16[256,1408]{1,0:T(8,128)(2,1)}, bf16[256,1408]{1,0:T(8,128)(2,1)S(1)}, u32[]{:S(2)}, u32[]{:S(2)}) %collective-permute-start.37) | collective-permute-done | bytes 720928 | tf_op jit(solution)/shard_map/ppermute | solution.py:340
  509.1 13.5 %collective-permute-done.39.refs_7_ = bf16[256,1408]{1,0:T(8,128)(2,1)} collective-permute-done((bf16[256,1408]{1,0:T(8,128)(2,1)}, bf16[256,1408]{1,0:T(8,128)(2,1)}, u32[]{:S(2)}, u32[]{:S(2)}) %collective-permute-start.39) | collective-permute-done | bytes 720928 | tf_op jit(solution)/shard_map/ppermute | solution.py:340
  528.4 13.0 %fusion.46 = f32[1024,1408]{1,0:T(8,128)} fusion(bf16[1408,2048]{1,0:T(8,128)(2,1)} %bitcast.308, bf16[256,2048]{1,0:T(8,128)(2,1)} %collective-permute-done.51, bf16[256,2048]{1,0:T(8,128)(2,1)} %collective-permute-done.50, bf16[256,2048]{1,0:T(8,128)(2,1)} %collective-permute-done.49, bf16[256,2048]{1,0:T(8,128)(2,1)} %broadcast_select_fusion), kind=kOutput, calls=%fused_computation.126 | convolution fusion | flops 5922357248 | bytes 15728640 | tf_op jit(solution)/shard_map/dot_general | solution.py:34
  552.3 16.4 %multiply_convert_fusion.1 = (bf16[1024,1408]{1,0:T(8,128)(2,1)}, bf16[1024,1408]{1,0:T(8,128)(2,1)}, bf16[1024,1408]{1,0:T(8,128)(2,1)}) fusion(f32[1024,1408]{1,0:T(8,128)} %fusion.46, f32[1024,1408]{1,0:T(8,128)} %fusion.83, bf16[2048,1408]{1,0:T(8,128)(2,1)S(1)} %bitcast.300, bf16[256,2048]{1,0:T(8,128)(2,1)S(1)} %collective-permute-done.21, ...), kind=kOutput, calls=%fused_computation.12 | convolution fusion | flops 5945425920 | bytes 30146560 | tf_op jit(solution)/shard_map/dot_general | solution.py:348
  568.7 12.4 %fusion.91 = (bf16[1024,2048]{1,0:T(8,128)(2,1)}, f32[1024,2048]{1,0:T(8,128)}) fusion(bf16[1024,1408]{1,0:T(8,128)(2,1)} %get-tuple-element.58, bf16[1408,2048]{1,0:T(8,128)(2,1)} %bitcast.309), kind=kOutput, calls=%fused_computation.224 | convolution fusion | flops 5907677184 | bytes 21233664 | tf_op jit(solution)/shard_map/dot_general | solution.py:348
  592.4 11.4 fusion.92
  617.3 12.7 %fusion.90 = (bf16[1024,2048]{1,0:T(8,128)(2,1)}, f32[1024,2048]{1,0:T(8,128)}) fusion(f32[1024,2048]{1,0:T(8,128)} %fusion.92, bf16[1024,1408]{1,0:T(8,128)(2,1)} %get-tuple-element.57, bf16[2048,1408]{1,0:T(8,128)(2,1)S(1)} %bitcast.301), kind=kOutput, calls=%fused_computation.223 | convolution fusion | flops 5909774336 | bytes 29622272 | tf_op jit(solution)/shard_map/dot_general | solution.py:34
  656.8 61.6 %collective-permute-done.73 = bf16[4,256,1408]{2,1,0:T(8,128)(2,1)} collective-permute-done((bf16[4,256,1408]{2,1,0:T(8,128)(2,1)}, bf16[4,256,1408]{2,1,0:T(8,128)(2,1)}, u32[]{:S(2)}, u32[]{:S(2)}) %collective-permute-start.73) | collective-permute-done | bytes 2883616 | tf_op jit(solution)/shard_map/ppermute | solution.py:340
  731.0 48.3 %collective-permute-done.67 = bf16[4,256,1408]{2,1,0:T(8,128)(2,1)} collective-permute-done((bf16[4,256,1408]{2,1,0:T(8,128)(2,1)S(1)}, bf16[4,256,1408]{2,1,0:T(8,128)(2,1)}, u32[]{:S(2)}, u32[]{:S(2)}) %collective-permute-start.67) | collective-permute-done | bytes 2883616 | tf_op jit(solution)/shard_map/ppermute | solution.py:340
  794.1 27.0 %collective-permute-done.76 = bf16[256,1408]{1,0:T(8,128)(2,1)} collective-permute-done((bf16[256,1408]{1,0:T(8,128)(2,1)S(1)}, bf16[256,1408]{1,0:T(8,128)(2,1)}, u32[]{:S(2)}, u32[]{:S(2)}) %collective-permute-start.76) | collective-permute-done | bytes 720928 | tf_op jit(solution)/shard_map/ppermute | solution.py:344
  823.3 14.2 %collective-permute-done.68 = bf16[256,1408]{1,0:T(8,128)(2,1)} collective-permute-done((bf16[256,1408]{1,0:T(8,128)(2,1)}, bf16[256,1408]{1,0:T(8,128)(2,1)}, u32[]{:S(2)}, u32[]{:S(2)}) %collective-permute-start.68) | collective-permute-done | bytes 720928 | tf_op jit(solution)/shard_map/ppermute | solution.py:344
  837.4 30.9 %collective-permute-done.69 = bf16[256,1408]{1,0:T(8,128)(2,1)} collective-permute-done((bf16[256,1408]{1,0:T(8,128)(2,1)}, bf16[256,1408]{1,0:T(8,128)(2,1)}, u32[]{:S(2)}, u32[]{:S(2)}) %collective-permute-start.69) | collective-permute-done | bytes 720928 | tf_op jit(solution)/shard_map/ppermute | solution.py:344
  868.9 14.0 %collective-permute-done.70 = bf16[256,1408]{1,0:T(8,128)(2,1)} collective-permute-done((bf16[256,1408]{1,0:T(8,128)(2,1)}, bf16[256,1408]{1,0:T(8,128)(2,1)}, u32[]{:S(2)}, u32[]{:S(2)}) %collective-permute-start.70) | collective-permute-done | bytes 720928 | tf_op jit(solution)/shard_map/ppermute | solution.py:344
  885.9 13.3 %collective-permute-done.80 = bf16[176,2048]{1,0:T(8,128)(2,1)S(1)} collective-permute-done((bf16[176,2048]{1,0:T(8,128)(2,1)}, bf16[176,2048]{1,0:T(8,128)(2,1)S(1)}, u32[]{:S(2)}, u32[]{:S(2)}) %collective-permute-start.80) | collective-permute-done | bytes 720928 | tf_op jit(solution)/shard_map/ppermute | solution.py:344
  899.2 12.8 %collective-permute-done.81 = bf16[176,2048]{1,0:T(8,128)(2,1)S(1)} collective-permute-done((bf16[176,2048]{1,0:T(8,128)(2,1)}, bf16[176,2048]{1,0:T(8,128)(2,1)S(1)}, u32[]{:S(2)}, u32[]{:S(2)}) %collective-permute-start.81) | collective-permute-done | bytes 720928 | tf_op jit(solution)/shard_map/ppermute | solution.py:344
  976.8 49.5 %collective-permute-done.72 = bf16[2,64,1408]{2,1,0:T(8,128)(2,1)S(1)} collective-permute-done((bf16[2,64,1408]{2,1,0:T(8,128)(2,1)}, bf16[2,64,1408]{2,1,0:T(8,128)(2,1)S(1)}, u32[]{:S(2)}, u32[]{:S(2)}) %collective-permute-start.72) | collective-permute-done | bytes 360480 | tf_op jit(solution)/shard_map/ppermute | solution.py:340
  1047.9 23.1 %all-to-all-done.5 = f32[32,1,128]{2,1,0:T(1,128)S(1)} async-done(((f32[32,1,128]{2,1,0:T(1,128)}), f32[32,1,128]{2,1,0:T(1,128)S(1)}, u32[]{:S(2)}, u32[]{:S(2)}) %all-to-all-start.5) | async-done | bytes 16416 | tf_op jit(solution)/shard_map/all_to_all | solution.py:673
  1107.8 11.2 collective-permute-done.57
  1131.3 18.6 %collective-permute-done.63 = bf16[4,64,2048]{2,1,0:T(8,128)(2,1)} collective-permute-done((bf16[4,64,2048]{2,1,0:T(8,128)(2,1)}, bf16[4,64,2048]{2,1,0:T(8,128)(2,1)}, u32[]{:S(2)}, u32[]{:S(2)}) %collective-permute-start.63) | collective-permute-done | bytes 1048608 | tf_op jit(solution)/shard_map/ppermute | solution.py:340
  1156.1 14.7 %collective-permute-done.58 = bf16[128,1280]{1,0:T(8,128)(2,1)S(1)} collective-permute-done((bf16[128,1280]{1,0:T(8,128)(2,1)S(1)}, bf16[128,1280]{1,0:T(8,128)(2,1)S(1)}, u32[]{:S(2)}, u32[]{:S(2)}) %collective-permute-start.58) | collective-permute-done | bytes 327712 | tf_op jit(solution)/shard_map/ppermute | solution.py:344
  1170.8 18.3 %collective-permute-done.59 = bf16[128,1280]{1,0:T(8,128)(2,1)S(1)} collective-permute-done((bf16[128,1280]{1,0:T(8,128)(2,1)S(1)}, bf16[128,1280]{1,0:T(8,128)(2,1)S(1)}, u32[]{:S(2)}, u32[]{:S(2)}) %collective-permute-start.59) | collective-permute-done | bytes 327712 | tf_op jit(solution)/shard_map/ppermute | solution.py:344
  (530 shorter events, 501.2 us)
Async XLA Ops:
  4.6 82.6 %collective-permute-start.12 = (bf16[64,2048]{1,0:T(8,128)(2,1)}, bf16[64,2048]{1,0:T(8,128)(2,1)}, u32[]{:S(2)}, u32[]{:S(2)}) collective-permute-start(bf16[64,2048]{1,0:T(8,128)(2,1)} %refs_0_.2), channel_id=1, source_target_pairs={{24,0},{0,8},{8,16},{16,24},{25,1},{1,9},{9,17},{17,25},{26,2},{2,... | collective-permute-start | bytes 786440 | tf_op jit(solution)/shard_map/ppermute | solution.py:344
  29.3 156.3 %all-to-all-start = ((bf16[2,4,32,2048]{3,1,0,2:T(4,128)(2,1)}), bf16[2,4,32,2048]{3,1,0,2:T(4,128)(2,1)S(1)}, u32[]{:S(2)}, u32[]{:S(2)}) async-start(bf16[2,4,32,2048]{3,1,0,2:T(4,128)(2,1)} %copy.158), calls=%async_computation | async-start | bytes 2097152 | tf_op jit(solution)/shard_map/all_to_all | solution.py:561
  113.2 123.9 %collective-permute-start.9 = (bf16[8,2,64,1280]{3,2,1,0:T(8,128)(2,1)}, bf16[8,2,64,1280]{3,2,1,0:T(8,128)(2,1)}, u32[]{:S(2)}, u32[]{:S(2)}) collective-permute-start(bf16[8,2,64,1280]{3,2,1,0:T(8,128)(2,1)} %place_blocks.5), channel_id=1, source_target_pairs={{0,1},{1,0},{2,3},{3,2},{4,5},{5,4},{6,7},{7,6},{8,9},{9,8},{10,11... | collective-permute-start | bytes 7864328 | tf_op jit(solution)/shard_map/ppermute | solution.py:340
  114.8 66.3 %collective-permute-start.31 = (bf16[64,2816]{1,0:T(8,128)(2,1)S(1)}, bf16[64,2816]{1,0:T(8,128)(2,1)}, u32[]{:S(2)}, u32[]{:S(2)}) collective-permute-start(bf16[64,2816]{1,0:T(8,128)(2,1)S(1)} %copy-done.54), channel_id=1, source_target_pairs={{0,1},{1,0},{2,3},{3,2},{4,5},{5,4},{6,7},{7,6},{8,9},{9,8},{10,11... | collective-permute-start | bytes 1081352 | tf_op jit(solution)/shard_map/ppermute | solution.py:340
  119.2 151.8 %collective-permute-start.40 = (bf16[176,2048]{1,0:T(8,128)(2,1)}, bf16[176,2048]{1,0:T(8,128)(2,1)}, u32[]{:S(2)}, u32[]{:S(2)}) collective-permute-start(bf16[176,2048]{1,0:T(8,128)(2,1)} %refs_0_.3), channel_id=1, source_target_pairs={{8,0},{16,8},{24,16},{0,24},{9,1},{17,9},{25,17},{1,25},{10,2},{18... | collective-permute-start | bytes 2162696 | tf_op jit(solution)/shard_map/ppermute | solution.py:344
  125.9 106.0 %collective-permute-start.17 = (bf16[8,64,2048]{2,1,0:T(8,128)(2,1)}, bf16[8,64,2048]{2,1,0:T(8,128)(2,1)}, u32[]{:S(2)}, u32[]{:S(2)}) collective-permute-start(bf16[8,64,2048]{2,1,0:T(8,128)(2,1)} %place_blocks.6), channel_id=1, source_target_pairs={{0,1},{1,0},{2,3},{3,2},{4,5},{5,4},{6,7},{7,6},{8,9},{9,8},{10,11... | collective-permute-start | bytes 6291464 | tf_op jit(solution)/shard_map/ppermute | solution.py:340
  128.2 144.9 %collective-permute-start.41 = (bf16[176,2048]{1,0:T(8,128)(2,1)}, bf16[176,2048]{1,0:T(8,128)(2,1)}, u32[]{:S(2)}, u32[]{:S(2)}) collective-permute-start(bf16[176,2048]{1,0:T(8,128)(2,1)} %refs_0_.3), channel_id=1, source_target_pairs={{16,0},{24,8},{0,16},{8,24},{17,1},{25,9},{1,17},{9,25},{18,2},{26... | collective-permute-start | bytes 2162696 | tf_op jit(solution)/shard_map/ppermute | solution.py:344
  181.1 93.5 %collective-permute-start.42 = (bf16[176,2048]{1,0:T(8,128)(2,1)}, bf16[176,2048]{1,0:T(8,128)(2,1)}, u32[]{:S(2)}, u32[]{:S(2)}) collective-permute-start(bf16[176,2048]{1,0:T(8,128)(2,1)} %refs_0_.3), channel_id=1, source_target_pairs={{24,0},{0,8},{8,16},{16,24},{25,1},{1,9},{9,17},{17,25},{26,2},{2,... | collective-permute-start | bytes 2162696 | tf_op jit(solution)/shard_map/ppermute | solution.py:344
  185.6 177.6 %all-to-all-start.3 = ((bf16[2,4,32,2048]{3,1,0,2:T(4,128)(2,1)}), bf16[2,4,32,2048]{3,1,0,2:T(4,128)(2,1)}, u32[]{:S(2)}, u32[]{:S(2)}) async-start(bf16[2,4,32,2048]{3,1,0,2:T(4,128)(2,1)} %copy.186), calls=%async_computation.3 | async-start | bytes 2097152 | tf_op jit(solution)/shard_map/all_to_all | solution.py:561
  267.8 134.2 %collective-permute-start.18 = (f32[256,2048]{1,0:T(8,128)}, f32[256,2048]{1,0:T(8,128)}, u32[]{:S(2)}, u32[]{:S(2)}) collective-permute-start(f32[256,2048]{1,0:T(8,128)} %slice.115), channel_id=1, source_target_pairs={{0,2},{2,0},{1,3},{3,1},{4,6},{6,4},{5,7},{7,5},{8,10},{10,8},{9,1... | collective-permute-start | bytes 6291464 | tf_op jit(solution)/shard_map/ppermute | solution.py:340
  273.1 86.4 %collective-permute-start.25 = (bf16[256,1408]{1,0:T(8,128)(2,1)}, bf16[256,1408]{1,0:T(8,128)(2,1)}, u32[]{:S(2)}, u32[]{:S(2)}) collective-permute-start(bf16[256,1408]{1,0:T(8,128)(2,1)} %bitcast.23.refs_0_), channel_id=1, source_target_pairs={{16,0},{24,8},{0,16},{8,24},{17,1},{25,9},{1,17},{9,25},{18,2},{26... | collective-permute-start | bytes 2162696 | tf_op jit(solution)/shard_map/ppermute | solution.py:344
  274.6 88.3 %collective-permute-start.26 = (bf16[256,1408]{1,0:T(8,128)(2,1)}, bf16[256,1408]{1,0:T(8,128)(2,1)}, u32[]{:S(2)}, u32[]{:S(2)}) collective-permute-start(bf16[256,1408]{1,0:T(8,128)(2,1)} %bitcast.23.refs_0_), channel_id=1, source_target_pairs={{24,0},{0,8},{8,16},{16,24},{25,1},{1,9},{9,17},{17,25},{26,2},{2,... | collective-permute-start | bytes 2162696 | tf_op jit(solution)/shard_map/ppermute | solution.py:344
  289.0 78.3 %collective-permute-start.27 = (bf16[256,1408]{1,0:T(8,128)(2,1)}, bf16[256,1408]{1,0:T(8,128)(2,1)}, u32[]{:S(2)}, u32[]{:S(2)}) collective-permute-start(bf16[256,1408]{1,0:T(8,128)(2,1)} %bitcast.23.refs_0_), channel_id=1, source_target_pairs={{0,4},{4,0},{1,5},{5,1},{2,6},{6,2},{3,7},{7,3},{8,12},{12,8},{9,1... | collective-permute-start | bytes 2162696 | tf_op jit(solution)/shard_map/ppermute | solution.py:340
  447.2 80.6 %collective-permute-start.20 = (bf16[256,2048]{1,0:T(8,128)(2,1)S(1)}, bf16[256,2048]{1,0:T(8,128)(2,1)}, u32[]{:S(2)}, u32[]{:S(2)}) collective-permute-start(bf16[256,2048]{1,0:T(8,128)(2,1)S(1)} %multiply_convert_fusion.4), channel_id=1, source_target_pairs={{0,1},{1,0},{2,3},{3,2},{4,5},{5,4},{6,7},{7,6},{8,9},{9,8},{10,11... | collective-permute-start | bytes 3145736 | tf_op jit(solution)/shard_map/ppermute | solution.py:340
  462.7 65.6 %collective-permute-start.49 = (bf16[256,2048]{1,0:T(8,128)(2,1)}, bf16[256,2048]{1,0:T(8,128)(2,1)}, u32[]{:S(2)}, u32[]{:S(2)}) collective-permute-start(bf16[256,2048]{1,0:T(8,128)(2,1)} %broadcast_select_fusion), channel_id=1, source_target_pairs={{0,2},{2,0},{1,3},{3,1},{4,6},{6,4},{5,7},{7,5},{8,10},{10,8},{9,1... | collective-permute-start | bytes 3145736 | tf_op jit(solution)/shard_map/ppermute | solution.py:340
  462.7 65.6 %collective-permute-start.51 = (bf16[256,2048]{1,0:T(8,128)(2,1)}, bf16[256,2048]{1,0:T(8,128)(2,1)}, u32[]{:S(2)}, u32[]{:S(2)}) collective-permute-start(bf16[256,2048]{1,0:T(8,128)(2,1)} %collective-permute-done.50), channel_id=1, source_target_pairs={{0,2},{2,0},{1,3},{3,1},{4,6},{6,4},{5,7},{7,5},{8,10},{10,8},{9,1... | collective-permute-start | bytes 3145736 | tf_op jit(solution)/shard_map/ppermute | solution.py:340
  590.9 131.8 %collective-permute-start.79 = (bf16[4,176,2048]{2,1,0:T(8,128)(2,1)}, bf16[4,176,2048]{2,1,0:T(8,128)(2,1)S(1)}, u32[]{:S(2)}, u32[]{:S(2)}) collective-permute-start(bf16[4,176,2048]{2,1,0:T(8,128)(2,1)} %dynamic-slice_bitcast_fusion), channel_id=1, source_target_pairs={{0,4},{4,0},{1,5},{5,1},{2,6},{6,2},{3,7},{7,3},{8,12},{12,8},{9,1... | collective-permute-start | bytes 8650760 | tf_op jit(solution)/shard_map/ppermute | solution.py:340
  616.2 102.1 %collective-permute-start.73 = (bf16[4,256,1408]{2,1,0:T(8,128)(2,1)}, bf16[4,256,1408]{2,1,0:T(8,128)(2,1)}, u32[]{:S(2)}, u32[]{:S(2)}) collective-permute-start(bf16[4,256,1408]{2,1,0:T(8,128)(2,1)} %dynamic-slice_bitcast_fusion.1), channel_id=1, source_target_pairs={{0,4},{4,0},{1,5},{5,1},{2,6},{6,2},{3,7},{7,3},{8,12},{12,8},{9,1... | collective-permute-start | bytes 8650760 | tf_op jit(solution)/shard_map/ppermute | solution.py:340
  645.8 133.5 %collective-permute-start.67 = (bf16[4,256,1408]{2,1,0:T(8,128)(2,1)S(1)}, bf16[4,256,1408]{2,1,0:T(8,128)(2,1)}, u32[]{:S(2)}, u32[]{:S(2)}) collective-permute-start(bf16[4,256,1408]{2,1,0:T(8,128)(2,1)S(1)} %dynamic-slice_bitcast_fusion.2), channel_id=1, source_target_pairs={{0,4},{4,0},{1,5},{5,1},{2,6},{6,2},{3,7},{7,3},{8,12},{12,8},{9,1... | collective-permute-start | bytes 8650760 | tf_op jit(solution)/shard_map/ppermute | solution.py:340
  650.4 135.3 %collective-permute-start.53 = (bf16[256,2048]{1,0:T(8,128)(2,1)}, bf16[256,2048]{1,0:T(8,128)(2,1)}, u32[]{:S(2)}, u32[]{:S(2)}) collective-permute-start(bf16[256,2048]{1,0:T(8,128)(2,1)} %fusion.8), channel_id=1, source_target_pairs={{0,1},{1,0},{2,3},{3,2},{4,5},{5,4},{6,7},{7,6},{8,9},{9,8},{10,11... | collective-permute-start | bytes 3145736 | tf_op jit(solution)/shard_map/ppermute | solution.py:340
  728.0 64.5 %collective-permute-start.75 = (bf16[256,1408]{1,0:T(8,128)(2,1)}, bf16[256,1408]{1,0:T(8,128)(2,1)}, u32[]{:S(2)}, u32[]{:S(2)}) collective-permute-start(bf16[256,1408]{1,0:T(8,128)(2,1)} %get-tuple-element.69), channel_id=1, source_target_pairs={{16,0},{24,8},{0,16},{8,24},{17,1},{25,9},{1,17},{9,25},{18,2},{26... | collective-permute-start | bytes 2162696 | tf_op jit(solution)/shard_map/ppermute | solution.py:344
  729.0 92.2 %collective-permute-start.76 = (bf16[256,1408]{1,0:T(8,128)(2,1)S(1)}, bf16[256,1408]{1,0:T(8,128)(2,1)}, u32[]{:S(2)}, u32[]{:S(2)}) collective-permute-start(bf16[256,1408]{1,0:T(8,128)(2,1)S(1)} %get-tuple-element.68), channel_id=1, source_target_pairs={{24,0},{0,8},{8,16},{16,24},{25,1},{1,9},{9,17},{17,25},{26,2},{2,... | collective-permute-start | bytes 2162696 | tf_op jit(solution)/shard_map/ppermute | solution.py:344
  785.8 82.6 %collective-permute-start.69 = (bf16[256,1408]{1,0:T(8,128)(2,1)}, bf16[256,1408]{1,0:T(8,128)(2,1)}, u32[]{:S(2)}, u32[]{:S(2)}) collective-permute-start(bf16[256,1408]{1,0:T(8,128)(2,1)} %get-tuple-element.72), channel_id=1, source_target_pairs={{16,0},{24,8},{0,16},{8,24},{17,1},{25,9},{1,17},{9,25},{18,2},{26... | collective-permute-start | bytes 2162696 | tf_op jit(solution)/shard_map/ppermute | solution.py:344
  789.7 93.2 %collective-permute-start.70 = (bf16[256,1408]{1,0:T(8,128)(2,1)}, bf16[256,1408]{1,0:T(8,128)(2,1)}, u32[]{:S(2)}, u32[]{:S(2)}) collective-permute-start(bf16[256,1408]{1,0:T(8,128)(2,1)} %get-tuple-element.71), channel_id=1, source_target_pairs={{24,0},{0,8},{8,16},{16,24},{25,1},{1,9},{9,17},{17,25},{26,2},{2,... | collective-permute-start | bytes 2162696 | tf_op jit(solution)/shard_map/ppermute | solution.py:344
  792.6 243.1 %collective-permute-start.48 = (bf16[256,2048]{1,0:T(8,128)(2,1)}, bf16[256,2048]{1,0:T(8,128)(2,1)}, u32[]{:S(2)}, u32[]{:S(2)}) collective-permute-start(bf16[256,2048]{1,0:T(8,128)(2,1)} %fusion.10), channel_id=1, source_target_pairs={{0,1},{1,0},{2,3},{3,2},{4,5},{5,4},{6,7},{7,6},{8,9},{9,8},{10,11... | collective-permute-start | bytes 3145736 | tf_op jit(solution)/shard_map/ppermute | solution.py:340
  821.1 78.1 %collective-permute-start.80 = (bf16[176,2048]{1,0:T(8,128)(2,1)}, bf16[176,2048]{1,0:T(8,128)(2,1)S(1)}, u32[]{:S(2)}, u32[]{:S(2)}) collective-permute-start(bf16[176,2048]{1,0:T(8,128)(2,1)} %get-tuple-element.64), channel_id=1, source_target_pairs={{8,0},{16,8},{24,16},{0,24},{9,1},{17,9},{25,17},{1,25},{10,2},{18... | collective-permute-start | bytes 2162696 | tf_op jit(solution)/shard_map/ppermute | solution.py:344
  837.4 74.6 %collective-permute-start.81 = (bf16[176,2048]{1,0:T(8,128)(2,1)}, bf16[176,2048]{1,0:T(8,128)(2,1)S(1)}, u32[]{:S(2)}, u32[]{:S(2)}) collective-permute-start(bf16[176,2048]{1,0:T(8,128)(2,1)} %get-tuple-element.66), channel_id=1, source_target_pairs={{16,0},{24,8},{0,16},{8,24},{17,1},{25,9},{1,17},{9,25},{18,2},{26... | collective-permute-start | bytes 2162696 | tf_op jit(solution)/shard_map/ppermute | solution.py:344
  948.6 79.1 %collective-permute-start.55 = (f32[256,2048]{1,0:T(8,128)}, f32[256,2048]{1,0:T(8,128)}, u32[]{:S(2)}, u32[]{:S(2)}) collective-permute-start(f32[256,2048]{1,0:T(8,128)} %slice.130), channel_id=1, source_target_pairs={{0,2},{2,0},{1,3},{3,1},{4,6},{6,4},{5,7},{7,5},{8,10},{10,8},{9,1... | collective-permute-start | bytes 6291464 | tf_op jit(solution)/shard_map/ppermute | solution.py:340
  958.5 86.1 %collective-permute-start.56 = (bf16[8,2,64,1280]{3,2,1,0:T(8,128)(2,1)}, bf16[8,2,64,1280]{3,2,1,0:T(8,128)(2,1)}, u32[]{:S(2)}, u32[]{:S(2)}) collective-permute-start(bf16[8,2,64,1280]{3,2,1,0:T(8,128)(2,1)} %dynamic-slice_bitcast_fusion.3), channel_id=1, source_target_pairs={{0,1},{1,0},{2,3},{3,2},{4,5},{5,4},{6,7},{7,6},{8,9},{9,8},{10,11... | collective-permute-start | bytes 7864328 | tf_op jit(solution)/shard_map/ppermute | solution.py:340
  973.5 106.3 %collective-permute-start.62 = (bf16[8,64,2048]{2,1,0:T(8,128)(2,1)}, bf16[8,64,2048]{2,1,0:T(8,128)(2,1)}, u32[]{:S(2)}, u32[]{:S(2)}) collective-permute-start(bf16[8,64,2048]{2,1,0:T(8,128)(2,1)} %dynamic-slice_bitcast_fusion.4), channel_id=1, source_target_pairs={{0,1},{1,0},{2,3},{3,2},{4,5},{5,4},{6,7},{7,6},{8,9},{9,8},{10,11... | collective-permute-start | bytes 6291464 | tf_op jit(solution)/shard_map/ppermute | solution.py:340
  1083.3 66.6 %collective-permute-start.63 = (bf16[4,64,2048]{2,1,0:T(8,128)(2,1)}, bf16[4,64,2048]{2,1,0:T(8,128)(2,1)}, u32[]{:S(2)}, u32[]{:S(2)}) collective-permute-start(bf16[4,64,2048]{2,1,0:T(8,128)(2,1)} %dynamic-slice_bitcast_fusion.6), channel_id=1, source_target_pairs={{0,4},{4,0},{1,5},{5,1},{2,6},{6,2},{3,7},{7,3},{8,12},{12,8},{9,1... | collective-permute-start | bytes 3145736 | tf_op jit(solution)/shard_map/ppermute | solution.py:340
  1121.7 82.7 %all-to-all-start.4 = ((bf16[2,128,1,2048]{3,0,2,1:T(2,128)(2,1)}), bf16[2,128,1,2048]{3,0,2,1:T(2,128)(2,1)S(1)}, u32[]{:S(2)}, u32[]{:S(2)}) async-start(bf16[2,128,1,2048]{3,0,2,1:T(2,128)(2,1)} %copy.201), calls=%async_computation.4 | async-start | bytes 2097152 | tf_op jit(solution)/shard_map/all_to_all | solution.py:565
  (151 other events, 4317.7 us)

commit v2 on v1

--- a/solution.py
+++ b/solution.py
@@ -334,6 +334,7 @@
 
 GRID = ("z", "y", "core", "pair")
 SWAP = ((0, 1), (1, 0))
+LANES = 128
 
 
 def swap(value, axis):
@@ -344,24 +345,34 @@
     return lax.ppermute(value, "z", [((i + hops) % size, i) for i in range(size)])
 
 
+def after(value, *earlier):
+    return lax.optimization_barrier((value, *earlier))[0]
+
+
+def short(value):
+    return value.astype(jnp.bfloat16)
+
+
+def long(value):
+    return value.astype(jnp.float32)
+
+
 def matmul(left, right):
     return jnp.dot(left, right, preferred_element_type=jnp.float32)
 
 
 def place_kernel(depth, *refs):
-    blocks, whole, held, sems = refs[: 2 * depth], *refs[2 * depth :]
-    z, y = lax.axis_index("z"), lax.axis_index("y")
+    blocks, whole, held, sems = refs[:depth], *refs[depth:]
+    z = lax.axis_index("z")
     fetched, placed = [], []
-    for side in range(2):
-        for hops in range(depth):
-            at = lax.rem(z + hops, depth) * 2 + (y if side == 0 else 1 - y)
-            slot = side * depth + hops
-            fetched.append(
-                pltpu.make_async_copy(blocks[slot], held.at[slot], sems.at[0, slot])
-            )
-            placed.append(
-                pltpu.make_async_copy(held.at[slot], whole.at[at], sems.at[1, slot])
-            )
+    for hops in range(depth):
+        at = lax.rem(z + hops, depth)
+        fetched.append(
+            pltpu.make_async_copy(blocks[hops], held.at[hops], sems.at[0, hops])
+        )
+        placed.append(
+            pltpu.make_async_copy(held.at[hops], whole.at[at], sems.at[1, hops])
+        )
     for copy in fetched:
         copy.start()
     for arrived, copy in zip(fetched, placed):
@@ -372,36 +383,43 @@
 
 
 def place_blocks(blocks):
-    depth = len(blocks) // 2
+    depth = len(blocks)
     shape, dtype = blocks[0].shape, blocks[0].dtype
-    moved = 4 * depth * math.prod(shape) * dtype.itemsize
+    moved = 2 * depth * math.prod(shape) * dtype.itemsize
     return pl.pallas_call(
         functools.partial(place_kernel, depth),
-        out_shape=jax.ShapeDtypeStruct((2 * depth,) + shape, dtype),
-        in_specs=[pl.BlockSpec(memory_space=pl.ANY)] * (2 * depth),
+        out_shape=jax.ShapeDtypeStruct((depth,) + shape, dtype),
+        in_specs=[pl.BlockSpec(memory_space=pl.ANY)] * depth,
         out_specs=pl.BlockSpec(memory_space=pl.ANY),
         scratch_shapes=[
-            pltpu.VMEM((2 * depth,) + shape, dtype),
-            pltpu.SemaphoreType.DMA((2, 2 * depth)),
+            pltpu.VMEM((depth,) + shape, dtype),
+            pltpu.SemaphoreType.DMA((2, depth)),
         ],
         cost_estimate=pl.CostEstimate(flops=0, bytes_accessed=moved, transcendentals=0),
         name="place_blocks",
     )(*blocks)
 
 
-def gather_zy(block, depth):
-    column = [block] + [from_above(block, hops, depth) for hops in range(1, depth)]
-    return place_blocks(column + [swap(part, "y") for part in column])
+def column_of(block, depth):
+    return [block] + [from_above(block, hops, depth) for hops in range(1, depth)]
+
+
+def gather_z(block):
+    return lax.all_gather(block, "z", axis=0, tiled=True)
+
+
+def scatter_z(partial):
+    return lax.psum_scatter(partial, "z", scatter_dimension=0, tiled=True)
 
 
 def reduce_z(partial, depth):
     z = lax.axis_index("z")
-    total = lax.dynamic_index_in_dim(partial, z, 0, False).astype(jnp.float32)
+    total = long(lax.dynamic_index_in_dim(partial, z, 0, False))
     for hops in range(1, depth):
         sent = lax.dynamic_index_in_dim(
             partial, lax.rem(z + depth - hops, depth), 0, False
         )
-        total = total + from_above(sent, hops, depth).astype(jnp.float32)
+        total = total + long(from_above(sent, hops, depth))
     return total
 
 
@@ -412,11 +430,17 @@
     )
 
 
-def exchange_sum(value, index, axis, name):
+def both(mine, other, index, axis):
+    return jnp.where(
+        index == 0, jnp.stack([mine, other], axis), jnp.stack([other, mine], axis)
+    )
+
+
+def trade(value, name, axis, into):
+    index = lax.axis_index(name)
     kept, sent = halves(value, index, axis)
-    return (kept.astype(jnp.float32) + swap(sent, name).astype(jnp.float32)).astype(
-        jnp.bfloat16
-    )
+    flat = sent.reshape(-1, sent.shape[-1]) if sent.ndim > 2 else sent
+    return both(kept, swap(flat, name).reshape(kept.shape), index, into)
 
 
 def row_norm(value):
@@ -445,37 +469,59 @@
 
 def attend(query, keys, values, lens):
     _, _, probs, _ = scores_of(query, keys, lens)
-    return jnp.einsum(
-        "bhij,bjhe->bihe", probs.astype(jnp.bfloat16), values, preferred_element_type=jnp.float32
-    ).astype(jnp.bfloat16)
+    return short(
+        jnp.einsum("bhij,bjhe->bihe", short(probs), values, preferred_element_type=jnp.float32)
+    )
 
 
 def attend_back(query, keys, values, lens, grads):
     scores, mask, probs, denom = scores_of(query, keys, lens)
     d_probs = jnp.einsum("bihe,bjhe->bhij", grads, values, preferred_element_type=jnp.float32)
     d_values = jnp.einsum(
-        "bhij,bihe->bjhe", probs.astype(jnp.bfloat16), grads, preferred_element_type=jnp.float32
+        "bhij,bihe->bjhe", short(probs), grads, preferred_element_type=jnp.float32
     )
     d_kernel = (d_probs - jnp.sum(d_probs * probs, -1, keepdims=True)) / denom
     d_scores = jnp.where(mask, d_kernel * (1.0 + scores), 0.0) * query.shape[-1] ** (-0.5)
-    d_scores = d_scores.astype(jnp.bfloat16)
+    d_scores = short(d_scores)
     d_query = jnp.einsum("bhij,bjhe->bihe", d_scores, keys, preferred_element_type=jnp.float32)
     d_keys = jnp.einsum("bhij,bihe->bjhe", d_scores, query, preferred_element_type=jnp.float32)
-    return tuple(part.astype(jnp.bfloat16) for part in (d_query, d_keys, d_values))
+    return short(d_query), short(d_keys), short(d_values)
 
 
 def share_four(mine):
-    near = swap(mine, "core")
-    across = swap(mine, "pair")
-    return jnp.concatenate([mine, near, across, swap(across, "core")], 0)
+    up = swap(mine, "y")
+    return jnp.concatenate([mine, up, swap(mine, "core"), swap(up, "core")], 0)
 
 
 def sum_four(partial):
     count = partial.shape[0] // 4
-    mine, near, across, far = (partial[i * count : (i + 1) * count] for i in range(4))
-    got = swap(jnp.concatenate([near, far], 0).astype(jnp.bfloat16), "core").astype(jnp.float32)
-    across = (across + got[count:]).astype(jnp.bfloat16)
-    return mine + got[:count] + swap(across, "pair").astype(jnp.float32)
+    got = swap(partial[2 * count :], "core")
+    up = short(long(partial[count : 2 * count]) + long(got[count:]))
+    return long(partial[:count]) + long(got[:count]) + long(swap(up, "y"))
+
+
+def share_eight(mine):
+    half = mine.shape[0] // 2
+    up, across = swap(mine, "y"), swap(mine, "pair")
+    far_a = swap(across[:half], "y")
+    far_b = swap(up[half:], "pair")
+    own = [mine, up, across, far_a, far_b]
+    near = [swap(mine, "core"), swap(up, "core"), swap(across, "core")]
+    near += [swap(far_a, "core"), swap(far_b, "core")]
+    return jnp.concatenate(own + near, 0)
+
+
+def sum_eight(partial):
+    count = partial.shape[0] // 8
+    half = count // 2
+    got = swap(partial[4 * count :], "core")
+    own = long(partial[: 4 * count]) + long(got)
+    far = short(own[3 * count :])
+    mine, up, across = (own[i * count : (i + 1) * count] for i in range(3))
+    near_a, near_b = swap(far[:half], "y"), swap(far[half:], "pair")
+    across = jnp.concatenate([across[:half] + long(near_a), across[half:]], 0)
+    up = jnp.concatenate([up[:half], up[half:] + long(near_b)], 0)
+    return mine + long(swap(short(up), "y")) + long(swap(short(across), "pair"))
 
 
 def on_grid(
@@ -495,178 +541,164 @@
     w_down,
 ):
     batches, _, seqs, width = tokens.shape
-    core, pair = lax.axis_index("core"), lax.axis_index("pair")
-    y = lax.axis_index("y")
+    y, core, pair = (lax.axis_index(name) for name in ("y", "core", "pair"))
     device_index = lax.axis_index(GRID)
-    planes = 2 * depth
-    rows_in = w_query.shape[0]
+    rows_in, hidden = w_gate.shape
     ff_rows = w_down.shape[0]
-    hidden = w_gate.shape[1]
-    qk_width = w_query.shape[1]
-    own_heads = HEADS // 2
-    features = qk_width // HEADS
+    own_ff = depth * ff_rows
+    wide = -(-own_ff // LANES) * LANES
+    own_heads = depth
+    features = w_query.shape[1] // HEADS
     head_dim = width // HEADS
-
-    def core_columns(weight, step):
-        return weight.reshape(rows_in, planes, 2, step)
-
-    def half_heads(index):
-        return jnp.concatenate(
-            [
-                lax.dynamic_index_in_dim(core_columns(weight, step), index, 2, False).reshape(rows_in, -1)
-                for weight, step in ((w_query, features), (w_key, features), (w_value, head_dim))
-            ],
-            1,
-        )
-
-    qkv_mine = half_heads(core)
-    qkv_got = swap(half_heads(1 - core), "core")
-    qkv_block = jnp.where(
-        core == 0, jnp.stack([qkv_mine, qkv_got]), jnp.stack([qkv_got, qkv_mine])
-    ).reshape(2, rows_in, -1)
-    w_qkv = gather_zy(qkv_block, depth)
-    w_qkv_other = swap(w_qkv, "pair")
-    w_qkv = jnp.where(
-        pair == 0, jnp.stack([w_qkv, w_qkv_other], 2), jnp.stack([w_qkv_other, w_qkv], 2)
-    ).reshape(width, -1)
-    w_out_mine = gather_zy(w_out, depth)
-    w_out_other = swap(w_out_mine, "pair")
-    w_out_all = jnp.where(
-        pair == 0, jnp.stack([w_out_mine, w_out_other], 1), jnp.stack([w_out_other, w_out_mine], 1)
-    ).reshape(own_heads * head_dim, width)
-
-    def hidden_block(weight):
-        cut = weight.reshape(rows_in, planes, 2, 2, ff_rows)
-        kept, sent = halves(cut, pair, 3)
-        got = swap(sent.reshape(rows_in, -1), "pair").reshape(kept.shape)
-        by_pair = jnp.where(pair == 0, jnp.stack([kept, got]), jnp.stack([got, kept]))
-        kept, sent = halves(by_pair, core, 3)
-        got = swap(sent.reshape(2, rows_in, -1), "core")
-        kept = kept.reshape(got.shape)
-        by_core = jnp.where(core == 0, jnp.stack([kept, got]), jnp.stack([got, kept]))
-        return by_core.reshape(4 * rows_in, planes * ff_rows)
-
-    w_gate_own = gather_zy(hidden_block(w_gate), depth).reshape(width, -1)
-    w_up_own = gather_zy(hidden_block(w_up), depth).reshape(width, -1)
-    w_down_own = gather_zy(w_down, depth).reshape(-1, width)
+    own_qk = own_heads * features
+
+    def deal(value):
+        dealt = lax.all_to_all(value, GRID, split_axis=2, concat_axis=1, tiled=True)
+        return dealt.reshape(-1, width)
+
+    def undeal(value):
+        return lax.all_to_all(
+            value.reshape(batches, -1, 1, width), GRID, split_axis=1, concat_axis=2, tiled=True
+        )
 
     gains = jnp.stack([norm_gain, mlp_gain])
     gains = lax.all_to_all(
         jnp.broadcast_to(gains[None], (seqs,) + gains.shape), GRID, split_axis=0, concat_axis=0, tiled=True
     )
-    gains = gains.transpose(1, 0, 2).reshape(2, 1, width).astype(jnp.float32)
+    gains = long(gains.transpose(1, 0, 2).reshape(2, 1, width))
     gain1, gain2 = gains[0], gains[1]
-
-    def deal(value):
-        dealt = lax.all_to_all(value, GRID, split_axis=2, concat_axis=1, tiled=True)
-        return dealt.reshape(-1, width)
-
-    def undeal(value):
-        return lax.all_to_all(
-            value.reshape(batches, -1, 1, width), GRID, split_axis=1, concat_axis=2, tiled=True
-        )
-
     start_rows = deal(tokens)
-    cot_rows = deal(cotangent)
+
+    qkv = jnp.concatenate(
+        [
+            weight.reshape(rows_in, depth, 2, 2, step).transpose(2, 3, 0, 1, 4).reshape(2, 2, rows_in, -1)
+            for weight, step in ((w_query, features), (w_key, features), (w_value, head_dim))
+        ],
+        3,
+    )
+    qkv = trade(trade(qkv, "core", 1, 1), "y", 0, 0)
+    out_column = column_of(w_out, depth)
+    qkv_column = column_of(qkv.reshape(4 * rows_in, -1), depth)
+
+    def joined(column, shape, axis):
+        mine = place_blocks(column)
+        return both(mine.reshape(shape), swap(mine, "pair").reshape(shape), pair, axis)
+
+    w_qkv = joined(qkv_column, (4 * depth, rows_in, -1), 1).reshape(width, -1)
+    w_out_own = joined(out_column, (depth, rows_in, width), 1).reshape(-1, width)
+
+    def hidden_block(weight):
+        cut = weight.reshape(rows_in, depth, 2, 2, 2, ff_rows)
+        cut = cut.transpose(2, 3, 4, 0, 1, 5).reshape(2, 2, 2, rows_in, own_ff)
+        return cut
+
+    cut = jnp.concatenate([hidden_block(w_gate), hidden_block(w_up)], 4)
+    cut = trade(cut, "y", 0, 0)
+    cut = trade(cut, "pair", 2, 2)
+    cut = trade(cut, "core", 1, 1).reshape(8 * rows_in, 2 * own_ff)
+    gate_up = gather_z(cut)
+    cot_rows = deal(after(cotangent, cut))
+    filler = jnp.zeros((width, wide - own_ff), jnp.bfloat16)
+    gate_up = jnp.concatenate([gate_up[:, :own_ff], filler, gate_up[:, own_ff:], filler], 1)
+    w_down_own = jnp.pad(gather_z(w_down), ((0, wide - own_ff), (0, 0)))
+
     count = start_rows.shape[0]
     seq_len = count // batches
 
     def lens_of(device):
         return jnp.sum(jnp.where(order == device, lengths, 0), 1)
 
-    lens = jnp.concatenate([lens_of(device_index), lens_of(device_index + 2 - 4 * core)])
+    by_core, by_y = device_index + 2 - 4 * core, 4 - 8 * y
+    lens = jnp.concatenate(
+        [lens_of(device_index), lens_of(device_index + by_y), lens_of(by_core), lens_of(by_core + by_y)]
+    )
     live = (
         lax.broadcasted_iota(jnp.int32, (batches, seq_len), 1) < lens[:batches, None]
     ).reshape(count, 1)
     d_out = jnp.where(live, cot_rows, jnp.zeros_like(cot_rows))
-    d_out_four = share_four(d_out)
-
-    start = start_rows.astype(jnp.float32)
+    d_out_all = share_eight(d_out)
+
+    start = long(start_rows)
     scale1 = row_norm(start)
-    hidden1 = (start * scale1 * gain1).astype(jnp.bfloat16)
-    hidden1 = jnp.concatenate([hidden1, swap(hidden1, "core")], 0)
-    qkv = matmul(hidden1, w_qkv).astype(jnp.bfloat16)
-    own_qk = own_heads * features
-    by_seq = (2 * batches, seq_len, own_heads, -1)
+    hidden1 = share_four(short(start * scale1 * gain1))
+    qkv = short(matmul(hidden1, w_qkv))
+    by_seq = (4 * batches, seq_len, own_heads, -1)
     query = qkv[:, :own_qk].reshape(by_seq)
     keys = qkv[:, own_qk : 2 * own_qk].reshape(by_seq)
     values = qkv[:, 2 * own_qk :].reshape(by_seq)
-    attended = attend(query, keys, values, lens).reshape(2 * count, -1)
-    branch = matmul(attended, w_out_all)
-    resid = start + branch[:count] + swap(branch[count:], "core")
+    attended = attend(query, keys, values, lens).reshape(4 * count, -1)
+    resid = start + sum_four(short(matmul(attended, w_out_own)))
     scale2 = row_norm(resid)
     normed2 = resid * scale2
-    hidden2 = share_four((normed2 * gain2).astype(jnp.bfloat16))
-
-    gate_pre = matmul(hidden2, w_gate_own)
-    up_pre = matmul(hidden2, w_up_own)
+    hidden2 = share_eight(short(normed2 * gain2))
+
+    both_pre = matmul(hidden2, gate_up)
+    gate_pre, up_pre = both_pre[:, :wide], both_pre[:, wide:]
     sigma = jax.nn.sigmoid(gate_pre)
-    inner = (gate_pre * sigma * up_pre).astype(jnp.bfloat16)
-    result = resid + sum_four(matmul(inner, w_down_own))
-    activations = undeal(result.astype(jnp.bfloat16))
+    inner = short(gate_pre * sigma * up_pre)
+    g_down = short(take_rows(inner, d_out_all)[:own_ff])
+    d_out_all, g_down = lax.optimization_barrier((d_out_all, g_down))
+    g_down = long(scatter_z(g_down))
+
+    d_inner = back_cols(d_out_all, w_down_own)
+    d_gate = short(d_inner * up_pre * sigma * (1.0 + gate_pre * (1.0 - sigma)))
+    d_up = short(d_inner * gate_pre * sigma)
+    d_both = jnp.concatenate([d_gate, d_up], 1)
+
+    def owned_hidden(columns):
+        rows = jnp.concatenate([columns[:, :own_ff], columns[:, wide : wide + own_ff]], 1)
+        rows = scatter_z(rows)
+        rows = rows.reshape(2, 2, 2, rows_in, -1)
+        rows = trade(rows, "y", 0, 0)
+        rows = trade(rows, "pair", 2, 2)
+        rows = trade(rows, "core", 1, 1)
+        def natural(part):
+            part = part.reshape(2, 2, 2, rows_in, depth, ff_rows).transpose(3, 4, 0, 1, 2, 5)
+            return long(part.reshape(rows_in, hidden))
+        return natural(rows[..., :own_ff]), natural(rows[..., own_ff:])
+
+    g_both = short(take_rows(hidden2, d_both))
+    d_both, inner, g_both = lax.optimization_barrier((d_both, inner, g_both))
+    g_gate, g_up = owned_hidden(g_both)
+    d_hidden2 = sum_eight(short(back_cols(d_both, gate_up)))
+    result = resid + sum_eight(short(matmul(inner, w_down_own)))
+    activations = undeal(short(result))
+
+    g_mlp = jnp.sum(d_hidden2 * normed2, 0)
+    d_resid = long(d_out) + norm_back(d_hidden2, normed2, scale2, gain2)
+    d_branch = share_four(short(d_resid))
+    d_attended = short(back_cols(d_branch, w_out_own))
 
     def owned_rows(partial):
-        return reduce_z(exchange_sum(partial, y, 1, "y"), depth)
-
-    def grid_rows(value):
-        return value.reshape((depth, 2, -1) + value.shape[1:])
-
-    g_down = owned_rows(grid_rows(take_rows(inner, d_out_four).astype(jnp.bfloat16)))
-
-    d_inner = back_cols(d_out_four, w_down_own)
-    d_gate = (d_inner * up_pre * sigma * (1.0 + gate_pre * (1.0 - sigma))).astype(jnp.bfloat16)
-    d_up = (d_inner * gate_pre * sigma).astype(jnp.bfloat16)
-
-    def owned_hidden(partial):
-        rows = owned_rows(grid_rows(partial)).astype(jnp.bfloat16).reshape(2, 2, rows_in, -1)
-        kept, sent = halves(rows, core, 0)
-        got = swap(sent, "core")
-        rows = jnp.where(core == 0, jnp.stack([kept, got]), jnp.stack([got, kept]))
-        kept, sent = halves(rows, pair, 1)
-        got = swap(sent, "pair")
-        rows = jnp.where(pair == 0, jnp.stack([kept, got], 1), jnp.stack([got, kept], 1))
-        rows = rows.reshape(2, 2, rows_in, planes, ff_rows).transpose(2, 3, 0, 1, 4)
-        return rows.reshape(rows_in, hidden).astype(jnp.float32)
-
-    g_gate = owned_hidden(take_rows(hidden2, d_gate).astype(jnp.bfloat16))
-    g_up = owned_hidden(take_rows(hidden2, d_up).astype(jnp.bfloat16))
-
-    d_hidden2 = sum_four(back_cols(d_gate, w_gate_own) + back_cols(d_up, w_up_own))
-    g_mlp = jnp.sum(d_hidden2 * normed2, 0)
-    d_resid = d_out.astype(jnp.float32) + norm_back(d_hidden2, normed2, scale2, gain2)
-    d_branch = d_resid.astype(jnp.bfloat16)
-    d_branch = jnp.concatenate([d_branch, swap(d_branch, "core")], 0)
-    d_attended = back_cols(d_branch, w_out_all).astype(jnp.bfloat16)
-
-    g_out = take_rows(attended, d_branch).astype(jnp.bfloat16)
-    g_out = exchange_sum(g_out.reshape(planes, 2, rows_in, width), pair, 1, "pair")
-    g_out = owned_rows(grid_rows(g_out.reshape(-1, width)))
+        kept, sent = halves(partial, pair, 2)
+        got = swap(sent.reshape(-1, sent.shape[-1]), "pair").reshape(kept.shape)
+        rows = short(long(kept) + long(got))
+        return reduce_z(rows.reshape(depth, -1, rows.shape[-1]), depth)
+
+    g_out = short(take_rows(attended, d_branch))
+    g_out = owned_rows(g_out.reshape(depth, 1, 2, rows_in, width))
 
     d_query, d_keys, d_values = attend_back(query, keys, values, lens, d_attended.reshape(by_seq))
     d_qkv = jnp.concatenate(
-        [part.reshape(2 * count, -1) for part in (d_query, d_keys, d_values)], 1
-    )
-    d_hidden1 = back_cols(d_qkv, w_qkv)
-    d_hidden1 = d_hidden1[:count] + swap(d_hidden1[count:], "core")
+        [part.reshape(4 * count, -1) for part in (d_query, d_keys, d_values)], 1
+    )
+    g_qkv = short(take_rows(hidden1, d_qkv))
+    g_qkv = short(owned_rows(g_qkv.reshape(depth, 4, 2, rows_in, -1)))
+    g_qkv = trade(trade(g_qkv.reshape(2, 2, rows_in, -1), "y", 0, 0), "core", 1, 1)
+
+    def all_heads(part, step):
+        part = part.reshape(2, 2, rows_in, depth, step).transpose(2, 3, 0, 1, 4)
+        return long(part.reshape(rows_in, -1))
+
+    g_query = all_heads(g_qkv[..., :own_qk], features)
+    g_key = all_heads(g_qkv[..., own_qk : 2 * own_qk], features)
+    g_value = all_heads(g_qkv[..., 2 * own_qk :], head_dim)
+
+    d_hidden1 = sum_four(short(back_cols(d_qkv, w_qkv)))
     normed1 = start * scale1
     g_norm = jnp.sum(d_hidden1 * normed1, 0)
     d_start = d_resid + norm_back(d_hidden1, normed1, scale1, gain1)
-    input_grad = undeal(d_start.astype(jnp.bfloat16))
-
-    g_qkv = take_rows(hidden1, d_qkv).astype(jnp.bfloat16)
-    g_qkv = exchange_sum(g_qkv.reshape(planes, 2, 2, rows_in, -1), pair, 2, "pair")
-    g_qkv = owned_rows(grid_rows(g_qkv.reshape(planes * 2 * rows_in, -1)))
-    kept, sent = halves(g_qkv.astype(jnp.bfloat16).reshape(2, rows_in, -1), core, 0)
-    got = swap(sent, "core")
-    g_qkv = jnp.where(core == 0, jnp.stack([kept, got]), jnp.stack([got, kept]))
-
-    def both_cores(part, step):
-        part = part.reshape(2, rows_in, planes, step).transpose(1, 2, 0, 3)
-        return part.reshape(rows_in, -1).astype(jnp.float32)
-
-    g_query = both_cores(g_qkv[..., :own_qk], features)
-    g_key = both_cores(g_qkv[..., own_qk : 2 * own_qk], features)
-    g_value = both_cores(g_qkv[..., 2 * own_qk :], head_dim)
+    input_grad = undeal(short(d_start))
 
     g_gains = jnp.stack([g_norm, g_mlp]).reshape(2, seqs, rows_in).transpose(1, 0, 2)
     g_gains = jnp.sum(

time: 1220 us -> 859 us (0.70)
  waiting for transfers between devices: 695 us -> 375 us
  starting transfers between devices: 129 us -> 83.4 us
  matrix products: 146 us -> 127 us
  Pallas kernels: 20.5 us -> 4.15 us
  other arithmetic: 75.7 us -> 90.3 us
  local copies, waits for them, and re-layouts: 140 us -> 153 us
  between operations: 2.6 us -> 15.5 us
    ppermute x30 -> x12, waiting for transfers between devices: 283 us -> 99.3 us  [from_above(): lax.ppermute(value, 'z', [((i + hops) % size, i) for i in range(size)])]
    ppermute x53 -> x52, waiting for transfers between devices: 386 us -> 258 us  [swap(): return lax.ppermute(value, axis, SWAP)]
    ppermute x30 -> x12, starting transfers between devices: 46.3 us -> 12.3 us  [from_above(): lax.ppermute(value, 'z', [((i + hops) % size, i) for i in range(size)])]
    all_to_all x1, waiting for transfers between devices: 23.1 us -> 0.01 us  [on_grid(): lax.all_to_all(g_gains, GRID, split_axis=0, concat_axis=0, tiled=True)]
    unnamed x208 -> x160, local copies, waits for them, and re-layouts: 26.5 us -> 47.5 us
    slice x7 -> x13, local copies, waits for them, and re-layouts: 8.94 us -> 29.1 us  [the longest x1 6.25 us: on_grid(): gate_up[:, own_ff:]]
    pallas_call x5 -> x2, Pallas kernels: 20.5 us -> 4.15 us  [place_blocks(): pl.pallas_call(functools.partial(place_kernel, depth), out_shape=jax.Shap...]
    convert_element_type x24 -> x15, other arithmetic: 40.7 us -> 24.7 us  [the longest x9 19.8 us: short(): return value.astype(jnp.bfloat16)]
  transfers between devices with their start and end apart: 89 -> 74, of which waited for: 42 -> 25; matrix products, arithmetic and copies ran while one was open for 25% -> 31% of each run, Pallas kernels for 2% -> 0%
where the time goes in v2:
time: 859 us; the launch traced here: 849 us
  waiting for transfers between devices  375 us (44%)
  local copies, waits for them, and re-layouts  153 us (18%)
  matrix products  127 us (15%)
  other arithmetic  90.3 us (11%)
  starting transfers between devices  83.4 us (10%)
  between operations  15.5 us (2%)
    ppermute x52, waiting for transfers between devices, swap(): return lax.ppermute(value, axis, SWAP)  258 us
    ppermute x12, waiting for transfers between devices, from_above(): lax.ppermute(value, 'z', [((i + hops) % size, i) for i in range(size)])  99.3 us
    unnamed x160, local copies, waits for them, and re-layouts  47.5 us
    dot_general x4, matrix products, back_cols(): lax.dot_general(left, right, (((1,), (1,)), ((), ())), preferred_element_...  40.5 us
    ppermute x52, starting transfers between devices, swap(): return lax.ppermute(value, axis, SWAP)  39.4 us
    dot_general x4, matrix products, take_rows(): lax.dot_general(left, right, (((0,), (0,)), ((), ())), preferred_element_...  37.8 us
    dot_general x4, matrix products, matmul(): return jnp.dot(left, right, preferred_element_type=jnp.float32)  33.1 us
    convert_element_type x15, local copies, waits for them, and re-layouts, long(): return value.astype(jnp.float32)  26.3 us
  transfers between devices with their start and end apart: 74, of which 25 were waited for; matrix products, arithmetic and copies ran while one was open for 31% of the time, Pallas kernels for 0%

profile of v2, /device:TPU:16, one launch (start us, length us, event | category | flops | bytes accessed | tf_op | source)
XLA Modules:
  0.0 848.7 jit_solution(5265198245041498203)
XLA Ops:
  30.8 8.2 all-to-all-done.1
  49.0 25.2 %collective-permute-done.16 = bf16[256,1408]{1,0:T(8,128)(2,1)} collective-permute-done((bf16[256,1408]{1,0:T(8,128)(2,1)S(1)}, bf16[256,1408]{1,0:T(8,128)(2,1)}, u32[]{:S(2)}, u32[]{:S(2)}) %collective-permute-start.16) | collective-permute-done | bytes 720928 | tf_op jit(solution)/shard_map/ppermute | solution.py:341
  93.9 17.6 %collective-permute-done.11.refs_3_ = bf16[64,2048]{1,0:T(8,128)(2,1)S(1)} collective-permute-done((bf16[64,2048]{1,0:T(8,128)(2,1)}, bf16[64,2048]{1,0:T(8,128)(2,1)S(1)}, u32[]{:S(2)}, u32[]{:S(2)}) %collective-permute-start.11) | collective-permute-done | bytes 262176 | tf_op jit(solution)/shard_map/ppermute | solution.py:345
  111.5 65.1 %collective-permute-done.9.refs_1_ = bf16[64,2048]{1,0:T(8,128)(2,1)S(1)} collective-permute-done((bf16[64,2048]{1,0:T(8,128)(2,1)}, bf16[64,2048]{1,0:T(8,128)(2,1)S(1)}, u32[]{:S(2)}, u32[]{:S(2)}) %collective-permute-start.9) | collective-permute-done | bytes 262176 | tf_op jit(solution)/shard_map/ppermute | solution.py:345
  184.9 20.8 %collective-permute-done.12 = bf16[4,64,2048]{2,1,0:T(8,128)(2,1)} collective-permute-done((bf16[4,64,2048]{2,1,0:T(8,128)(2,1)}, bf16[4,64,2048]{2,1,0:T(8,128)(2,1)}, u32[]{:S(2)}, u32[]{:S(2)}) %collective-permute-start.12) | collective-permute-done | bytes 1048608 | tf_op jit(solution)/shard_map/ppermute | solution.py:341
  209.1 23.5 %collective-permute-done.8 = bf16[4,256,640]{2,1,0:T(8,128)(2,1)} collective-permute-done((bf16[4,256,640]{2,1,0:T(8,128)(2,1)}, bf16[4,256,640]{2,1,0:T(8,128)(2,1)}, u32[]{:S(2)}, u32[]{:S(2)}) %collective-permute-start.8) | collective-permute-done | bytes 1310752 | tf_op jit(solution)/shard_map/ppermute | solution.py:341
  243.5 5.9 convolution_convert_fusion.7
  262.3 6.0 all-to-all-done.2
  278.1 19.9 %collective-permute-done.19 = bf16[256,2048]{1,0:T(8,128)(2,1)S(1)} collective-permute-done((bf16[256,2048]{1,0:T(8,128)(2,1)}, bf16[256,2048]{1,0:T(8,128)(2,1)S(1)}, u32[]{:S(2)}, u32[]{:S(2)}) %collective-permute-start.19) | collective-permute-done | bytes 1048608 | tf_op jit(solution)/shard_map/ppermute | solution.py:341
  305.6 26.2 %collective-permute-done.20 = bf16[128,2048]{1,0:T(8,128)(2,1)} collective-permute-done((bf16[128,2048]{1,0:T(8,128)(2,1)}, bf16[128,2048]{1,0:T(8,128)(2,1)}, u32[]{:S(2)}, u32[]{:S(2)}) %collective-permute-start.20) | collective-permute-done | bytes 524320 | tf_op jit(solution)/shard_map/ppermute | solution.py:341
  345.4 18.1 %collective-permute-done.28 = bf16[256,2048]{1,0:T(8,128)(2,1)S(1)} collective-permute-done((bf16[256,2048]{1,0:T(8,128)(2,1)S(1)}, bf16[256,2048]{1,0:T(8,128)(2,1)S(1)}, u32[]{:S(2)}, u32[]{:S(2)}) %collective-permute-start.28) | collective-permute-done | bytes 1048608 | tf_op jit(solution)/shard_map/ppermute | solution.py:341
  370.7 6.3 collective-permute-done.29
  384.9 6.3 fusion.73
  392.0 10.0 %concatenate.56 = bf16[2048,1536]{1,0:T(8,128)(2,1)} concatenate(bf16[2048,704]{1,0:T(8,128)(2,1)} %get-tuple-element.87, bf16[2048,64]{1,0:T(8,128)(2,1)} %broadcast_in_dim.69, bf16[2048,704]{1,0:T(8,128)(2,1)S(1)} %get-tuple-element.86, bf16[2048,64]{1,0:T(8,128)(2,1)} %broadcast_in_dim.69), dimensions={1} | concatenate | bytes 12582912 | tf_op jit(solution)/shard_map/concatenate | solution.py:602
  402.0 17.7 %fusion.76 = f32[2048,1536]{0,1:T(8,128)S(1)} fusion(bf16[2048,2048]{1,0:T(8,128)(2,1)} %constant_dynamic-update-slice_fusion.10, bf16[2048,1536]{1,0:T(8,128)(2,1)} %concatenate.56), kind=kOutput, calls=%fused_computation.218 | convolution fusion | flops 12884901888 | bytes 27262976 | tf_op jit(solution)/shard_map/dot_general | solution.py:361
  424.3 10.2 %fusion.77 = bf16[768,2048]{1,0:T(8,128)(2,1)S(1)} fusion(bf16[2048,768]{0,1:T(8,128)(2,1)S(1)} %multiply_convert_fusion.2, bf16[2048,2048]{1,0:T(8,128)(2,1)} %constant_dynamic-update-slice_fusion), kind=kOutput, calls=%fused_computation.219 | convolution fusion | flops 6442450944 | bytes 14680064 | tf_op jit(solution)/shard_map/dot_general | solution.py:28
  436.3 15.6 %multiply_convert_fusion.1 = (bf16[2048,768]{0,1:T(8,128)(2,1)S(1)}, bf16[2048,768]{0,1:T(8,128)(2,1)S(1)}) fusion(f32[2048,1536]{0,1:T(8,128)} %copy-done.5, bf16[2048,2048]{1,0:T(8,128)(2,1)} %constant_dynamic-update-slice_fusion, bf16[704,2048]{1,0:T(8,128)(2,1)} %all-gather.5.cloned.1.call-done), kind=kOutput, calls=%fused_computation.8 | convolution fusion | flops 6462898176 | bytes 30146560 | tf_op jit(solution)/shard_map/dot_general | solution.py:34
  453.7 17.5 %convolution_convert_fusion.2 = bf16[2048,1536]{1,0:T(8,128)(2,1)} fusion(bf16[2048,2048]{1,0:T(8,128)(2,1)} %constant_dynamic-update-slice_fusion.10, bf16[2048,768]{0,1:T(8,128)(2,1)S(1)} %get-tuple-element.75, bf16[2048,768]{0,1:T(8,128)(2,1)S(1)} %get-tuple-element.74), kind=kOutput, calls=%fused_computation.5 | convolution fusion | flops 12900630528 | bytes 20971520 | tf_op jit(solution)/shard_map/dot_general | solution.py:28
  474.0 16.2 %convolution_convert_fusion = bf16[2048,2048]{1,0:T(8,128)(2,1)S(1)} fusion(bf16[2048,1536]{0,1:T(8,128)(2,1)S(1)} %pad_maximum_fusion, bf16[2048,1536]{1,0:T(8,128)(2,1)} %concatenate.56), kind=kOutput, calls=%fused_computation.3 | convolution fusion | flops 12889096192 | bytes 20971520 | tf_op jit(solution)/shard_map/dot_general | solution.py:34
  497.3 7.1 convolution_convert_fusion.1
  514.5 8.5 convert_add_fusion
  529.2 10.7 %fusion.63 = (bf16[1024,2048]{1,0:T(8,128)(2,1)}, f32[1024,2048]{1,0:T(8,128)}) fusion(bf16[1024,2048]{1,0:T(8,128)(2,1)} %collective-permute-done.36, bf16[2048,2048]{1,0:T(8,128)(2,1)} %copy-done.7), kind=kLoop, calls=%fused_computation.211 | loop fusion | flops 8388608 | bytes 20971520 | tf_op jit(solution)/shard_map/convert.37
  549.3 7.2 collective-permute-done.37
  568.6 10.5 %collective-permute-done.43 = bf16[256,2048]{1,0:T(8,128)(2,1)S(1)} collective-permute-done((bf16[256,2048]{1,0:T(8,128)(2,1)}, bf16[256,2048]{1,0:T(8,128)(2,1)S(1)}, u32[]{:S(2)}, u32[]{:S(2)}) %collective-permute-start.43) | collective-permute-done | bytes 1048608 | tf_op jit(solution)/shard_map/ppermute | solution.py:341
  582.0 18.3 %collective-permute-done.38 = bf16[256,2048]{1,0:T(8,128)(2,1)} collective-permute-done((bf16[256,2048]{1,0:T(8,128)(2,1)}, bf16[256,2048]{1,0:T(8,128)(2,1)}, u32[]{:S(2)}, u32[]{:S(2)}) %collective-permute-start.38) | collective-permute-done | bytes 1048608 | tf_op jit(solution)/shard_map/ppermute | solution.py:341
  600.3 6.8 fusion.71
  608.5 22.6 %collective-permute-done.46 = bf16[256,2048]{1,0:T(8,128)(2,1)S(1)} collective-permute-done((bf16[256,2048]{1,0:T(8,128)(2,1)}, bf16[256,2048]{1,0:T(8,128)(2,1)S(1)}, u32[]{:S(2)}, u32[]{:S(2)}) %collective-permute-start.46) | collective-permute-done | bytes 1048608 | tf_op jit(solution)/shard_map/ppermute | solution.py:341
  693.1 15.0 %collective-permute-done.51 = bf16[1024,640]{1,0:T(8,128)(2,1)} collective-permute-done((bf16[1024,640]{1,0:T(8,128)(2,1)}, bf16[1024,640]{1,0:T(8,128)(2,1)}, u32[]{:S(2)}, u32[]{:S(2)}) %collective-permute-start.51) | collective-permute-done | bytes 1310752 | tf_op jit(solution)/shard_map/ppermute | solution.py:341
  715.8 14.0 %collective-permute-done.57 = bf16[256,2048]{1,0:T(8,128)(2,1)} collective-permute-done((bf16[256,2048]{1,0:T(8,128)(2,1)}, bf16[256,2048]{1,0:T(8,128)(2,1)}, u32[]{:S(2)}, u32[]{:S(2)}) %collective-permute-start.57) | collective-permute-done | bytes 1048608 | tf_op jit(solution)/shard_map/ppermute | solution.py:341
  736.4 11.7 %collective-permute-done.53 = bf16[256,640]{1,0:T(8,128)(2,1)S(1)} collective-permute-done((bf16[256,640]{1,0:T(8,128)(2,1)S(1)}, bf16[256,640]{1,0:T(8,128)(2,1)S(1)}, u32[]{:S(2)}, u32[]{:S(2)}) %collective-permute-start.53) | collective-permute-done | bytes 327712 | tf_op jit(solution)/shard_map/ppermute | solution.py:345
  770.3 11.8 %collective-permute-done.61 = bf16[256,1408]{1,0:T(8,128)(2,1)S(1)} collective-permute-done((bf16[256,1408]{1,0:T(8,128)(2,1)S(1)}, bf16[256,1408]{1,0:T(8,128)(2,1)S(1)}, u32[]{:S(2)}, u32[]{:S(2)}) %collective-permute-start.61) | collective-permute-done | bytes 720928 | tf_op jit(solution)/shard_map/ppermute | solution.py:341
  792.6 16.4 %collective-permute-done.62 = bf16[256,1408]{1,0:T(8,128)(2,1)S(1)} collective-permute-done((bf16[256,1408]{1,0:T(8,128)(2,1)S(1)}, bf16[256,1408]{1,0:T(8,128)(2,1)S(1)}, u32[]{:S(2)}, u32[]{:S(2)}) %collective-permute-start.62) | collective-permute-done | bytes 720928 | tf_op jit(solution)/shard_map/ppermute | solution.py:341
  (441 shorter events, 336.4 us)
Async XLA Ops:
  38.9 39.0 %all-to-all-start = ((bf16[2,4,32,2048]{3,1,0,2:T(4,128)(2,1)}), bf16[2,4,32,2048]{3,1,0,2:T(4,128)(2,1)S(1)}, u32[]{:S(2)}, u32[]{:S(2)}) async-start(bf16[2,4,32,2048]{3,1,0,2:T(4,128)(2,1)} %copy.144), calls=%async_computation | async-start | bytes 2097152 | tf_op jit(solution)/shard_map/all_to_all | solution.py:556
  44.9 340.0 %all-gather.3.cloned.1.call-start = ((), (), s32[]{:S(2)}) async-start(), calls=%async_computation.8 | async-start | bytes 7208960 | tf_op jit(solution)/shard_map/all_gather | solution.py:408
  48.2 45.6 %collective-permute-start.10 = (bf16[64,2048]{1,0:T(8,128)(2,1)}, bf16[64,2048]{1,0:T(8,128)(2,1)}, u32[]{:S(2)}, u32[]{:S(2)}) collective-permute-start(bf16[64,2048]{1,0:T(8,128)(2,1)} %refs_0_.1), channel_id=1, source_target_pairs={{16,0},{24,8},{0,16},{8,24},{17,1},{25,9},{1,17},{9,25},{18,2},{26... | collective-permute-start | bytes 786440 | tf_op jit(solution)/shard_map/ppermute | solution.py:345
  87.7 95.9 %collective-permute-start = (bf16[256,2048]{1,0:T(8,128)(2,1)}, bf16[256,2048]{1,0:T(8,128)(2,1)}, u32[]{:S(2)}, u32[]{:S(2)}) collective-permute-start(bf16[256,2048]{1,0:T(8,128)(2,1)} %multiply_convert_fusion.5), channel_id=1, source_target_pairs={{0,4},{4,0},{1,5},{5,1},{2,6},{6,2},{3,7},{7,3},{8,12},{12,8},{9,1... | collective-permute-start | bytes 3145736 | tf_op jit(solution)/shard_map/ppermute | solution.py:341
  91.5 87.9 %collective-permute-start.5 = (bf16[256,640]{1,0:T(8,128)(2,1)S(1)}, bf16[256,640]{1,0:T(8,128)(2,1)}, u32[]{:S(2)}, u32[]{:S(2)}) collective-permute-start(bf16[256,640]{1,0:T(8,128)(2,1)S(1)} %bitcast.247), channel_id=1, source_target_pairs={{8,0},{16,8},{24,16},{0,24},{9,1},{17,9},{25,17},{1,25},{10,2},{18... | collective-permute-start | bytes 983048 | tf_op jit(solution)/shard_map/ppermute | solution.py:345
  92.1 87.2 %collective-permute-start.6 = (bf16[256,640]{1,0:T(8,128)(2,1)S(1)}, bf16[256,640]{1,0:T(8,128)(2,1)}, u32[]{:S(2)}, u32[]{:S(2)}) collective-permute-start(bf16[256,640]{1,0:T(8,128)(2,1)S(1)} %bitcast.248), channel_id=1, source_target_pairs={{16,0},{24,8},{0,16},{8,24},{17,1},{25,9},{1,17},{9,25},{18,2},{26... | collective-permute-start | bytes 983048 | tf_op jit(solution)/shard_map/ppermute | solution.py:345
  93.9 85.5 %collective-permute-start.7 = (bf16[256,640]{1,0:T(8,128)(2,1)S(1)}, bf16[256,640]{1,0:T(8,128)(2,1)}, u32[]{:S(2)}, u32[]{:S(2)}) collective-permute-start(bf16[256,640]{1,0:T(8,128)(2,1)S(1)} %bitcast.249), channel_id=1, source_target_pairs={{24,0},{0,8},{8,16},{16,24},{25,1},{1,9},{9,17},{17,25},{26,2},{2,... | collective-permute-start | bytes 983048 | tf_op jit(solution)/shard_map/ppermute | solution.py:345
  111.5 65.1 %collective-permute-start.9 = (bf16[64,2048]{1,0:T(8,128)(2,1)}, bf16[64,2048]{1,0:T(8,128)(2,1)S(1)}, u32[]{:S(2)}, u32[]{:S(2)}) collective-permute-start(bf16[64,2048]{1,0:T(8,128)(2,1)} %refs_0_.1), channel_id=1, source_target_pairs={{8,0},{16,8},{24,16},{0,24},{9,1},{17,9},{25,17},{1,25},{10,2},{18... | collective-permute-start | bytes 786440 | tf_op jit(solution)/shard_map/ppermute | solution.py:345
  181.6 51.1 %collective-permute-start.8 = (bf16[4,256,640]{2,1,0:T(8,128)(2,1)}, bf16[4,256,640]{2,1,0:T(8,128)(2,1)}, u32[]{:S(2)}, u32[]{:S(2)}) collective-permute-start(bf16[4,256,640]{2,1,0:T(8,128)(2,1)} %place_blocks.2), channel_id=1, source_target_pairs={{0,1},{1,0},{2,3},{3,2},{4,5},{5,4},{6,7},{7,6},{8,9},{9,8},{10,11... | collective-permute-start | bytes 3932168 | tf_op jit(solution)/shard_map/ppermute | solution.py:341
  183.6 59.9 %collective-permute-start.1 = (bf16[256,2048]{1,0:T(8,128)(2,1)}, bf16[256,2048]{1,0:T(8,128)(2,1)}, u32[]{:S(2)}, u32[]{:S(2)}) collective-permute-start(bf16[256,2048]{1,0:T(8,128)(2,1)} %multiply_convert_fusion.5), channel_id=1, source_target_pairs={{0,2},{2,0},{1,3},{3,1},{4,6},{6,4},{5,7},{7,5},{8,10},{10,8},{9,1... | collective-permute-start | bytes 3145736 | tf_op jit(solution)/shard_map/ppermute | solution.py:341
  183.6 59.9 %collective-permute-start.2 = (bf16[256,2048]{1,0:T(8,128)(2,1)}, bf16[256,2048]{1,0:T(8,128)(2,1)}, u32[]{:S(2)}, u32[]{:S(2)}) collective-permute-start(bf16[256,2048]{1,0:T(8,128)(2,1)} %collective-permute-done), channel_id=1, source_target_pairs={{0,2},{2,0},{1,3},{3,1},{4,6},{6,4},{5,7},{7,5},{8,10},{10,8},{9,1... | collective-permute-start | bytes 3145736 | tf_op jit(solution)/shard_map/ppermute | solution.py:341
  243.0 193.3 %all-gather.5.cloned.1.call-start = ((), (), s32[]{:S(2)}) async-start(), calls=%async_computation.9 | async-start | bytes 3604480 | tf_op jit(solution)/shard_map/all_gather | solution.py:408
  276.5 57.2 %collective-permute-start.14 = (bf16[256,2048]{1,0:T(8,128)(2,1)}, bf16[256,2048]{1,0:T(8,128)(2,1)}, u32[]{:S(2)}, u32[]{:S(2)}) collective-permute-start(bf16[256,2048]{1,0:T(8,128)(2,1)} %add_convert_fusion.2), channel_id=1, source_target_pairs={{0,4},{4,0},{1,5},{5,1},{2,6},{6,2},{3,7},{7,3},{8,12},{12,8},{9,1... | collective-permute-start | bytes 3145736 | tf_op jit(solution)/shard_map/ppermute | solution.py:341
  298.8 385.5 %reduce-scatter.5.cloned.1.call-start = ((), (), s32[]{:S(2)}) async-start(), calls=%async_computation.11 | async-start | bytes 3604480 | tf_op jit(solution)/shard_map/reduce_scatter | solution.py:412
  299.1 41.7 %collective-permute-start.22 = (bf16[256,2048]{1,0:T(8,128)(2,1)}, bf16[256,2048]{1,0:T(8,128)(2,1)S(1)}, u32[]{:S(2)}, u32[]{:S(2)}) collective-permute-start(bf16[256,2048]{1,0:T(8,128)(2,1)} %get-tuple-element.73), channel_id=1, source_target_pairs={{0,2},{2,0},{1,3},{3,1},{4,6},{6,4},{5,7},{7,5},{8,10},{10,8},{9,1... | collective-permute-start | bytes 3145736 | tf_op jit(solution)/shard_map/ppermute | solution.py:341
  300.7 37.5 %collective-permute-start.21 = (bf16[128,2048]{1,0:T(8,128)(2,1)S(1)}, bf16[128,2048]{1,0:T(8,128)(2,1)S(1)}, u32[]{:S(2)}, u32[]{:S(2)}) collective-permute-start(bf16[128,2048]{1,0:T(8,128)(2,1)S(1)} %slice.241), channel_id=1, source_target_pairs={{0,1},{1,0},{2,3},{3,2},{4,5},{5,4},{6,7},{7,6},{8,9},{9,8},{10,11... | collective-permute-start | bytes 1572872 | tf_op jit(solution)/shard_map/ppermute | solution.py:341
  302.2 39.6 %collective-permute-start.23 = (bf16[256,2048]{1,0:T(8,128)(2,1)}, bf16[256,2048]{1,0:T(8,128)(2,1)S(1)}, u32[]{:S(2)}, u32[]{:S(2)}) collective-permute-start(bf16[256,2048]{1,0:T(8,128)(2,1)} %collective-permute-done.18), channel_id=1, source_target_pairs={{0,2},{2,0},{1,3},{3,1},{4,6},{6,4},{5,7},{7,5},{8,10},{10,8},{9,1... | collective-permute-start | bytes 3145736 | tf_op jit(solution)/shard_map/ppermute | solution.py:341
  345.4 34.6 %collective-permute-start.31 = (bf16[256,2048]{1,0:T(8,128)(2,1)S(1)}, bf16[256,2048]{1,0:T(8,128)(2,1)S(1)}, u32[]{:S(2)}, u32[]{:S(2)}) collective-permute-start(bf16[256,2048]{1,0:T(8,128)(2,1)S(1)} %get-tuple-element.69), channel_id=1, source_target_pairs={{0,2},{2,0},{1,3},{3,1},{4,6},{6,4},{5,7},{7,5},{8,10},{10,8},{9,1... | collective-permute-start | bytes 3145736 | tf_op jit(solution)/shard_map/ppermute | solution.py:341
  509.4 252.8 %reduce-scatter.3.cloned.1.call-start = ((), (), s32[]{:S(2)}) async-start(), calls=%async_computation.10 | async-start | bytes 7208960 | tf_op jit(solution)/shard_map/reduce_scatter | solution.py:412
  546.1 33.1 %collective-permute-start.43 = (bf16[256,2048]{1,0:T(8,128)(2,1)}, bf16[256,2048]{1,0:T(8,128)(2,1)S(1)}, u32[]{:S(2)}, u32[]{:S(2)}) collective-permute-start(bf16[256,2048]{1,0:T(8,128)(2,1)} %pad_maximum_fusion.6), channel_id=1, source_target_pairs={{0,4},{4,0},{1,5},{5,1},{2,6},{6,2},{3,7},{7,3},{8,12},{12,8},{9,1... | collective-permute-start | bytes 3145736 | tf_op jit(solution)/shard_map/ppermute | solution.py:341
  559.7 40.6 %collective-permute-start.38 = (bf16[256,2048]{1,0:T(8,128)(2,1)}, bf16[256,2048]{1,0:T(8,128)(2,1)}, u32[]{:S(2)}, u32[]{:S(2)}) collective-permute-start(bf16[256,2048]{1,0:T(8,128)(2,1)} %pad_maximum_fusion.4), channel_id=1, source_target_pairs={{0,4},{4,0},{1,5},{5,1},{2,6},{6,2},{3,7},{7,3},{8,12},{12,8},{9,1... | collective-permute-start | bytes 3145736 | tf_op jit(solution)/shard_map/ppermute | solution.py:341
  562.4 37.9 %collective-permute-start.40 = (bf16[256,2048]{1,0:T(8,128)(2,1)}, bf16[256,2048]{1,0:T(8,128)(2,1)}, u32[]{:S(2)}, u32[]{:S(2)}) collective-permute-start(bf16[256,2048]{1,0:T(8,128)(2,1)} %pad_maximum_fusion.5), channel_id=1, source_target_pairs={{0,1},{1,0},{2,3},{3,2},{4,5},{5,4},{6,7},{7,6},{8,9},{9,8},{10,11... | collective-permute-start | bytes 3145736 | tf_op jit(solution)/shard_map/ppermute | solution.py:341
  633.4 56.9 %all-to-all-start.3 = ((bf16[2,128,1,2048]{3,0,2,1:T(2,128)(2,1)}), bf16[2,128,1,2048]{3,0,2,1:T(2,128)(2,1)}, u32[]{:S(2)}, u32[]{:S(2)}) async-start(bf16[2,128,1,2048]{3,0,2,1:T(2,128)(2,1)} %copy.172), calls=%async_computation.3 | async-start | bytes 2097152 | tf_op jit(solution)/shard_map/all_to_all | solution.py:560
  668.1 45.8 %collective-permute-start.49 = (bf16[512,2048]{1,0:T(8,128)(2,1)}, bf16[512,2048]{1,0:T(8,128)(2,1)S(1)}, u32[]{:S(2)}, u32[]{:S(2)}) collective-permute-start(bf16[512,2048]{1,0:T(8,128)(2,1)} %slice.269), channel_id=1, source_target_pairs={{0,2},{2,0},{1,3},{3,1},{4,6},{6,4},{5,7},{7,5},{8,10},{10,8},{9,1... | collective-permute-start | bytes 6291464 | tf_op jit(solution)/shard_map/ppermute | solution.py:341
  683.5 46.3 %collective-permute-start.57 = (bf16[256,2048]{1,0:T(8,128)(2,1)}, bf16[256,2048]{1,0:T(8,128)(2,1)}, u32[]{:S(2)}, u32[]{:S(2)}) collective-permute-start(bf16[256,2048]{1,0:T(8,128)(2,1)} %bitcast.80), channel_id=1, source_target_pairs={{0,1},{1,0},{2,3},{3,2},{4,5},{5,4},{6,7},{7,6},{8,9},{9,8},{10,11... | collective-permute-start | bytes 3145736 | tf_op jit(solution)/shard_map/ppermute | solution.py:341
  710.5 37.6 %collective-permute-start.53 = (bf16[256,640]{1,0:T(8,128)(2,1)S(1)}, bf16[256,640]{1,0:T(8,128)(2,1)S(1)}, u32[]{:S(2)}, u32[]{:S(2)}) collective-permute-start(bf16[256,640]{1,0:T(8,128)(2,1)S(1)} %get-tuple-element.115), channel_id=1, source_target_pairs={{16,0},{24,8},{0,16},{8,24},{17,1},{25,9},{1,17},{9,25},{18,2},{26... | collective-permute-start | bytes 983048 | tf_op jit(solution)/shard_map/ppermute | solution.py:345
  713.8 39.1 %collective-permute-start.54 = (bf16[256,640]{1,0:T(8,128)(2,1)S(1)}, bf16[256,640]{1,0:T(8,128)(2,1)S(1)}, u32[]{:S(2)}, u32[]{:S(2)}) collective-permute-start(bf16[256,640]{1,0:T(8,128)(2,1)S(1)} %get-tuple-element.114), channel_id=1, source_target_pairs={{24,0},{0,8},{8,16},{16,24},{25,1},{1,9},{9,17},{17,25},{26,2},{2,... | collective-permute-start | bytes 983048 | tf_op jit(solution)/shard_map/ppermute | solution.py:345
  714.3 40.4 %collective-permute-start.50 = (bf16[256,2048]{1,0:T(8,128)(2,1)S(1)}, bf16[256,2048]{1,0:T(8,128)(2,1)S(1)}, u32[]{:S(2)}, u32[]{:S(2)}) collective-permute-start(bf16[256,2048]{1,0:T(8,128)(2,1)S(1)} %add_convert_fusion.1), channel_id=1, source_target_pairs={{0,4},{4,0},{1,5},{5,1},{2,6},{6,2},{3,7},{7,3},{8,12},{12,8},{9,1... | collective-permute-start | bytes 3145736 | tf_op jit(solution)/shard_map/ppermute | solution.py:341
  732.4 56.8 %collective-permute-start.58 = (bf16[64,2048]{1,0:T(8,128)(2,1)}, bf16[64,2048]{1,0:T(8,128)(2,1)}, u32[]{:S(2)}, u32[]{:S(2)}) collective-permute-start(bf16[64,2048]{1,0:T(8,128)(2,1)} %get-tuple-element.118), channel_id=1, source_target_pairs={{8,0},{16,8},{24,16},{0,24},{9,1},{17,9},{25,17},{1,25},{10,2},{18... | collective-permute-start | bytes 786440 | tf_op jit(solution)/shard_map/ppermute | solution.py:345
  733.2 56.0 %collective-permute-start.59 = (bf16[64,2048]{1,0:T(8,128)(2,1)}, bf16[64,2048]{1,0:T(8,128)(2,1)}, u32[]{:S(2)}, u32[]{:S(2)}) collective-permute-start(bf16[64,2048]{1,0:T(8,128)(2,1)} %get-tuple-element.120), channel_id=1, source_target_pairs={{16,0},{24,8},{0,16},{8,24},{17,1},{25,9},{1,17},{9,25},{18,2},{26... | collective-permute-start | bytes 786440 | tf_op jit(solution)/shard_map/ppermute | solution.py:345
  748.0 41.1 %collective-permute-start.60 = (bf16[64,2048]{1,0:T(8,128)(2,1)}, bf16[64,2048]{1,0:T(8,128)(2,1)}, u32[]{:S(2)}, u32[]{:S(2)}) collective-permute-start(bf16[64,2048]{1,0:T(8,128)(2,1)} %get-tuple-element.119), channel_id=1, source_target_pairs={{24,0},{0,8},{8,16},{16,24},{25,1},{1,9},{9,17},{17,25},{26,2},{2,... | collective-permute-start | bytes 786440 | tf_op jit(solution)/shard_map/ppermute | solution.py:345
  753.1 38.2 %collective-permute-start.55 = (bf16[128,640]{1,0:T(8,128)(2,1)S(1)}, bf16[128,640]{1,0:T(8,128)(2,1)}, u32[]{:S(2)}, u32[]{:S(2)}) collective-permute-start(bf16[128,640]{1,0:T(8,128)(2,1)S(1)} %bitcast.271), channel_id=1, source_target_pairs={{0,4},{4,0},{1,5},{5,1},{2,6},{6,2},{3,7},{7,3},{8,12},{12,8},{9,1... | collective-permute-start | bytes 491528 | tf_op jit(solution)/shard_map/ppermute | solution.py:341
  (105 other events, 1929.2 us)
Sparse Core Ops, SparseCore 0:
  85.6 137.2 all-gather.2
  298.9 58.2 all-gather.4
  509.5 56.3 reduce-scatter.4
  568.8 123.5 reduce-scatter.2

commit v3 on v2

--- a/solution.py
+++ b/solution.py
@@ -361,49 +361,6 @@
     return jnp.dot(left, right, preferred_element_type=jnp.float32)
 
 
-def place_kernel(depth, *refs):
-    blocks, whole, held, sems = refs[:depth], *refs[depth:]
-    z = lax.axis_index("z")
-    fetched, placed = [], []
-    for hops in range(depth):
-        at = lax.rem(z + hops, depth)
-        fetched.append(
-            pltpu.make_async_copy(blocks[hops], held.at[hops], sems.at[0, hops])
-        )
-        placed.append(
-            pltpu.make_async_copy(held.at[hops], whole.at[at], sems.at[1, hops])
-        )
-    for copy in fetched:
-        copy.start()
-    for arrived, copy in zip(fetched, placed):
-        arrived.wait()
-        copy.start()
-    for copy in placed:
-        copy.wait()
-
-
-def place_blocks(blocks):
-    depth = len(blocks)
-    shape, dtype = blocks[0].shape, blocks[0].dtype
-    moved = 2 * depth * math.prod(shape) * dtype.itemsize
-    return pl.pallas_call(
-        functools.partial(place_kernel, depth),
-        out_shape=jax.ShapeDtypeStruct((depth,) + shape, dtype),
-        in_specs=[pl.BlockSpec(memory_space=pl.ANY)] * depth,
-        out_specs=pl.BlockSpec(memory_space=pl.ANY),
-        scratch_shapes=[
-            pltpu.VMEM((depth,) + shape, dtype),
-            pltpu.SemaphoreType.DMA((2, depth)),
-        ],
-        cost_estimate=pl.CostEstimate(flops=0, bytes_accessed=moved, transcendentals=0),
-        name="place_blocks",
-    )(*blocks)
-
-
-def column_of(block, depth):
-    return [block] + [from_above(block, hops, depth) for hops in range(1, depth)]
-
-
 def gather_z(block):
     return lax.all_gather(block, "z", axis=0, tiled=True)
 
@@ -434,13 +391,6 @@
     return jnp.where(
         index == 0, jnp.stack([mine, other], axis), jnp.stack([other, mine], axis)
     )
-
-
-def trade(value, name, axis, into):
-    index = lax.axis_index(name)
-    kept, sent = halves(value, index, axis)
-    flat = sent.reshape(-1, sent.shape[-1]) if sent.ndim > 2 else sent
-    return both(kept, swap(flat, name).reshape(kept.shape), index, into)
 
 
 def row_norm(value):
@@ -545,8 +495,9 @@
     device_index = lax.axis_index(GRID)
     rows_in, hidden = w_gate.shape
     ff_rows = w_down.shape[0]
-    own_ff = depth * ff_rows
-    wide = -(-own_ff // LANES) * LANES
+    ff_block = -(-depth * ff_rows // LANES) * LANES // depth
+    fill = ff_block - ff_rows
+    own_ff = depth * ff_block
     own_heads = depth
     features = w_query.shape[1] // HEADS
     head_dim = width // HEADS
@@ -561,47 +512,41 @@
             value.reshape(batches, -1, 1, width), GRID, split_axis=1, concat_axis=2, tiled=True
         )
 
+    def spread(value, names):
+        return lax.all_to_all(value, names, split_axis=0, concat_axis=0, tiled=True)
+
+    qkv = jnp.concatenate(
+        [
+            weight.reshape(rows_in, depth, 4, step).transpose(2, 0, 1, 3).reshape(4, rows_in, -1)
+            for weight, step in ((w_query, features), (w_key, features), (w_value, head_dim))
+        ],
+        2,
+    )
+    qkv = spread(qkv, ("y", "core"))
+    start_rows = deal(after(tokens, qkv))
     gains = jnp.stack([norm_gain, mlp_gain])
-    gains = lax.all_to_all(
-        jnp.broadcast_to(gains[None], (seqs,) + gains.shape), GRID, split_axis=0, concat_axis=0, tiled=True
-    )
+    gains = spread(jnp.broadcast_to(gains[None], (seqs,) + gains.shape), GRID)
     gains = long(gains.transpose(1, 0, 2).reshape(2, 1, width))
     gain1, gain2 = gains[0], gains[1]
-    start_rows = deal(tokens)
-
-    qkv = jnp.concatenate(
-        [
-            weight.reshape(rows_in, depth, 2, 2, step).transpose(2, 3, 0, 1, 4).reshape(2, 2, rows_in, -1)
-            for weight, step in ((w_query, features), (w_key, features), (w_value, head_dim))
-        ],
-        3,
-    )
-    qkv = trade(trade(qkv, "core", 1, 1), "y", 0, 0)
-    out_column = column_of(w_out, depth)
-    qkv_column = column_of(qkv.reshape(4 * rows_in, -1), depth)
-
-    def joined(column, shape, axis):
-        mine = place_blocks(column)
+
+    def hidden_block(weight):
+        cut = weight.reshape(rows_in, depth, 8, ff_rows).transpose(2, 0, 1, 3)
+        cut = jnp.pad(cut, ((0, 0), (0, 0), (0, 0), (0, fill)))
+        return cut.reshape(8, rows_in, own_ff)
+
+    cut = jnp.concatenate([hidden_block(w_gate), hidden_block(w_up)], 2)
+    cut = spread(cut, ("y", "core", "pair"))
+
+    out_rows = gather_z(w_out)
+    qkv_rows = gather_z(after(qkv.reshape(4 * rows_in, -1), out_rows))
+    w_down_own = gather_z(after(jnp.pad(w_down, ((0, fill), (0, 0))), qkv_rows))
+    gate_up = gather_z(after(cut.reshape(8 * rows_in, 2 * own_ff), w_down_own))
+
+    def joined(mine, shape, axis):
         return both(mine.reshape(shape), swap(mine, "pair").reshape(shape), pair, axis)
 
-    w_qkv = joined(qkv_column, (4 * depth, rows_in, -1), 1).reshape(width, -1)
-    w_out_own = joined(out_column, (depth, rows_in, width), 1).reshape(-1, width)
-
-    def hidden_block(weight):
-        cut = weight.reshape(rows_in, depth, 2, 2, 2, ff_rows)
-        cut = cut.transpose(2, 3, 4, 0, 1, 5).reshape(2, 2, 2, rows_in, own_ff)
-        return cut
-
-    cut = jnp.concatenate([hidden_block(w_gate), hidden_block(w_up)], 4)
-    cut = trade(cut, "y", 0, 0)
-    cut = trade(cut, "pair", 2, 2)
-    cut = trade(cut, "core", 1, 1).reshape(8 * rows_in, 2 * own_ff)
-    gate_up = gather_z(cut)
-    cot_rows = deal(after(cotangent, cut))
-    filler = jnp.zeros((width, wide - own_ff), jnp.bfloat16)
-    gate_up = jnp.concatenate([gate_up[:, :own_ff], filler, gate_up[:, own_ff:], filler], 1)
-    w_down_own = jnp.pad(gather_z(w_down), ((0, wide - own_ff), (0, 0)))
-
+    w_qkv = joined(qkv_rows, (4 * depth, rows_in, -1), 1).reshape(width, -1)
+    w_out_own = joined(out_rows, (depth, rows_in, width), 1).reshape(-1, width)
     count = start_rows.shape[0]
     seq_len = count // batches
 
@@ -612,15 +557,15 @@
     lens = jnp.concatenate(
         [lens_of(device_index), lens_of(device_index + by_y), lens_of(by_core), lens_of(by_core + by_y)]
     )
+    start = long(start_rows)
+    scale1 = row_norm(start)
+    hidden1 = share_four(short(start * scale1 * gain1))
+    cot_rows = deal(after(cotangent, hidden1))
     live = (
         lax.broadcasted_iota(jnp.int32, (batches, seq_len), 1) < lens[:batches, None]
     ).reshape(count, 1)
     d_out = jnp.where(live, cot_rows, jnp.zeros_like(cot_rows))
     d_out_all = share_eight(d_out)
-
-    start = long(start_rows)
-    scale1 = row_norm(start)
-    hidden1 = share_four(short(start * scale1 * gain1))
     qkv = short(matmul(hidden1, w_qkv))
     by_seq = (4 * batches, seq_len, own_heads, -1)
     query = qkv[:, :own_qk].reshape(by_seq)
@@ -633,34 +578,24 @@
     hidden2 = share_eight(short(normed2 * gain2))
 
     both_pre = matmul(hidden2, gate_up)
-    gate_pre, up_pre = both_pre[:, :wide], both_pre[:, wide:]
+    gate_pre, up_pre = both_pre[:, :own_ff], both_pre[:, own_ff:]
     sigma = jax.nn.sigmoid(gate_pre)
     inner = short(gate_pre * sigma * up_pre)
-    g_down = short(take_rows(inner, d_out_all)[:own_ff])
+    g_down = short(take_rows(inner, d_out_all))
     d_out_all, g_down = lax.optimization_barrier((d_out_all, g_down))
-    g_down = long(scatter_z(g_down))
+    g_down = scatter_z(g_down)
 
     d_inner = back_cols(d_out_all, w_down_own)
     d_gate = short(d_inner * up_pre * sigma * (1.0 + gate_pre * (1.0 - sigma)))
     d_up = short(d_inner * gate_pre * sigma)
     d_both = jnp.concatenate([d_gate, d_up], 1)
-
-    def owned_hidden(columns):
-        rows = jnp.concatenate([columns[:, :own_ff], columns[:, wide : wide + own_ff]], 1)
-        rows = scatter_z(rows)
-        rows = rows.reshape(2, 2, 2, rows_in, -1)
-        rows = trade(rows, "y", 0, 0)
-        rows = trade(rows, "pair", 2, 2)
-        rows = trade(rows, "core", 1, 1)
-        def natural(part):
-            part = part.reshape(2, 2, 2, rows_in, depth, ff_rows).transpose(3, 4, 0, 1, 2, 5)
-            return long(part.reshape(rows_in, hidden))
-        return natural(rows[..., :own_ff]), natural(rows[..., own_ff:])
-
+    d_part = short(back_cols(d_both, gate_up))
+    d_both, d_part = lax.optimization_barrier((d_both, d_part))
     g_both = short(take_rows(hidden2, d_both))
-    d_both, inner, g_both = lax.optimization_barrier((d_both, inner, g_both))
-    g_gate, g_up = owned_hidden(g_both)
-    d_hidden2 = sum_eight(short(back_cols(d_both, gate_up)))
+    inner, g_both = lax.optimization_barrier((inner, g_both))
+    g_both = scatter_z(after(g_both, g_down))
+    g_down = long(g_down[:ff_rows])
+    d_hidden2 = sum_eight(d_part)
     result = resid + sum_eight(short(matmul(inner, w_down_own)))
     activations = undeal(short(result))
 
@@ -682,19 +617,27 @@
     d_qkv = jnp.concatenate(
         [part.reshape(4 * count, -1) for part in (d_query, d_keys, d_values)], 1
     )
+    d_qkv, g_both = lax.optimization_barrier((d_qkv, g_both))
+    d_hidden1 = sum_four(short(back_cols(d_qkv, w_qkv)))
     g_qkv = short(take_rows(hidden1, d_qkv))
     g_qkv = short(owned_rows(g_qkv.reshape(depth, 4, 2, rows_in, -1)))
-    g_qkv = trade(trade(g_qkv.reshape(2, 2, rows_in, -1), "y", 0, 0), "core", 1, 1)
+    g_qkv = spread(g_qkv.reshape(4, rows_in, -1), ("y", "core"))
+    g_both = spread(g_both.reshape(8, rows_in, -1), ("y", "core", "pair"))
+
+    def natural(part):
+        part = part.reshape(8, rows_in, depth, ff_block)[..., :ff_rows].transpose(1, 2, 0, 3)
+        return long(part.reshape(rows_in, hidden))
+
+    g_gate, g_up = natural(g_both[..., :own_ff]), natural(g_both[..., own_ff:])
 
     def all_heads(part, step):
-        part = part.reshape(2, 2, rows_in, depth, step).transpose(2, 3, 0, 1, 4)
+        part = part.reshape(4, rows_in, depth, step).transpose(1, 2, 0, 3)
         return long(part.reshape(rows_in, -1))
 
     g_query = all_heads(g_qkv[..., :own_qk], features)
     g_key = all_heads(g_qkv[..., own_qk : 2 * own_qk], features)
     g_value = all_heads(g_qkv[..., 2 * own_qk :], head_dim)
 
-    d_hidden1 = sum_four(short(back_cols(d_qkv, w_qkv)))
     normed1 = start * scale1
     g_norm = jnp.sum(d_hidden1 * normed1, 0)
     d_start = d_resid + norm_back(d_hidden1, normed1, scale1, gain1)

time: 859 us -> 735 us (0.86)
  waiting for transfers between devices: 375 us -> 320 us
  local copies, waits for them, and re-layouts: 153 us -> 107 us
  other arithmetic: 90.3 us -> 69.7 us
    ppermute x12 -> x6, waiting for transfers between devices: 99.3 us -> 22 us  [from_above(): lax.ppermute(value, 'z', [((i + hops) % size, i) for i in range(size)])]
    all_to_all x2, waiting for transfers between devices: 5.99 us -> 71.3 us  [deal(): dealt = lax.all_to_all(value, GRID, split_axis=2, concat_axis=1, tiled=True)]
    ppermute x52 -> x42, waiting for transfers between devices: 258 us -> 201 us  [swap(): return lax.ppermute(value, axis, SWAP)]
    convert_element_type x15 -> x11, local copies, waits for them, and re-layouts: 26.3 us -> 10.5 us  [long(): return value.astype(jnp.float32)]
    all_to_all x1 -> x5, starting transfers between devices: 4.98 us -> 20.8 us  [spread(): return lax.all_to_all(value, names, split_axis=0, concat_axis=0, tiled=True)]
    ppermute x52 -> x42, starting transfers between devices: 39.4 us -> 25.8 us  [swap(): return lax.ppermute(value, axis, SWAP)]
    slice x3 -> x1, local copies, waits for them, and re-layouts: 12.9 us -> 2.38 us  [on_grid(): g_both[..., own_ff:]]
    concatenate x2 -> x0, local copies, waits for them, and re-layouts: 10.2 us -> none  [the longest x1 9.99 us: on_grid(): jnp.concatenate([gate_up[:, :own_ff], filler, gate_up[:, own_ff:], filler...]
  transfers between devices with their start and end apart: 74 -> 64, of which waited for: 25 -> 30; matrix products, arithmetic and copies ran while one was open for 31% -> 37% of each run, Pallas kernels for 0% -> 0%
where the time goes in v3:
time: 735 us; the launch traced here: 728 us
  waiting for transfers between devices  320 us (44%)
  matrix products  134 us (18%)
  local copies, waits for them, and re-layouts  107 us (15%)
  starting transfers between devices  80.9 us (11%)
  other arithmetic  69.7 us (9%)
  between operations  15.7 us (2%)
    ppermute x42, waiting for transfers between devices, swap(): return lax.ppermute(value, axis, SWAP)  201 us
    all_to_all x2, waiting for transfers between devices, deal(): dealt = lax.all_to_all(value, GRID, split_axis=2, concat_axis=1, tiled=True)  71.3 us
    dot_general x4, matrix products, back_cols(): lax.dot_general(left, right, (((1,), (1,)), ((), ())), preferred_element_...  43.5 us
    unnamed x135, local copies, waits for them, and re-layouts  39.5 us
    dot_general x4, matrix products, take_rows(): lax.dot_general(left, right, (((0,), (0,)), ((), ())), preferred_element_...  38 us
    dot_general x4, matrix products, matmul(): return jnp.dot(left, right, preferred_element_type=jnp.float32)  33.6 us
    ppermute x42, starting transfers between devices, swap(): return lax.ppermute(value, axis, SWAP)  25.8 us
    ppermute x6, waiting for transfers between devices, from_above(): lax.ppermute(value, 'z', [((i + hops) % size, i) for i in range(size)])  22 us
  transfers between devices with their start and end apart: 64, of which 30 were waited for; matrix products, arithmetic and copies ran while one was open for 37% of the time, Pallas kernels for 0%

profile of v3, /device:TPU:16, one launch (start us, length us, event | category | flops | bytes accessed | tf_op | source)
XLA Modules:
  0.0 728.4 jit_solution(1767772263572696777)
XLA Ops:
  14.9 6.7 all-to-all-done
  39.8 37.5 %all-to-all-done.1 = bf16[2,4,32,2048]{3,1,0,2:T(4,128)(2,1)S(1)} async-done(((bf16[2,4,32,2048]{3,1,0,2:T(4,128)(2,1)}), bf16[2,4,32,2048]{3,1,0,2:T(4,128)(2,1)S(1)}, u32[]{:S(2)}, u32[]{:S(2)}) %all-to-all-start.1) | async-done | bytes 1048608 | tf_op jit(solution)/shard_map/all_to_all | solution.py:507
  116.1 24.1 %collective-permute-done.3 = bf16[1024,640]{1,0:T(8,128)(2,1)} collective-permute-done((bf16[1024,640]{1,0:T(8,128)(2,1)}, bf16[1024,640]{1,0:T(8,128)(2,1)}, u32[]{:S(2)}, u32[]{:S(2)}) %collective-permute-start.3) | collective-permute-done | bytes 1310752 | tf_op jit(solution)/shard_map/ppermute | solution.py:341
  143.1 6.0 convolution_convert_fusion.8
  154.6 6.8 all-to-all-start.4
  171.7 33.8 %all-to-all-done.4 = bf16[2,4,32,2048]{3,1,0,2:T(4,128)(2,1)S(1)} async-done(((bf16[2,4,32,2048]{3,1,0,2:T(4,128)(2,1)}), bf16[2,4,32,2048]{3,1,0,2:T(4,128)(2,1)S(1)}, u32[]{:S(2)}, u32[]{:S(2)}) %all-to-all-start.4) | async-done | bytes 1048608 | tf_op jit(solution)/shard_map/all_to_all | solution.py:507
  215.6 19.9 %collective-permute-done.17 = bf16[256,2048]{1,0:T(8,128)(2,1)S(1)} collective-permute-done((bf16[256,2048]{1,0:T(8,128)(2,1)}, bf16[256,2048]{1,0:T(8,128)(2,1)S(1)}, u32[]{:S(2)}, u32[]{:S(2)}) %collective-permute-start.17) | collective-permute-done | bytes 1048608 | tf_op jit(solution)/shard_map/ppermute | solution.py:341
  243.3 26.0 %collective-permute-done.18 = bf16[128,2048]{1,0:T(8,128)(2,1)} collective-permute-done((bf16[128,2048]{1,0:T(8,128)(2,1)}, bf16[128,2048]{1,0:T(8,128)(2,1)}, u32[]{:S(2)}, u32[]{:S(2)}) %collective-permute-start.18) | collective-permute-done | bytes 524320 | tf_op jit(solution)/shard_map/ppermute | solution.py:341
  282.9 18.1 %collective-permute-done.8 = bf16[256,2048]{1,0:T(8,128)(2,1)S(1)} collective-permute-done((bf16[256,2048]{1,0:T(8,128)(2,1)S(1)}, bf16[256,2048]{1,0:T(8,128)(2,1)S(1)}, u32[]{:S(2)}, u32[]{:S(2)}) %collective-permute-start.8) | collective-permute-done | bytes 1048608 | tf_op jit(solution)/shard_map/ppermute | solution.py:341
  308.0 6.3 collective-permute-done.9
  322.4 17.7 %fusion.66 = f32[2048,1536]{0,1:T(8,128)S(1)} fusion(bf16[2048,2048]{1,0:T(8,128)(2,1)} %constant_dynamic-update-slice_fusion, bf16[2048,1536]{1,0:T(8,128)(2,1)} %all-gather.11.cloned.1.call-done), kind=kOutput, calls=%fused_computation.178 | convolution fusion | flops 12884901888 | bytes 27262976 | tf_op jit(solution)/shard_map/dot_general | solution.py:361
  346.4 10.3 %convolution_convert_fusion.5 = bf16[768,2048]{1,0:T(8,128)(2,1)} fusion(bf16[2048,768]{0,1:T(8,128)(2,1)S(1)} %multiply_convert_fusion.2, bf16[2048,2048]{1,0:T(8,128)(2,1)} %constant_dynamic-update-slice_fusion.10), kind=kOutput, calls=%fused_computation.15 | convolution fusion | flops 6444023808 | bytes 14680064 | tf_op jit(solution)/shard_map/dot_general | solution.py:28
  356.8 15.2 %multiply_convert_fusion.1 = (bf16[2048,768]{0,1:T(8,128)(2,1)S(1)}, bf16[2048,768]{0,1:T(8,128)(2,1)S(1)}) fusion(f32[2048,1536]{0,1:T(8,128)} %copy-done.4, bf16[2048,2048]{1,0:T(8,128)(2,1)} %constant_dynamic-update-slice_fusion.10, bf16[768,2048]{1,0:T(8,128)(2,1)} %all-gather.9.cloned.1.call-done), kind=kOutput, calls=%fused_computation.8 | convolution fusion | flops 6462898176 | bytes 30408704 | tf_op jit(solution)/shard_map/dot_general | solution.py:34
  372.0 17.6 %convolution_convert_fusion.1 = bf16[2048,2048]{1,0:T(8,128)(2,1)} fusion(bf16[2048,1536]{1,0:T(8,128)(2,1)} %all-gather.11.cloned.1.call-done, bf16[2048,768]{0,1:T(8,128)(2,1)S(1)} %get-tuple-element.91, bf16[2048,768]{0,1:T(8,128)(2,1)S(1)} %get-tuple-element.90), kind=kOutput, calls=%fused_computation.4 | convolution fusion | flops 12901679104 | bytes 20971520 | tf_op jit(solution)/shard_map/dot_general | solution.py:34
  390.7 17.5 %convolution_convert_fusion.2 = bf16[2048,1536]{1,0:T(8,128)(2,1)} fusion(bf16[2048,2048]{1,0:T(8,128)(2,1)} %constant_dynamic-update-slice_fusion, bf16[2048,1536]{0,1:T(8,128)(2,1)S(1)} %pad_maximum_fusion), kind=kOutput, calls=%fused_computation.5 | convolution fusion | flops 12888047616 | bytes 20971520 | tf_op jit(solution)/shard_map/dot_general | solution.py:28
  413.6 7.5 %convolution_convert_fusion = bf16[2048,2048]{1,0:T(8,128)(2,1)S(1)} fusion(bf16[2048,768]{0,1:T(8,128)(2,1)S(1)} %copy-done.13, bf16[768,2048]{1,0:T(8,128)(2,1)S(1)} %copy-done.47), kind=kOutput, calls=%fused_computation.3 | convolution fusion | flops 6446645248 | bytes 14680064 | tf_op jit(solution)/shard_map/dot_general | solution.py:361
  425.8 5.6 convert_add_fusion
  434.8 9.0 %fusion.54 = (bf16[1024,2048]{1,0:T(8,128)(2,1)S(1)}, f32[1024,2048]{1,0:T(8,128)}) fusion(bf16[1024,2048]{1,0:T(8,128)(2,1)} %collective-permute-done.25, bf16[2048,2048]{1,0:T(8,128)(2,1)} %copy-done.5), kind=kLoop, calls=%fused_computation.172 | loop fusion | flops 8388608 | bytes 20971520 | tf_op jit(solution)/shard_map/convert.35
  451.0 7.8 %collective-permute-done.26 = bf16[128,2048]{1,0:T(8,128)(2,1)S(1)} collective-permute-done((bf16[128,2048]{1,0:T(8,128)(2,1)S(1)}, bf16[128,2048]{1,0:T(8,128)(2,1)S(1)}, u32[]{:S(2)}, u32[]{:S(2)}) %collective-permute-start.26) | collective-permute-done | bytes 524320 | tf_op jit(solution)/shard_map/ppermute | solution.py:341
  464.5 18.1 %collective-permute-done.32 = bf16[256,2048]{1,0:T(8,128)(2,1)S(1)} collective-permute-done((bf16[256,2048]{1,0:T(8,128)(2,1)S(1)}, bf16[256,2048]{1,0:T(8,128)(2,1)S(1)}, u32[]{:S(2)}, u32[]{:S(2)}) %collective-permute-start.32) | collective-permute-done | bytes 1048608 | tf_op jit(solution)/shard_map/ppermute | solution.py:341
  483.5 20.8 %collective-permute-done.27 = bf16[256,2048]{1,0:T(8,128)(2,1)S(1)} collective-permute-done((bf16[256,2048]{1,0:T(8,128)(2,1)S(1)}, bf16[256,2048]{1,0:T(8,128)(2,1)S(1)}, u32[]{:S(2)}, u32[]{:S(2)}) %collective-permute-start.27) | collective-permute-done | bytes 1048608 | tf_op jit(solution)/shard_map/ppermute | solution.py:341
  504.3 5.3 fusion.62
  510.1 24.3 %collective-permute-done.35 = bf16[256,2048]{1,0:T(8,128)(2,1)} collective-permute-done((bf16[256,2048]{1,0:T(8,128)(2,1)}, bf16[256,2048]{1,0:T(8,128)(2,1)}, u32[]{:S(2)}, u32[]{:S(2)}) %collective-permute-start.35) | collective-permute-done | bytes 1048608 | tf_op jit(solution)/shard_map/ppermute | solution.py:341
  536.6 6.5 all-to-all-start.5
  543.1 5.5 convolution_convert_fusion.11
  568.2 5.2 convolution_convert_fusion.3
  576.2 5.7 convolution_convert_fusion.6
  600.6 14.6 %collective-permute-done.40 = bf16[1024,640]{1,0:T(8,128)(2,1)} collective-permute-done((bf16[1024,640]{1,0:T(8,128)(2,1)}, bf16[1024,640]{1,0:T(8,128)(2,1)}, u32[]{:S(2)}, u32[]{:S(2)}) %collective-permute-start.40) | collective-permute-done | bytes 1310752 | tf_op jit(solution)/shard_map/ppermute | solution.py:341
  624.8 12.8 %collective-permute-done.44 = bf16[256,2048]{1,0:T(8,128)(2,1)} collective-permute-done((bf16[256,2048]{1,0:T(8,128)(2,1)}, bf16[256,2048]{1,0:T(8,128)(2,1)}, u32[]{:S(2)}, u32[]{:S(2)}) %collective-permute-start.44) | collective-permute-done | bytes 1048608 | tf_op jit(solution)/shard_map/ppermute | solution.py:341
  644.2 15.0 %collective-permute-done.42 = bf16[256,640]{1,0:T(8,128)(2,1)S(1)} collective-permute-done((bf16[256,640]{1,0:T(8,128)(2,1)S(1)}, bf16[256,640]{1,0:T(8,128)(2,1)S(1)}, u32[]{:S(2)}, u32[]{:S(2)}) %collective-permute-start.42) | collective-permute-done | bytes 327712 | tf_op jit(solution)/shard_map/ppermute | solution.py:345
  671.5 6.0 all-to-all-done.8
  687.3 5.9 all-to-all-start.6
  (375 shorter events, 273.8 us)
Async XLA Ops:
  32.1 45.2 %all-to-all-start.1 = ((bf16[2,4,32,2048]{3,1,0,2:T(4,128)(2,1)}), bf16[2,4,32,2048]{3,1,0,2:T(4,128)(2,1)S(1)}, u32[]{:S(2)}, u32[]{:S(2)}) async-start(bf16[2,4,32,2048]{3,1,0,2:T(4,128)(2,1)} %copy.128), calls=%async_computation.1 | async-start | bytes 2097152 | tf_op jit(solution)/shard_map/all_to_all | solution.py:507
  37.2 46.0 %all-gather.7.cloned.1.call-start = ((), (), s32[]{:S(2)}) async-start(), calls=%async_computation.13 | async-start | bytes 1638400 | tf_op jit(solution)/shard_map/all_gather | solution.py:365
  38.5 123.0 %all-gather.9.cloned.1.call-start = ((), (), s32[]{:S(2)}) async-start(), calls=%async_computation.14 | async-start | bytes 3932160 | tf_op jit(solution)/shard_map/all_gather | solution.py:365
  87.7 52.5 %collective-permute-start.3 = (bf16[1024,640]{1,0:T(8,128)(2,1)}, bf16[1024,640]{1,0:T(8,128)(2,1)}, u32[]{:S(2)}, u32[]{:S(2)}) collective-permute-start(bf16[1024,640]{1,0:T(8,128)(2,1)} %all-gather.7.cloned.1.call-done), channel_id=1, source_target_pairs={{0,1},{1,0},{2,3},{3,2},{4,5},{5,4},{6,7},{7,6},{8,9},{9,8},{10,11... | collective-permute-start | bytes 3932168 | tf_op jit(solution)/shard_map/ppermute | solution.py:341
  102.0 52.5 %all-to-all-start.3 = ((bf16[8,64,1536]{2,1,0:T(8,128)(2,1)}), bf16[8,64,1536]{2,1,0:T(8,128)(2,1)}, u32[]{:S(2)}, u32[]{:S(2)}) async-start(bf16[8,64,1536]{2,1,0:T(8,128)(2,1)} %pad_maximum_fusion.3), calls=%async_computation.3 | async-start | bytes 3145728 | tf_op jit(solution)/shard_map/all_to_all | solution.py:516
  106.7 36.4 %collective-permute-start.1 = (bf16[256,2048]{1,0:T(8,128)(2,1)}, bf16[256,2048]{1,0:T(8,128)(2,1)}, u32[]{:S(2)}, u32[]{:S(2)}) collective-permute-start(bf16[256,2048]{1,0:T(8,128)(2,1)} %multiply_convert_fusion.5), channel_id=1, source_target_pairs={{0,2},{2,0},{1,3},{3,1},{4,6},{6,4},{5,7},{7,5},{8,10},{10,8},{9,1... | collective-permute-start | bytes 3145736 | tf_op jit(solution)/shard_map/ppermute | solution.py:341
  109.7 33.5 %collective-permute-start.2 = (bf16[256,2048]{1,0:T(8,128)(2,1)}, bf16[256,2048]{1,0:T(8,128)(2,1)}, u32[]{:S(2)}, u32[]{:S(2)}) collective-permute-start(bf16[256,2048]{1,0:T(8,128)(2,1)} %collective-permute-done), channel_id=1, source_target_pairs={{0,2},{2,0},{1,3},{3,1},{4,6},{6,4},{5,7},{7,5},{8,10},{10,8},{9,1... | collective-permute-start | bytes 3145736 | tf_op jit(solution)/shard_map/ppermute | solution.py:341
  154.6 50.9 %all-to-all-start.4 = ((bf16[2,4,32,2048]{3,1,0,2:T(4,128)(2,1)}), bf16[2,4,32,2048]{3,1,0,2:T(4,128)(2,1)S(1)}, u32[]{:S(2)}, u32[]{:S(2)}) async-start(bf16[2,4,32,2048]{3,1,0,2:T(4,128)(2,1)} %copy.139), calls=%async_computation.4 | async-start | bytes 2097152 | tf_op jit(solution)/shard_map/all_to_all | solution.py:507
  161.4 161.0 %all-gather.11.cloned.1.call-start = ((), (), s32[]{:S(2)}) async-start(), calls=%async_computation.15 | async-start | bytes 7864320 | tf_op jit(solution)/shard_map/all_gather | solution.py:365
  161.9 263.8 %reduce-scatter.3.cloned.1.call-start = ((), (), s32[]{:S(2)}) async-start(), calls=%async_computation.16 | async-start | bytes 3932160 | tf_op jit(solution)/shard_map/reduce_scatter | solution.py:369
  171.4 39.8 %collective-permute-start.5 = (bf16[512,2048]{1,0:T(8,128)(2,1)}, bf16[512,2048]{1,0:T(8,128)(2,1)}, u32[]{:S(2)}, u32[]{:S(2)}) collective-permute-start(bf16[512,2048]{1,0:T(8,128)(2,1)} %slice.227), channel_id=1, source_target_pairs={{0,2},{2,0},{1,3},{3,1},{4,6},{6,4},{5,7},{7,5},{8,10},{10,8},{9,1... | collective-permute-start | bytes 6291464 | tf_op jit(solution)/shard_map/ppermute | solution.py:341
  214.2 57.0 %collective-permute-start.6 = (bf16[256,2048]{1,0:T(8,128)(2,1)}, bf16[256,2048]{1,0:T(8,128)(2,1)}, u32[]{:S(2)}, u32[]{:S(2)}) collective-permute-start(bf16[256,2048]{1,0:T(8,128)(2,1)} %add_convert_fusion.2), channel_id=1, source_target_pairs={{0,4},{4,0},{1,5},{5,1},{2,6},{6,2},{3,7},{7,3},{8,12},{12,8},{9,1... | collective-permute-start | bytes 3145736 | tf_op jit(solution)/shard_map/ppermute | solution.py:341
  236.3 33.0 %collective-permute-start.18 = (bf16[128,2048]{1,0:T(8,128)(2,1)}, bf16[128,2048]{1,0:T(8,128)(2,1)}, u32[]{:S(2)}, u32[]{:S(2)}) collective-permute-start(bf16[128,2048]{1,0:T(8,128)(2,1)} %slice.236), channel_id=1, source_target_pairs={{0,4},{4,0},{1,5},{5,1},{2,6},{6,2},{3,7},{7,3},{8,12},{12,8},{9,1... | collective-permute-start | bytes 1572872 | tf_op jit(solution)/shard_map/ppermute | solution.py:341
  236.4 41.8 %collective-permute-start.20 = (bf16[256,2048]{1,0:T(8,128)(2,1)}, bf16[256,2048]{1,0:T(8,128)(2,1)S(1)}, u32[]{:S(2)}, u32[]{:S(2)}) collective-permute-start(bf16[256,2048]{1,0:T(8,128)(2,1)} %get-tuple-element.85), channel_id=1, source_target_pairs={{0,2},{2,0},{1,3},{3,1},{4,6},{6,4},{5,7},{7,5},{8,10},{10,8},{9,1... | collective-permute-start | bytes 3145736 | tf_op jit(solution)/shard_map/ppermute | solution.py:341
  238.1 37.5 %collective-permute-start.19 = (bf16[128,2048]{1,0:T(8,128)(2,1)S(1)}, bf16[128,2048]{1,0:T(8,128)(2,1)S(1)}, u32[]{:S(2)}, u32[]{:S(2)}) collective-permute-start(bf16[128,2048]{1,0:T(8,128)(2,1)S(1)} %slice.237), channel_id=1, source_target_pairs={{0,1},{1,0},{2,3},{3,2},{4,5},{5,4},{6,7},{7,6},{8,9},{9,8},{10,11... | collective-permute-start | bytes 1572872 | tf_op jit(solution)/shard_map/ppermute | solution.py:341
  239.8 39.5 %collective-permute-start.21 = (bf16[256,2048]{1,0:T(8,128)(2,1)}, bf16[256,2048]{1,0:T(8,128)(2,1)S(1)}, u32[]{:S(2)}, u32[]{:S(2)}) collective-permute-start(bf16[256,2048]{1,0:T(8,128)(2,1)} %collective-permute-done.16), channel_id=1, source_target_pairs={{0,2},{2,0},{1,3},{3,1},{4,6},{6,4},{5,7},{7,5},{8,10},{10,8},{9,1... | collective-permute-start | bytes 3145736 | tf_op jit(solution)/shard_map/ppermute | solution.py:341
  282.9 34.6 %collective-permute-start.11 = (bf16[256,2048]{1,0:T(8,128)(2,1)S(1)}, bf16[256,2048]{1,0:T(8,128)(2,1)S(1)}, u32[]{:S(2)}, u32[]{:S(2)}) collective-permute-start(bf16[256,2048]{1,0:T(8,128)(2,1)S(1)} %get-tuple-element.87), channel_id=1, source_target_pairs={{0,2},{2,0},{1,3},{3,1},{4,6},{6,4},{5,7},{7,5},{8,10},{10,8},{9,1... | collective-permute-start | bytes 3145736 | tf_op jit(solution)/shard_map/ppermute | solution.py:341
  356.7 210.4 %reduce-scatter.5.cloned.1.call-start = ((), (), s32[]{:S(2)}) async-start(), calls=%async_computation.17 | async-start | bytes 7864320 | tf_op jit(solution)/shard_map/reduce_scatter | solution.py:369
  450.6 32.0 %collective-permute-start.32 = (bf16[256,2048]{1,0:T(8,128)(2,1)S(1)}, bf16[256,2048]{1,0:T(8,128)(2,1)S(1)}, u32[]{:S(2)}, u32[]{:S(2)}) collective-permute-start(bf16[256,2048]{1,0:T(8,128)(2,1)S(1)} %pad_maximum_fusion.7), channel_id=1, source_target_pairs={{0,4},{4,0},{1,5},{5,1},{2,6},{6,2},{3,7},{7,3},{8,12},{12,8},{9,1... | collective-permute-start | bytes 3145736 | tf_op jit(solution)/shard_map/ppermute | solution.py:341
  462.1 42.2 %collective-permute-start.27 = (bf16[256,2048]{1,0:T(8,128)(2,1)S(1)}, bf16[256,2048]{1,0:T(8,128)(2,1)S(1)}, u32[]{:S(2)}, u32[]{:S(2)}) collective-permute-start(bf16[256,2048]{1,0:T(8,128)(2,1)S(1)} %pad_maximum_fusion.5), channel_id=1, source_target_pairs={{0,4},{4,0},{1,5},{5,1},{2,6},{6,2},{3,7},{7,3},{8,12},{12,8},{9,1... | collective-permute-start | bytes 3145736 | tf_op jit(solution)/shard_map/ppermute | solution.py:341
  463.3 41.0 %collective-permute-start.29 = (bf16[256,2048]{1,0:T(8,128)(2,1)S(1)}, bf16[256,2048]{1,0:T(8,128)(2,1)S(1)}, u32[]{:S(2)}, u32[]{:S(2)}) collective-permute-start(bf16[256,2048]{1,0:T(8,128)(2,1)S(1)} %pad_maximum_fusion.6), channel_id=1, source_target_pairs={{0,1},{1,0},{2,3},{3,2},{4,5},{5,4},{6,7},{7,6},{8,9},{9,8},{10,11... | collective-permute-start | bytes 3145736 | tf_op jit(solution)/shard_map/ppermute | solution.py:341
  510.1 33.0 %collective-permute-start.36 = (bf16[256,2048]{1,0:T(8,128)(2,1)}, bf16[256,2048]{1,0:T(8,128)(2,1)}, u32[]{:S(2)}, u32[]{:S(2)}) collective-permute-start(bf16[256,2048]{1,0:T(8,128)(2,1)} %get-tuple-element.82), channel_id=1, source_target_pairs={{0,2},{2,0},{1,3},{3,1},{4,6},{6,4},{5,7},{7,5},{8,10},{10,8},{9,1... | collective-permute-start | bytes 3145736 | tf_op jit(solution)/shard_map/ppermute | solution.py:341
  536.6 56.9 %all-to-all-start.5 = ((bf16[2,128,1,2048]{3,0,2,1:T(2,128)(2,1)}), bf16[2,128,1,2048]{3,0,2,1:T(2,128)(2,1)}, u32[]{:S(2)}, u32[]{:S(2)}) async-start(bf16[2,128,1,2048]{3,0,2,1:T(2,128)(2,1)} %copy.141), calls=%async_computation.5 | async-start | bytes 2097152 | tf_op jit(solution)/shard_map/all_to_all | solution.py:511
  576.1 40.8 %collective-permute-start.38 = (bf16[512,2048]{1,0:T(8,128)(2,1)}, bf16[512,2048]{1,0:T(8,128)(2,1)S(1)}, u32[]{:S(2)}, u32[]{:S(2)}) collective-permute-start(bf16[512,2048]{1,0:T(8,128)(2,1)} %slice.255), channel_id=1, source_target_pairs={{0,2},{2,0},{1,3},{3,1},{4,6},{6,4},{5,7},{7,5},{8,10},{10,8},{9,1... | collective-permute-start | bytes 6291464 | tf_op jit(solution)/shard_map/ppermute | solution.py:341
  591.7 46.0 %collective-permute-start.44 = (bf16[256,2048]{1,0:T(8,128)(2,1)}, bf16[256,2048]{1,0:T(8,128)(2,1)}, u32[]{:S(2)}, u32[]{:S(2)}) collective-permute-start(bf16[256,2048]{1,0:T(8,128)(2,1)} %bitcast.58), channel_id=1, source_target_pairs={{0,1},{1,0},{2,3},{3,2},{4,5},{5,4},{6,7},{7,6},{8,9},{9,8},{10,11... | collective-permute-start | bytes 3145736 | tf_op jit(solution)/shard_map/ppermute | solution.py:341
  596.3 71.0 %all-to-all-start.9 = ((bf16[8,64,1536]{2,1,0:T(8,128)(2,1)}), bf16[8,64,1536]{2,1,0:T(8,128)(2,1)}, u32[]{:S(2)}, u32[]{:S(2)}) async-start(bf16[8,64,1536]{2,1,0:T(8,128)(2,1)} %bitcast.210), calls=%async_computation.11 | async-start | bytes 3145728 | tf_op jit(solution)/shard_map/all_to_all | solution.py:516
  619.3 45.3 %collective-permute-start.39 = (bf16[256,2048]{1,0:T(8,128)(2,1)S(1)}, bf16[256,2048]{1,0:T(8,128)(2,1)S(1)}, u32[]{:S(2)}, u32[]{:S(2)}) collective-permute-start(bf16[256,2048]{1,0:T(8,128)(2,1)S(1)} %add_convert_fusion.1), channel_id=1, source_target_pairs={{0,4},{4,0},{1,5},{5,1},{2,6},{6,2},{3,7},{7,3},{8,12},{12,8},{9,1... | collective-permute-start | bytes 3145736 | tf_op jit(solution)/shard_map/ppermute | solution.py:341
  621.5 37.7 %collective-permute-start.42 = (bf16[256,640]{1,0:T(8,128)(2,1)S(1)}, bf16[256,640]{1,0:T(8,128)(2,1)S(1)}, u32[]{:S(2)}, u32[]{:S(2)}) collective-permute-start(bf16[256,640]{1,0:T(8,128)(2,1)S(1)} %get-tuple-element.115), channel_id=1, source_target_pairs={{16,0},{24,8},{0,16},{8,24},{17,1},{25,9},{1,17},{9,25},{18,2},{26... | collective-permute-start | bytes 983048 | tf_op jit(solution)/shard_map/ppermute | solution.py:345
  624.8 38.9 %collective-permute-start.43 = (bf16[256,640]{1,0:T(8,128)(2,1)S(1)}, bf16[256,640]{1,0:T(8,128)(2,1)S(1)}, u32[]{:S(2)}, u32[]{:S(2)}) collective-permute-start(bf16[256,640]{1,0:T(8,128)(2,1)S(1)} %get-tuple-element.114), channel_id=1, source_target_pairs={{24,0},{0,8},{8,16},{16,24},{25,1},{1,9},{9,17},{17,25},{26,2},{2,... | collective-permute-start | bytes 983048 | tf_op jit(solution)/shard_map/ppermute | solution.py:345
  640.4 52.9 %collective-permute-start.45 = (bf16[64,2048]{1,0:T(8,128)(2,1)}, bf16[64,2048]{1,0:T(8,128)(2,1)}, u32[]{:S(2)}, u32[]{:S(2)}) collective-permute-start(bf16[64,2048]{1,0:T(8,128)(2,1)} %get-tuple-element.118), channel_id=1, source_target_pairs={{8,0},{16,8},{24,16},{0,24},{9,1},{17,9},{25,17},{1,25},{10,2},{18... | collective-permute-start | bytes 786440 | tf_op jit(solution)/shard_map/ppermute | solution.py:345
  643.5 49.7 %collective-permute-start.46 = (bf16[64,2048]{1,0:T(8,128)(2,1)}, bf16[64,2048]{1,0:T(8,128)(2,1)}, u32[]{:S(2)}, u32[]{:S(2)}) collective-permute-start(bf16[64,2048]{1,0:T(8,128)(2,1)} %get-tuple-element.120), channel_id=1, source_target_pairs={{16,0},{24,8},{0,16},{8,24},{17,1},{25,9},{1,17},{9,25},{18,2},{26... | collective-permute-start | bytes 786440 | tf_op jit(solution)/shard_map/ppermute | solution.py:345
  659.2 34.0 %collective-permute-start.47 = (bf16[64,2048]{1,0:T(8,128)(2,1)}, bf16[64,2048]{1,0:T(8,128)(2,1)}, u32[]{:S(2)}, u32[]{:S(2)}) collective-permute-start(bf16[64,2048]{1,0:T(8,128)(2,1)} %get-tuple-element.119), channel_id=1, source_target_pairs={{24,0},{0,8},{8,16},{16,24},{25,1},{1,9},{9,17},{17,25},{26,2},{2,... | collective-permute-start | bytes 786440 | tf_op jit(solution)/shard_map/ppermute | solution.py:345
  (84 other events, 1260.8 us)
Sparse Core Ops, SparseCore 0:
  9.6 28.7 all-gather.4
  40.6 42.5 all-gather.6
  85.3 62.5 all-gather.8
  163.5 122.5 all-gather.10
  356.9 61.2 reduce-scatter.2
  425.9 112.7 reduce-scatter.4

commit v4 on v3

--- a/solution.py
+++ b/solution.py
@@ -424,7 +424,7 @@
     )
 
 
-def attend_back(query, keys, values, lens, grads):
+def attend_back(query, keys, values, lens, grads, result):
     scores, mask, probs, denom = scores_of(query, keys, lens)
     d_probs = jnp.einsum("bihe,bjhe->bhij", grads, values, preferred_element_type=jnp.float32)
     d_values = jnp.einsum(
@@ -432,10 +432,10 @@
     )
     d_kernel = (d_probs - jnp.sum(d_probs * probs, -1, keepdims=True)) / denom
     d_scores = jnp.where(mask, d_kernel * (1.0 + scores), 0.0) * query.shape[-1] ** (-0.5)
-    d_scores = short(d_scores)
+    d_scores, d_values, result = lax.optimization_barrier((short(d_scores), short(d_values), result))
     d_query = jnp.einsum("bhij,bjhe->bihe", d_scores, keys, preferred_element_type=jnp.float32)
     d_keys = jnp.einsum("bhij,bihe->bjhe", d_scores, query, preferred_element_type=jnp.float32)
-    return short(d_query), short(d_keys), short(d_values)
+    return short(d_query), short(d_keys), d_values, result
 
 
 def share_four(mine):
@@ -461,17 +461,32 @@
     return jnp.concatenate(own + near, 0)
 
 
-def sum_eight(partial):
-    count = partial.shape[0] // 8
+def sum_near(partial):
+    half = partial.shape[0] // 2
+    return swap(partial[half:], "core")
+
+
+def sum_far(partial, got):
+    count = got.shape[0] // 4
     half = count // 2
-    got = swap(partial[4 * count :], "core")
-    own = long(partial[: 4 * count]) + long(got)
-    far = short(own[3 * count :])
-    mine, up, across = (own[i * count : (i + 1) * count] for i in range(3))
-    near_a, near_b = swap(far[:half], "y"), swap(far[half:], "pair")
-    across = jnp.concatenate([across[:half] + long(near_a), across[half:]], 0)
-    up = jnp.concatenate([up[:half], up[half:] + long(near_b)], 0)
-    return mine + long(swap(short(up), "y")) + long(swap(short(across), "pair"))
+    far = short(long(partial[3 * count : 4 * count]) + long(got[3 * count :]))
+    return swap(far[:half], "y"), swap(far[half:], "pair")
+
+
+def sum_last(partial, got, near_a, near_b):
+    count = got.shape[0] // 4
+    half = count // 2
+
+    def own(start, stop):
+        return long(partial[start:stop]) + long(got[start:stop])
+
+    up = jnp.concatenate(
+        [short(own(count, count + half)), short(own(count + half, 2 * count) + long(near_b))], 0
+    )
+    across = jnp.concatenate(
+        [short(own(2 * count, 2 * count + half) + long(near_a)), short(own(2 * count + half, 3 * count))], 0
+    )
+    return own(0, count) + long(swap(up, "y")) + long(swap(across, "pair"))
 
 
 def on_grid(
@@ -522,24 +537,26 @@
         ],
         2,
     )
+    own_qkv = qkv.shape[2]
+    gains = jnp.pad(jnp.stack([norm_gain, mlp_gain], 1), ((0, 0), (0, LANES - 2)))
+    qkv = jnp.concatenate([qkv, jnp.broadcast_to(gains[None], (4, rows_in, LANES))], 2)
     qkv = spread(qkv, ("y", "core"))
     start_rows = deal(after(tokens, qkv))
-    gains = jnp.stack([norm_gain, mlp_gain])
-    gains = spread(jnp.broadcast_to(gains[None], (seqs,) + gains.shape), GRID)
-    gains = long(gains.transpose(1, 0, 2).reshape(2, 1, width))
-    gain1, gain2 = gains[0], gains[1]
-
     def hidden_block(weight):
         cut = weight.reshape(rows_in, depth, 8, ff_rows).transpose(2, 0, 1, 3)
         cut = jnp.pad(cut, ((0, 0), (0, 0), (0, 0), (0, fill)))
         return cut.reshape(8, rows_in, own_ff)
 
     cut = jnp.concatenate([hidden_block(w_gate), hidden_block(w_up)], 2)
-    cut = spread(cut, ("y", "core", "pair"))
+    down_block = jnp.pad(w_down, ((0, fill), (0, 0)))
+    start_rows, cut, down_block = lax.optimization_barrier((start_rows, cut, down_block))
+    start_all = share_four(start_rows)
+    cut = spread(after(cut, start_all), ("y", "core", "pair"))
+    cot_rows = deal(after(cotangent, cut))
 
     out_rows = gather_z(w_out)
-    qkv_rows = gather_z(after(qkv.reshape(4 * rows_in, -1), out_rows))
-    w_down_own = gather_z(after(jnp.pad(w_down, ((0, fill), (0, 0))), qkv_rows))
+    qkv_rows = gather_z(qkv.reshape(4 * rows_in, -1))
+    w_down_own = gather_z(after(down_block, qkv_rows))
     gate_up = gather_z(after(cut.reshape(8 * rows_in, 2 * own_ff), w_down_own))
 
     def joined(mine, shape, axis):
@@ -557,25 +574,29 @@
     lens = jnp.concatenate(
         [lens_of(device_index), lens_of(device_index + by_y), lens_of(by_core), lens_of(by_core + by_y)]
     )
-    start = long(start_rows)
+    gains = long(w_qkv[:, own_qkv:].T)
+    gain1, gain2 = gains[0:1], gains[1:2]
+    start = long(start_all)
     scale1 = row_norm(start)
-    hidden1 = share_four(short(start * scale1 * gain1))
-    cot_rows = deal(after(cotangent, hidden1))
-    live = (
-        lax.broadcasted_iota(jnp.int32, (batches, seq_len), 1) < lens[:batches, None]
-    ).reshape(count, 1)
-    d_out = jnp.where(live, cot_rows, jnp.zeros_like(cot_rows))
-    d_out_all = share_eight(d_out)
+    hidden1 = short(start * scale1 * gain1)
+    start, scale1 = start[:count], scale1[:count]
     qkv = short(matmul(hidden1, w_qkv))
     by_seq = (4 * batches, seq_len, own_heads, -1)
     query = qkv[:, :own_qk].reshape(by_seq)
     keys = qkv[:, own_qk : 2 * own_qk].reshape(by_seq)
-    values = qkv[:, 2 * own_qk :].reshape(by_seq)
+    values = qkv[:, 2 * own_qk : own_qkv].reshape(by_seq)
     attended = attend(query, keys, values, lens).reshape(4 * count, -1)
+    attended, cut_done = lax.optimization_barrier((attended, cut))
     resid = start + sum_four(short(matmul(attended, w_out_own)))
     scale2 = row_norm(resid)
     normed2 = resid * scale2
     hidden2 = share_eight(short(normed2 * gain2))
+    live = (
+        lax.broadcasted_iota(jnp.int32, (batches, seq_len), 1) < lens[:batches, None]
+    ).reshape(count, 1)
+    cot_rows = after(cot_rows, hidden2)
+    d_out = jnp.where(live, cot_rows, jnp.zeros_like(cot_rows))
+    d_out_all = share_eight(d_out)
 
     both_pre = matmul(hidden2, gate_up)
     gate_pre, up_pre = both_pre[:, :own_ff], both_pre[:, own_ff:]
@@ -591,38 +612,63 @@
     d_both = jnp.concatenate([d_gate, d_up], 1)
     d_part = short(back_cols(d_both, gate_up))
     d_both, d_part = lax.optimization_barrier((d_both, d_part))
+    got = sum_near(d_part)
     g_both = short(take_rows(hidden2, d_both))
-    inner, g_both = lax.optimization_barrier((inner, g_both))
-    g_both = scatter_z(after(g_both, g_down))
+    inner, got, g_both, g_down = lax.optimization_barrier((inner, got, g_both, g_down))
+    g_both = scatter_z(g_both)
     g_down = long(g_down[:ff_rows])
-    d_hidden2 = sum_eight(d_part)
-    result = resid + sum_eight(short(matmul(inner, w_down_own)))
-    activations = undeal(short(result))
-
+    d_hidden2 = sum_last(d_part, got, *sum_far(d_part, got))
+    result_part = short(matmul(inner, w_down_own))
+    result_got = sum_near(result_part)
     g_mlp = jnp.sum(d_hidden2 * normed2, 0)
     d_resid = long(d_out) + norm_back(d_hidden2, normed2, scale2, gain2)
     d_branch = share_four(short(d_resid))
     d_attended = short(back_cols(d_branch, w_out_own))
-
-    def owned_rows(partial):
-        kept, sent = halves(partial, pair, 2)
-        got = swap(sent.reshape(-1, sent.shape[-1]), "pair").reshape(kept.shape)
-        rows = short(long(kept) + long(got))
-        return reduce_z(rows.reshape(depth, -1, rows.shape[-1]), depth)
-
+    d_attended, result_got = lax.optimization_barrier((d_attended, result_got))
+    result_far = sum_far(result_part, result_got)
     g_out = short(take_rows(attended, d_branch))
-    g_out = owned_rows(g_out.reshape(depth, 1, 2, rows_in, width))
-
-    d_query, d_keys, d_values = attend_back(query, keys, values, lens, d_attended.reshape(by_seq))
+    d_attended, g_out, result_far = lax.optimization_barrier((d_attended, g_out, result_far))
+    result = short(resid + sum_last(result_part, result_got, *result_far))
+
+    def send_over_x(partial):
+        kept, sent = halves(partial, pair, 1)
+        return kept, swap(sent.reshape(-1, sent.shape[-1]), "pair")
+
+    def add_over_x(kept, got):
+        total = short(long(kept) + long(got.reshape(kept.shape)))
+        return total.reshape(depth, -1, kept.shape[-1])
+
+    g_out = add_over_x(*send_over_x(g_out.reshape(depth, 2, rows_in, width)))
+
+    d_query, d_keys, d_values, result = attend_back(
+        query, keys, values, lens, d_attended.reshape(by_seq), result
+    )
     d_qkv = jnp.concatenate(
         [part.reshape(4 * count, -1) for part in (d_query, d_keys, d_values)], 1
     )
-    d_qkv, g_both = lax.optimization_barrier((d_qkv, g_both))
-    d_hidden1 = sum_four(short(back_cols(d_qkv, w_qkv)))
-    g_qkv = short(take_rows(hidden1, d_qkv))
-    g_qkv = short(owned_rows(g_qkv.reshape(depth, 4, 2, rows_in, -1)))
-    g_qkv = spread(g_qkv.reshape(4, rows_in, -1), ("y", "core"))
+    d_part = short(back_cols(jnp.pad(d_qkv, ((0, 0), (0, LANES))), w_qkv))
+    d_qkv, d_part, g_both, g_out = lax.optimization_barrier((d_qkv, d_part, g_both, g_out))
+    d_hidden1 = sum_four(d_part)
+    g_qkv = short(take_rows(hidden1, d_qkv)).reshape(4 * depth, 2, rows_in, -1)
+    kept, got = send_over_x(g_qkv)
     g_both = spread(g_both.reshape(8, rows_in, -1), ("y", "core", "pair"))
+    activations = undeal(after(result, g_both))
+    normed1 = start * scale1
+    g_norm = jnp.sum(d_hidden1 * normed1, 0)
+    d_start = short(d_resid + norm_back(d_hidden1, normed1, scale1, gain1))
+    got, d_start = lax.optimization_barrier((got, d_start))
+    input_grad = undeal(after(d_start, activations))
+    g_qkv = short(reduce_z(add_over_x(kept, got), depth))
+    g_out = reduce_z(g_out, depth)
+
+    def trade(value, name, axis):
+        index = lax.axis_index(name)
+        kept, sent = halves(value, index, axis)
+        got = swap(sent.reshape(-1, sent.shape[-1]), name).reshape(kept.shape)
+        return both(kept, got, index, axis)
+
+    g_qkv = trade(trade(g_qkv.reshape(2, 2, rows_in, -1), "core", 1), "y", 0)
+    g_qkv = g_qkv.reshape(4, rows_in, -1)
 
     def natural(part):
         part = part.reshape(8, rows_in, depth, ff_block)[..., :ff_rows].transpose(1, 2, 0, 3)
@@ -638,15 +684,14 @@
     g_key = all_heads(g_qkv[..., own_qk : 2 * own_qk], features)
     g_value = all_heads(g_qkv[..., 2 * own_qk :], head_dim)
 
-    normed1 = start * scale1
-    g_norm = jnp.sum(d_hidden1 * normed1, 0)
-    d_start = d_resid + norm_back(d_hidden1, normed1, scale1, gain1)
-    input_grad = undeal(short(d_start))
-
-    g_gains = jnp.stack([g_norm, g_mlp]).reshape(2, seqs, rows_in).transpose(1, 0, 2)
-    g_gains = jnp.sum(
-        lax.all_to_all(g_gains, GRID, split_axis=0, concat_axis=0, tiled=True), 0
-    )
+    def swap_sum(partial, name, axis):
+        kept, sent = halves(partial, lax.axis_index(name), axis)
+        return kept + swap(sent, name)
+
+    g_gains = jnp.stack([g_norm, g_mlp]).reshape(2, depth, 2, 2, 2, rows_in)
+    for name, axis in (("y", 2), ("core", 2), ("pair", 2)):
+        g_gains = swap_sum(g_gains, name, axis)
+    g_gains = reduce_z(g_gains.transpose(1, 0, 2), depth)
     return (
         activations,
         input_grad,

time: 735 us -> 725 us (0.986)
  waiting for transfers between devices: 320 us -> 285 us
  local copies, waits for them, and re-layouts: 107 us -> 119 us
  blocking collectives: 0 us -> 10.6 us
  starting transfers between devices: 80.9 us -> 72.5 us
  other arithmetic: 69.7 us -> 77.6 us
    all_to_all x2, waiting for transfers between devices: 71.3 us -> 14.2 us  [deal(): dealt = lax.all_to_all(value, GRID, split_axis=2, concat_axis=1, tiled=True)]
    all_gather x4, waiting for transfers between devices: 3.43 us -> 23.6 us  [gather_z(): return lax.all_gather(block, 'z', axis=0, tiled=True)]
    all_to_all x5 -> x2, starting transfers between devices: 20.8 us -> 7.95 us  [spread(): return lax.all_to_all(value, names, split_axis=0, concat_axis=0, tiled=True)]
    another operation x4 -> x1, other arithmetic: 12.4 us -> 0.68 us  [on_grid(): jnp.stack([norm_gain, mlp_gain], 1)]
    convert_element_type x9 -> x13, other arithmetic: 21.6 us -> 33 us  [short(): return value.astype(jnp.bfloat16)]
    convert_element_type x7 -> x8, other arithmetic: 4.05 us -> 15.5 us  [long(): return value.astype(jnp.float32)]
    all_to_all x0 -> x1, blocking collectives: none -> 10.6 us  [spread(): return lax.all_to_all(value, names, split_axis=0, concat_axis=0, tiled=True)]
    ppermute x6 -> x9, waiting for transfers between devices: 22 us -> 32.2 us  [from_above(): lax.ppermute(value, 'z', [((i + hops) % size, i) for i in range(size)])]
  transfers between devices with their start and end apart: 64 -> 68, of which waited for: 30 -> 31; matrix products, arithmetic and copies ran while one was open for 37% -> 39% of each run, Pallas kernels for 0% -> 0%
where the time goes in v4:
time: 725 us; the launch traced here: 713 us
  waiting for transfers between devices  285 us (39%)
  matrix products  134 us (18%)
  local copies, waits for them, and re-layouts  119 us (16%)
  other arithmetic  77.6 us (11%)
  starting transfers between devices  72.5 us (10%)
  between operations  15.5 us (2%)
  blocking collectives  10.6 us (1%)
    ppermute x47, waiting for transfers between devices, swap(): return lax.ppermute(value, axis, SWAP)  205 us
    unnamed x147, local copies, waits for them, and re-layouts  48.3 us
    dot_general x4, matrix products, back_cols(): lax.dot_general(left, right, (((1,), (1,)), ((), ())), preferred_element_...  46 us
    dot_general x4, matrix products, take_rows(): lax.dot_general(left, right, (((0,), (0,)), ((), ())), preferred_element_...  39 us
    dot_general x4, matrix products, matmul(): return jnp.dot(left, right, preferred_element_type=jnp.float32)  36.5 us
    convert_element_type x13, other arithmetic, short(): return value.astype(jnp.bfloat16)  33 us
    ppermute x9, waiting for transfers between devices, from_above(): lax.ppermute(value, 'z', [((i + hops) % size, i) for i in range(size)])  32.2 us
    ppermute x47, starting transfers between devices, swap(): return lax.ppermute(value, axis, SWAP)  30.6 us
  transfers between devices with their start and end apart: 68, of which 31 were waited for; matrix products, arithmetic and copies ran while one was open for 39% of the time, Pallas kernels for 0%

profile of v4, /device:TPU:16, one launch (start us, length us, event | category | flops | bytes accessed | tf_op | source)
XLA Modules:
  0.0 713.4 jit_solution(16691059020008355219)
XLA Ops:
  12.3 10.6 %all_to_all.81 = bf16[4,64,768]{2,1,0:T(8,128)(2,1)} all-to-all(bf16[4,64,768]{2,1,0:T(8,128)(2,1)S(1)} %pad_maximum_fusion.9), channel_id=1, replica_groups=mesh['z'=4,'y'=2,'core'=2,'pair'=2] {'y','core'}, dimensions={0} | all-to-all | bytes 786432 | tf_op jit(solution)/shard_map/all_to_all | solution.py:531
  47.5 14.2 %all-to-all-done.1 = bf16[2,4,32,2048]{3,1,0,2:T(4,128)(2,1)S(1)} async-done(((bf16[2,4,32,2048]{3,1,0,2:T(4,128)(2,1)}), bf16[2,4,32,2048]{3,1,0,2:T(4,128)(2,1)S(1)}, u32[]{:S(2)}, u32[]{:S(2)}) %all-to-all-start.1) | async-done | bytes 1048608 | tf_op jit(solution)/shard_map/all_to_all | solution.py:522
  63.1 21.6 %all-gather.5.cloned.1.call-done = bf16[1024,768]{1,0:T(8,128)(2,1)} async-done(((bf16[256,768]{1,0:T(8,128)(2,1)}), bf16[1024,768]{1,0:T(8,128)(2,1)}) %all-gather.5.cloned.1.call-update) | async-done | bytes 1572880 | tf_op jit(solution)/shard_map/all_gather | solution.py:365
  96.3 24.8 %collective-permute-done.3 = bf16[1024,768]{1,0:T(8,128)(2,1)} collective-permute-done((bf16[1024,768]{1,0:T(8,128)(2,1)}, bf16[1024,768]{1,0:T(8,128)(2,1)}, u32[]{:S(2)}, u32[]{:S(2)}) %collective-permute-start.3) | collective-permute-done | bytes 1572896 | tf_op jit(solution)/shard_map/ppermute | solution.py:341
  132.2 7.0 convolution_convert_fusion.8
  144.2 8.0 %all-to-all-done.2 = bf16[8,64,1536]{2,1,0:T(8,128)(2,1)S(1)} async-done(((bf16[8,64,1536]{2,1,0:T(8,128)(2,1)}), bf16[8,64,1536]{2,1,0:T(8,128)(2,1)S(1)}, u32[]{:S(2)}, u32[]{:S(2)}) %all-to-all-start.2) | async-done | bytes 1572896 | tf_op jit(solution)/shard_map/all_to_all | solution.py:531
  163.4 6.6 convert_element_type.391
  171.8 5.9 all-to-all-start.3
  178.0 15.7 %collective-permute-done.6 = bf16[256,2048]{1,0:T(8,128)(2,1)} collective-permute-done((bf16[256,2048]{1,0:T(8,128)(2,1)}, bf16[256,2048]{1,0:T(8,128)(2,1)}, u32[]{:S(2)}, u32[]{:S(2)}) %collective-permute-start.6) | collective-permute-done | bytes 1048608 | tf_op jit(solution)/shard_map/ppermute | solution.py:341
  199.5 25.8 %collective-permute-done.8 = bf16[256,2048]{1,0:T(8,128)(2,1)S(1)} collective-permute-done((bf16[256,2048]{1,0:T(8,128)(2,1)}, bf16[256,2048]{1,0:T(8,128)(2,1)S(1)}, u32[]{:S(2)}, u32[]{:S(2)}) %collective-permute-start.8) | collective-permute-done | bytes 1048608 | tf_op jit(solution)/shard_map/ppermute | solution.py:341
  254.2 24.9 %collective-permute-done.17 = bf16[256,2048]{1,0:T(8,128)(2,1)S(1)} collective-permute-done((bf16[256,2048]{1,0:T(8,128)(2,1)S(1)}, bf16[256,2048]{1,0:T(8,128)(2,1)S(1)}, u32[]{:S(2)}, u32[]{:S(2)}) %collective-permute-start.17) | collective-permute-done | bytes 1048608 | tf_op jit(solution)/shard_map/ppermute | solution.py:341
  283.6 9.3 %collective-permute-done.18 = bf16[128,2048]{1,0:T(8,128)(2,1)S(1)} collective-permute-done((bf16[128,2048]{1,0:T(8,128)(2,1)S(1)}, bf16[128,2048]{1,0:T(8,128)(2,1)S(1)}, u32[]{:S(2)}, u32[]{:S(2)}) %collective-permute-start.18) | collective-permute-done | bytes 524320 | tf_op jit(solution)/shard_map/ppermute | solution.py:341
  299.9 17.7 %fusion.43 = f32[2048,1536]{0,1:T(8,128)S(1)} fusion(bf16[2048,2048]{1,0:T(8,128)(2,1)} %constant_dynamic-update-slice_fusion.4, bf16[2048,1536]{1,0:T(8,128)(2,1)} %all-gather.11.cloned.1.call-done), kind=kOutput, calls=%fused_computation.186 | convolution fusion | flops 12884901888 | bytes 27262976 | tf_op jit(solution)/shard_map/dot_general | solution.py:361
  323.9 10.3 %convolution_convert_fusion.5 = bf16[768,2048]{1,0:T(8,128)(2,1)} fusion(bf16[2048,768]{0,1:T(8,128)(2,1)S(1)} %multiply_convert_fusion.3, bf16[2048,2048]{1,0:T(8,128)(2,1)} %constant_dynamic-update-slice_fusion.14), kind=kOutput, calls=%fused_computation.14 | convolution fusion | flops 6444023808 | bytes 14680064 | tf_op jit(solution)/shard_map/dot_general | solution.py:28
  336.1 15.3 %multiply_convert_fusion.2 = (bf16[2048,768]{0,1:T(8,128)(2,1)S(1)}, bf16[2048,768]{0,1:T(8,128)(2,1)}) fusion(f32[2048,1536]{0,1:T(8,128)} %copy-done.6, bf16[2048,2048]{1,0:T(8,128)(2,1)} %constant_dynamic-update-slice_fusion.14, bf16[768,2048]{1,0:T(8,128)(2,1)S(1)} %copy-done.50), kind=kOutput, calls=%fused_computation.8 | convolution fusion | flops 6462898176 | bytes 30408704 | tf_op jit(solution)/shard_map/dot_general | solution.py:34
  355.5 19.4 %convolution_convert_fusion.1 = bf16[2048,2048]{1,0:T(8,128)(2,1)} fusion(bf16[2048,1536]{1,0:T(8,128)(2,1)} %all-gather.11.cloned.1.call-done, bf16[2048,768]{0,1:T(8,128)(2,1)} %get-tuple-element.143, bf16[2048,768]{0,1:T(8,128)(2,1)} %copy-done.18), kind=kOutput, calls=%fused_computation.4 | convolution fusion | flops 12901679104 | bytes 20971520 | tf_op jit(solution)/shard_map/dot_general | solution.py:34
  379.7 17.8 %convolution_convert_fusion.2 = bf16[2048,1536]{1,0:T(8,128)(2,1)} fusion(bf16[2048,2048]{1,0:T(8,128)(2,1)} %constant_dynamic-update-slice_fusion.4, bf16[2048,1536]{0,1:T(8,128)(2,1)S(1)} %pad_maximum_fusion), kind=kOutput, calls=%fused_computation.5 | convolution fusion | flops 12888047616 | bytes 20971520 | tf_op jit(solution)/shard_map/dot_general | solution.py:28
  401.6 12.4 %collective-permute-done.26 = bf16[128,2048]{1,0:T(8,128)(2,1)S(1)} collective-permute-done((bf16[128,2048]{1,0:T(8,128)(2,1)S(1)}, bf16[128,2048]{1,0:T(8,128)(2,1)S(1)}, u32[]{:S(2)}, u32[]{:S(2)}) %collective-permute-start.26) | collective-permute-done | bytes 524320 | tf_op jit(solution)/shard_map/ppermute | solution.py:341
  420.7 7.2 %convolution_convert_fusion = bf16[2048,2048]{1,0:T(8,128)(2,1)S(1)} fusion(bf16[2048,768]{0,1:T(8,128)(2,1)S(1)} %copy-done.20, bf16[768,2048]{1,0:T(8,128)(2,1)S(1)} %copy-done.51), kind=kOutput, calls=%fused_computation.3 | convolution fusion | flops 6446645248 | bytes 14680064 | tf_op jit(solution)/shard_map/dot_general | solution.py:361
  432.8 9.6 %collective-permute-done.27 = bf16[256,2048]{1,0:T(8,128)(2,1)S(1)} collective-permute-done((bf16[256,2048]{1,0:T(8,128)(2,1)S(1)}, bf16[256,2048]{1,0:T(8,128)(2,1)S(1)}, u32[]{:S(2)}, u32[]{:S(2)}) %collective-permute-start.27) | collective-permute-done | bytes 1048608 | tf_op jit(solution)/shard_map/ppermute | solution.py:341
  448.5 22.4 %collective-permute-done.30 = bf16[256,2048]{1,0:T(8,128)(2,1)} collective-permute-done((bf16[256,2048]{1,0:T(8,128)(2,1)}, bf16[256,2048]{1,0:T(8,128)(2,1)}, u32[]{:S(2)}, u32[]{:S(2)}) %collective-permute-start.30) | collective-permute-done | bytes 1048608 | tf_op jit(solution)/shard_map/ppermute | solution.py:341
  473.9 6.3 convolution_convert_fusion.11
  489.7 6.7 collective-permute-done.34
  514.9 5.8 multiply_convert_fusion.4
  520.7 7.7 %collective-permute-done.36 = bf16[256,2048]{1,0:T(8,128)(2,1)} collective-permute-done((bf16[256,2048]{1,0:T(8,128)(2,1)}, bf16[256,2048]{1,0:T(8,128)(2,1)}, u32[]{:S(2)}, u32[]{:S(2)}) %collective-permute-start.36) | collective-permute-done | bytes 1048608 | tf_op jit(solution)/shard_map/ppermute | solution.py:341
  528.4 17.0 %collective-permute-done.37 = bf16[256,2048]{1,0:T(8,128)(2,1)} collective-permute-done((bf16[256,2048]{1,0:T(8,128)(2,1)}, bf16[256,2048]{1,0:T(8,128)(2,1)}, u32[]{:S(2)}, u32[]{:S(2)}) %collective-permute-start.37) | collective-permute-done | bytes 1048608 | tf_op jit(solution)/shard_map/ppermute | solution.py:341
  555.4 5.2 convolution_convert_fusion.4
  577.5 6.4 convolution_convert_fusion.6
  619.4 8.9 %collective-permute-done.41 = bf16[256,2048]{1,0:T(8,128)(2,1)} collective-permute-done((bf16[256,2048]{1,0:T(8,128)(2,1)}, bf16[256,2048]{1,0:T(8,128)(2,1)}, u32[]{:S(2)}, u32[]{:S(2)}) %collective-permute-start.41) | collective-permute-done | bytes 1048608 | tf_op jit(solution)/shard_map/ppermute | solution.py:341
  665.0 14.1 %collective-permute-done.49 = bf16[256,640]{1,0:T(8,128)(2,1)} collective-permute-done((bf16[256,640]{1,0:T(8,128)(2,1)}, bf16[256,640]{1,0:T(8,128)(2,1)}, u32[]{:S(2)}, u32[]{:S(2)}) %collective-permute-start.49) | collective-permute-done | bytes 327712 | tf_op jit(solution)/shard_map/ppermute | solution.py:345
  679.2 5.0 collective-permute-done.50
  685.7 9.6 %collective-permute-done.47 = f32[2,64]{1,0:T(2,128)S(1)} collective-permute-done((f32[2,64]{1,0:T(2,128)S(1)}, f32[2,64]{1,0:T(2,128)S(1)}, u32[]{:S(2)}, u32[]{:S(2)}) %collective-permute-start.47) | collective-permute-done | bytes 544 | tf_op jit(solution)/shard_map/ppermute | solution.py:345
  (403 shorter events, 298.7 us)
Async XLA Ops:
  7.2 36.5 %all-gather.7.cloned.1.call-start = ((), (), s32[]{:S(2)}) async-start(), calls=%async_computation.10 | async-start | bytes 1310720 | tf_op jit(solution)/shard_map/all_gather | solution.py:365
  7.9 76.7 %all-gather.5.cloned.1.call-start = ((), (), s32[]{:S(2)}) async-start(), calls=%async_computation.9 | async-start | bytes 1966080 | tf_op jit(solution)/shard_map/all_gather | solution.py:365
  24.7 37.0 %all-to-all-start.1 = ((bf16[2,4,32,2048]{3,1,0,2:T(4,128)(2,1)}), bf16[2,4,32,2048]{3,1,0,2:T(4,128)(2,1)S(1)}, u32[]{:S(2)}, u32[]{:S(2)}) async-start(bf16[2,4,32,2048]{3,1,0,2:T(4,128)(2,1)} %copy.178), calls=%async_computation.1 | async-start | bytes 2097152 | tf_op jit(solution)/shard_map/all_to_all | solution.py:522
  29.7 133.7 %all-gather.9.cloned.1.call-start = ((), (), s32[]{:S(2)}) async-start(), calls=%async_computation.11 | async-start | bytes 3932160 | tf_op jit(solution)/shard_map/all_gather | solution.py:365
  43.6 44.0 %collective-permute-start.4 = (bf16[256,2048]{1,0:T(8,128)(2,1)}, bf16[256,2048]{1,0:T(8,128)(2,1)}, u32[]{:S(2)}, u32[]{:S(2)}) collective-permute-start(bf16[256,2048]{1,0:T(8,128)(2,1)} %all-gather.7.cloned.1.call-done), channel_id=1, source_target_pairs={{0,1},{1,0},{2,3},{3,2},{4,5},{5,4},{6,7},{7,6},{8,9},{9,8},{10,11... | collective-permute-start | bytes 3145736 | tf_op jit(solution)/shard_map/ppermute | solution.py:341
  62.6 28.5 %collective-permute-start = (bf16[256,2048]{1,0:T(8,128)(2,1)S(1)}, bf16[256,2048]{1,0:T(8,128)(2,1)}, u32[]{:S(2)}, u32[]{:S(2)}) collective-permute-start(bf16[256,2048]{1,0:T(8,128)(2,1)S(1)} %reshape.275), channel_id=1, source_target_pairs={{0,4},{4,0},{1,5},{5,1},{2,6},{6,2},{3,7},{7,3},{8,12},{12,8},{9,1... | collective-permute-start | bytes 3145736 | tf_op jit(solution)/shard_map/ppermute | solution.py:341
  84.7 36.5 %collective-permute-start.3 = (bf16[1024,768]{1,0:T(8,128)(2,1)}, bf16[1024,768]{1,0:T(8,128)(2,1)}, u32[]{:S(2)}, u32[]{:S(2)}) collective-permute-start(bf16[1024,768]{1,0:T(8,128)(2,1)} %all-gather.5.cloned.1.call-done), channel_id=1, source_target_pairs={{0,1},{1,0},{2,3},{3,2},{4,5},{5,4},{6,7},{7,6},{8,9},{9,8},{10,11... | collective-permute-start | bytes 4718600 | tf_op jit(solution)/shard_map/ppermute | solution.py:341
  91.1 33.9 %collective-permute-start.2 = (bf16[256,2048]{1,0:T(8,128)(2,1)}, bf16[256,2048]{1,0:T(8,128)(2,1)S(1)}, u32[]{:S(2)}, u32[]{:S(2)}) collective-permute-start(bf16[256,2048]{1,0:T(8,128)(2,1)} %collective-permute-done), channel_id=1, source_target_pairs={{0,2},{2,0},{1,3},{3,1},{4,6},{6,4},{5,7},{7,5},{8,10},{10,8},{9,1... | collective-permute-start | bytes 3145736 | tf_op jit(solution)/shard_map/ppermute | solution.py:341
  131.6 168.3 %all-gather.11.cloned.1.call-start = ((), (), s32[]{:S(2)}) async-start(), calls=%async_computation.12 | async-start | bytes 7864320 | tf_op jit(solution)/shard_map/all_gather | solution.py:365
  162.5 31.2 %collective-permute-start.6 = (bf16[256,2048]{1,0:T(8,128)(2,1)}, bf16[256,2048]{1,0:T(8,128)(2,1)}, u32[]{:S(2)}, u32[]{:S(2)}) collective-permute-start(bf16[256,2048]{1,0:T(8,128)(2,1)} %add_convert_fusion.5), channel_id=1, source_target_pairs={{0,4},{4,0},{1,5},{5,1},{2,6},{6,2},{3,7},{7,3},{8,12},{12,8},{9,1... | collective-permute-start | bytes 3145736 | tf_op jit(solution)/shard_map/ppermute | solution.py:341
  171.8 58.3 %all-to-all-start.3 = ((bf16[2,4,32,2048]{3,1,0,2:T(4,128)(2,1)}), bf16[2,4,32,2048]{3,1,0,2:T(4,128)(2,1)S(1)}, u32[]{:S(2)}, u32[]{:S(2)}) async-start(bf16[2,4,32,2048]{3,1,0,2:T(4,128)(2,1)} %copy.182), calls=%async_computation.3 | async-start | bytes 2097152 | tf_op jit(solution)/shard_map/all_to_all | solution.py:522
  177.8 219.8 %reduce-scatter.3.cloned.1.call-start = ((), (), s32[]{:S(2)}) async-start(), calls=%async_computation.13 | async-start | bytes 3932160 | tf_op jit(solution)/shard_map/reduce_scatter | solution.py:369
  198.4 26.8 %collective-permute-start.8 = (bf16[256,2048]{1,0:T(8,128)(2,1)}, bf16[256,2048]{1,0:T(8,128)(2,1)S(1)}, u32[]{:S(2)}, u32[]{:S(2)}) collective-permute-start(bf16[256,2048]{1,0:T(8,128)(2,1)} %get-tuple-element.139), channel_id=1, source_target_pairs={{0,1},{1,0},{2,3},{3,2},{4,5},{5,4},{6,7},{7,6},{8,9},{9,8},{10,11... | collective-permute-start | bytes 3145736 | tf_op jit(solution)/shard_map/ppermute | solution.py:341
  198.4 30.7 %collective-permute-start.7 = (bf16[256,2048]{1,0:T(8,128)(2,1)}, bf16[256,2048]{1,0:T(8,128)(2,1)S(1)}, u32[]{:S(2)}, u32[]{:S(2)}) collective-permute-start(bf16[256,2048]{1,0:T(8,128)(2,1)} %get-tuple-element.139), channel_id=1, source_target_pairs={{0,4},{4,0},{1,5},{5,1},{2,6},{6,2},{3,7},{7,3},{8,12},{12,8},{9,1... | collective-permute-start | bytes 3145736 | tf_op jit(solution)/shard_map/ppermute | solution.py:341
  199.5 46.7 %collective-permute-start.11 = (bf16[256,2048]{1,0:T(8,128)(2,1)}, bf16[256,2048]{1,0:T(8,128)(2,1)}, u32[]{:S(2)}, u32[]{:S(2)}) collective-permute-start(bf16[256,2048]{1,0:T(8,128)(2,1)} %get-tuple-element.139), channel_id=1, source_target_pairs={{0,2},{2,0},{1,3},{3,1},{4,6},{6,4},{5,7},{7,5},{8,10},{10,8},{9,1... | collective-permute-start | bytes 3145736 | tf_op jit(solution)/shard_map/ppermute | solution.py:341
  253.5 25.6 %collective-permute-start.17 = (bf16[256,2048]{1,0:T(8,128)(2,1)S(1)}, bf16[256,2048]{1,0:T(8,128)(2,1)S(1)}, u32[]{:S(2)}, u32[]{:S(2)}) collective-permute-start(bf16[256,2048]{1,0:T(8,128)(2,1)S(1)} %get-tuple-element.137), channel_id=1, source_target_pairs={{0,1},{1,0},{2,3},{3,2},{4,5},{5,4},{6,7},{7,6},{8,9},{9,8},{10,11... | collective-permute-start | bytes 3145736 | tf_op jit(solution)/shard_map/ppermute | solution.py:341
  253.9 25.6 %collective-permute-start.16 = (bf16[256,2048]{1,0:T(8,128)(2,1)S(1)}, bf16[256,2048]{1,0:T(8,128)(2,1)S(1)}, u32[]{:S(2)}, u32[]{:S(2)}) collective-permute-start(bf16[256,2048]{1,0:T(8,128)(2,1)S(1)} %get-tuple-element.137), channel_id=1, source_target_pairs={{0,4},{4,0},{1,5},{5,1},{2,6},{6,2},{3,7},{7,3},{8,12},{12,8},{9,1... | collective-permute-start | bytes 3145736 | tf_op jit(solution)/shard_map/ppermute | solution.py:341
  254.2 40.8 %collective-permute-start.20 = (bf16[256,2048]{1,0:T(8,128)(2,1)S(1)}, bf16[256,2048]{1,0:T(8,128)(2,1)S(1)}, u32[]{:S(2)}, u32[]{:S(2)}) collective-permute-start(bf16[256,2048]{1,0:T(8,128)(2,1)S(1)} %get-tuple-element.137), channel_id=1, source_target_pairs={{0,2},{2,0},{1,3},{3,1},{4,6},{6,4},{5,7},{7,5},{8,10},{10,8},{9,1... | collective-permute-start | bytes 3145736 | tf_op jit(solution)/shard_map/ppermute | solution.py:341
  334.2 226.3 %reduce-scatter.5.cloned.1.call-start = ((), (), s32[]{:S(2)}) async-start(), calls=%async_computation.14 | async-start | bytes 7864320 | tf_op jit(solution)/shard_map/reduce_scatter | solution.py:369
  432.8 47.4 %collective-permute-start.33 = (bf16[1024,2048]{1,0:T(8,128)(2,1)}, bf16[1024,2048]{1,0:T(8,128)(2,1)}, u32[]{:S(2)}, u32[]{:S(2)}) collective-permute-start(bf16[1024,2048]{1,0:T(8,128)(2,1)} %slice.277), channel_id=1, source_target_pairs={{0,2},{2,0},{1,3},{3,1},{4,6},{6,4},{5,7},{7,5},{8,10},{10,8},{9,1... | collective-permute-start | bytes 12582920 | tf_op jit(solution)/shard_map/ppermute | solution.py:341
  498.4 53.2 %collective-permute-start.38 = (bf16[256,2048]{1,0:T(8,128)(2,1)}, bf16[256,2048]{1,0:T(8,128)(2,1)}, u32[]{:S(2)}, u32[]{:S(2)}) collective-permute-start(bf16[256,2048]{1,0:T(8,128)(2,1)} %bitcast.31), channel_id=1, source_target_pairs={{0,1},{1,0},{2,3},{3,2},{4,5},{5,4},{6,7},{7,6},{8,9},{9,8},{10,11... | collective-permute-start | bytes 3145736 | tf_op jit(solution)/shard_map/ppermute | solution.py:341
  505.7 39.7 %collective-permute-start.37 = (bf16[256,2048]{1,0:T(8,128)(2,1)}, bf16[256,2048]{1,0:T(8,128)(2,1)}, u32[]{:S(2)}, u32[]{:S(2)}) collective-permute-start(bf16[256,2048]{1,0:T(8,128)(2,1)} %pad_maximum_fusion.6), channel_id=1, source_target_pairs={{0,1},{1,0},{2,3},{3,2},{4,5},{5,4},{6,7},{7,6},{8,9},{9,8},{10,11... | collective-permute-start | bytes 3145736 | tf_op jit(solution)/shard_map/ppermute | solution.py:341
  573.2 24.8 %all-to-all-start.4 = ((bf16[8,64,1536]{2,1,0:T(8,128)(2,1)}), bf16[8,64,1536]{2,1,0:T(8,128)(2,1)}, u32[]{:S(2)}, u32[]{:S(2)}) async-start(bf16[8,64,1536]{2,1,0:T(8,128)(2,1)} %bitcast.237), calls=%async_computation.6 | async-start | bytes 3145728 | tf_op jit(solution)/shard_map/all_to_all | solution.py:531
  585.7 50.0 %collective-permute-start.39 = (bf16[1024,640]{1,0:T(8,128)(2,1)}, bf16[1024,640]{1,0:T(8,128)(2,1)}, u32[]{:S(2)}, u32[]{:S(2)}) collective-permute-start(bf16[1024,640]{1,0:T(8,128)(2,1)} %bitcast.39), channel_id=1, source_target_pairs={{0,1},{1,0},{2,3},{3,2},{4,5},{5,4},{6,7},{7,6},{8,9},{9,8},{10,11... | collective-permute-start | bytes 3932168 | tf_op jit(solution)/shard_map/ppermute | solution.py:341
  590.5 37.8 %collective-permute-start.41 = (bf16[256,2048]{1,0:T(8,128)(2,1)}, bf16[256,2048]{1,0:T(8,128)(2,1)}, u32[]{:S(2)}, u32[]{:S(2)}) collective-permute-start(bf16[256,2048]{1,0:T(8,128)(2,1)} %add_convert_fusion.1), channel_id=1, source_target_pairs={{0,4},{4,0},{1,5},{5,1},{2,6},{6,2},{3,7},{7,3},{8,12},{12,8},{9,1... | collective-permute-start | bytes 3145736 | tf_op jit(solution)/shard_map/ppermute | solution.py:341
  601.3 56.9 %all-to-all-start.5 = ((bf16[2,128,1,2048]{3,0,2,1:T(2,128)(2,1)}), bf16[2,128,1,2048]{3,0,2,1:T(2,128)(2,1)}, u32[]{:S(2)}, u32[]{:S(2)}) async-start(bf16[2,128,1,2048]{3,0,2,1:T(2,128)(2,1)} %copy.201), calls=%async_computation.7 | async-start | bytes 2097152 | tf_op jit(solution)/shard_map/all_to_all | solution.py:526
  641.0 38.2 %collective-permute-start.49 = (bf16[256,640]{1,0:T(8,128)(2,1)}, bf16[256,640]{1,0:T(8,128)(2,1)}, u32[]{:S(2)}, u32[]{:S(2)}) collective-permute-start(bf16[256,640]{1,0:T(8,128)(2,1)} %get-tuple-element.160), channel_id=1, source_target_pairs={{16,0},{24,8},{0,16},{8,24},{17,1},{25,9},{1,17},{9,25},{18,2},{26... | collective-permute-start | bytes 983048 | tf_op jit(solution)/shard_map/ppermute | solution.py:345
  643.3 40.8 %collective-permute-start.50 = (bf16[256,640]{1,0:T(8,128)(2,1)}, bf16[256,640]{1,0:T(8,128)(2,1)}, u32[]{:S(2)}, u32[]{:S(2)}) collective-permute-start(bf16[256,640]{1,0:T(8,128)(2,1)} %get-tuple-element.159), channel_id=1, source_target_pairs={{24,0},{0,8},{8,16},{16,24},{25,1},{1,9},{9,17},{17,25},{26,2},{2,... | collective-permute-start | bytes 983048 | tf_op jit(solution)/shard_map/ppermute | solution.py:345
  653.3 32.4 %collective-permute-start.45 = (f32[2,64]{1,0:T(2,128)S(1)}, f32[2,64]{1,0:T(2,128)S(1)}, u32[]{:S(2)}, u32[]{:S(2)}) collective-permute-start(f32[2,64]{1,0:T(2,128)S(1)} %bitcast.268), channel_id=1, source_target_pairs={{8,0},{16,8},{24,16},{0,24},{9,1},{17,9},{25,17},{1,25},{10,2},{18... | collective-permute-start | bytes 1544 | tf_op jit(solution)/shard_map/ppermute | solution.py:345
  654.9 30.7 %collective-permute-start.46 = (f32[2,64]{1,0:T(2,128)S(1)}, f32[2,64]{1,0:T(2,128)S(1)}, u32[]{:S(2)}, u32[]{:S(2)}) collective-permute-start(f32[2,64]{1,0:T(2,128)S(1)} %bitcast.267), channel_id=1, source_target_pairs={{16,0},{24,8},{0,16},{8,24},{17,1},{25,9},{1,17},{9,25},{18,2},{26... | collective-permute-start | bytes 1544 | tf_op jit(solution)/shard_map/ppermute | solution.py:345
  660.3 44.5 %all-to-all-start.6 = ((bf16[2,128,1,2048]{3,0,2,1:T(2,128)(2,1)}), bf16[2,128,1,2048]{3,0,2,1:T(2,128)(2,1)S(1)}, u32[]{:S(2)}, u32[]{:S(2)}) async-start(bf16[2,128,1,2048]{3,0,2,1:T(2,128)(2,1)} %copy.202), calls=%async_computation.8 | async-start | bytes 2097152 | tf_op jit(solution)/shard_map/all_to_all | solution.py:526
  663.5 31.8 %collective-permute-start.47 = (f32[2,64]{1,0:T(2,128)S(1)}, f32[2,64]{1,0:T(2,128)S(1)}, u32[]{:S(2)}, u32[]{:S(2)}) collective-permute-start(f32[2,64]{1,0:T(2,128)S(1)} %bitcast.266), channel_id=1, source_target_pairs={{24,0},{0,8},{8,16},{16,24},{25,1},{1,9},{9,17},{17,25},{26,2},{2,... | collective-permute-start | bytes 1544 | tf_op jit(solution)/shard_map/ppermute | solution.py:345
  (91 other events, 1215.4 us)
Sparse Core Ops, SparseCore 0:
  9.6 34.0 all-gather.6
  45.2 39.3 all-gather.4
  91.2 62.5 all-gather.8
  163.5 135.0 all-gather.10
  334.4 60.2 reduce-scatter.2
  401.7 111.2 reduce-scatter.4
